TPU v7x, 32 devices: a whole 2x2x4 slice. The times are simulated.
32 devices in a mesh: enc: 4 (over z), roll: 8 (over y, x, core).
Axes of the slice: x: 2, y: 2, z: 4, core: 2. Of those that a mesh axis runs over, the one named last changes fastest.
Arguments:
- row_grads: bfloat16 [4, 256, 8192], P('enc', 'roll'), may hold values from -1.5 to 1.5
- row_dest: int32 [4, 256], P('enc', 'roll'), may hold values from 0 to 32, as said below
- merger_in: bfloat16 [4, 32, 5120], P('enc'), may hold values from -6 to 6
- hidden_pre: bfloat16 [4, 32, 5120], P('enc'), may hold values from -8 to 8
- w_second: bfloat16 [5120, 8192], P(None, 'roll'), may hold values from -0.125 to 0.125
Outputs:
- pre_grads: bfloat16 [4, 32, 5120], P('enc', None, 'roll')
- grad_first: float32 [5120, 5120], P('enc', 'roll')
- grad_second: float32 [5120, 8192], P('enc', 'roll')
Inputs may be any that keep to these rules, and one draw needn't show every extreme that they name: `row_dest`: slot j of rollout device r in a group (slots r * 32 to (r + 1) * 32 - 1) holds 32 for an unused slot or a merged row of its prompt, in [(r // 8) * 32, (r // 8 + 1) * 32); the used rows of one device are distinct.
All inputs are finite; a program needn't handle non-finite values.
Results may differ from a plain program's by a relative error of at most 0.017.
Values may be sent and summed in bfloat16 or wider, within the bound.
No kernel may reach another device: no remote copies, remote signals or barrier semaphores. Data moves between devices by JAX's collectives and lax.ppermute only.
A program may use at most 128 MiB of HBM per device.

v0:
```python
import math

import jax
import jax.numpy as jnp
from jax import lax
from jax.sharding import PartitionSpec as P

inv_root_two = 1.0 / math.sqrt(2.0)
inv_root_two_pi = 1.0 / math.sqrt(2.0 * math.pi)


def gelu_slope(values):
    return (
        0.5 * (1.0 + lax.erf(values * inv_root_two))
        + values * jnp.exp(-0.5 * values * values) * inv_root_two_pi
    )


def body(row_grads, row_dest, merger_in, hidden_pre, w_second):
    slots = row_grads[0]
    dest_all = lax.all_gather(row_dest[0], "roll", axis=0, tiled=True)
    columns = lax.all_to_all(slots, "roll", split_axis=1, concat_axis=0, tiled=True)
    merged_count = hidden_pre.shape[1]
    width = hidden_pre.shape[2]
    shards = lax.axis_size("roll")
    unit_cols = width // shards
    slot_count = slots.shape[0]
    prompts = merged_count // slot_count
    per_prompt = columns.shape[0] // prompts
    column_width = columns.shape[1]
    prompt_columns = columns.reshape(prompts, per_prompt, column_width)
    prompt_dest = dest_all.reshape(prompts, per_prompt)
    offsets = jnp.arange(prompts, dtype=jnp.int32)[:, None] * slot_count
    local_dest = prompt_dest - offsets
    row_ids = jnp.arange(slot_count, dtype=jnp.int32)
    picker = (local_dest[:, None, :] == row_ids[None, :, None]).astype(jnp.bfloat16)
    merged_blocks = lax.dot_general(
        picker, prompt_columns, (((2,), (1,)), ((0,), (0,))), preferred_element_type=jnp.float32
    )
    merged = merged_blocks.reshape(merged_count, column_width).astype(jnp.bfloat16)
    before_full = hidden_pre[0]
    hidden = jax.nn.gelu(before_full.astype(jnp.float32), approximate=False).astype(jnp.bfloat16)
    weight_rows = lax.all_to_all(w_second, "roll", split_axis=0, concat_axis=1, tiled=True)
    units = lax.dot_general(
        lax.all_gather(merged, "roll", axis=1, tiled=True),
        weight_rows,
        (((1,), (1,)), ((), ())),
        preferred_element_type=jnp.float32,
    )
    first_col = lax.axis_index("roll") * unit_cols
    before_part = lax.dynamic_slice_in_dim(before_full, first_col, unit_cols, 1).astype(jnp.float32)
    grads = (units * gelu_slope(before_part)).astype(jnp.bfloat16)
    factor = 1.0 / math.sqrt(merged_count * lax.axis_size("enc"))
    term_second = (
        lax.dot_general(
            hidden, merged, (((0,), (0,)), ((), ())), preferred_element_type=jnp.float32
        )
        * factor
    )
    term_first = (
        lax.dot_general(
            merger_in[0], grads, (((0,), (0,)), ((), ())), preferred_element_type=jnp.float32
        )
        * factor
    )
    grad_first, grad_second = (
        lax.psum_scatter(
            term_first.astype(jnp.bfloat16), "enc", scatter_dimension=0, tiled=True
        ).astype(jnp.float32),
        lax.psum_scatter(
            term_second.astype(jnp.bfloat16), "enc", scatter_dimension=0, tiled=True
        ).astype(jnp.float32),
    )
    return (grads[None], grad_first, grad_second)


def solution(mesh):
    return jax.shard_map(
        body,
        mesh=mesh,
        in_specs=(
            P("enc", "roll", None),
            P("enc", "roll"),
            P("enc", None, None),
            P("enc", None, None),
            P(None, "roll"),
        ),
        out_specs=(P("enc", None, "roll"), P("enc", "roll"), P("enc", "roll")),
        check_vma=False,
    )
```

profile of v0, /device:TPU:0, one launch (start us, length us, event | category | flops | bytes accessed | tf_op | source)
XLA Modules:
  0.0 342.8 jit_solution(14225147727547457344)
XLA Ops:
  7.2 0.0 copy-start
  7.2 1.4 copy.16
  8.6 1.1 copy.13
  9.7 5.2 %all-to-all-start = ((bf16[32,8,1024]{2,0,1:T(8,128)(2,1)}), bf16[32,8,1024]{2,0,1:T(8,128)(2,1)S(1)}, u32[]{:S(2)}, u32[]{:S(2)}) async-start(bf16[32,8,1024]{2,0,1:T(8,128)(2,1)} %copy.13), calls=%async_computation | async-start | bytes 1048576 | tf_op jit(solution)/shard_map/all_to_all | solution.py:22
  14.8 0.0 reduce-scatter.5.cloned.1.call-start
  14.9 1.2 dynamic-slice.1
  16.8 0.8 bitcast_dynamic-update-slice_fusion
  17.6 9.2 %all-reduce = s32[256]{0:T(256)S(1)} all-reduce(s32[256]{0:T(256)S(1)} %bitcast_dynamic-update-slice_fusion), channel_id=2, replica_groups=mesh['enc'=4,'roll'=8] {'roll'}, use_global_device_ids=true, to_apply=%add | all-reduce | flops 256 | bytes 2048
  26.8 0.0 all-to-all-done
  26.8 0.2 convolution_convert_fusion
  27.0 9.3 %multiply_convert_fusion = bf16[5120,1024]{1,0:T(8,128)(2,1)} fusion(bf16[32,1024]{1,0:T(8,128)(2,1)S(1)} %convolution_convert_fusion, bf16[1,32,5120]{2,1,0:T(8,128)(2,1)} %param.8), kind=kOutput, calls=%fused_computation | convolution fusion | flops 356843520 | bytes 10878976 | tf_op jit(solution)/shard_map/dot_general | solution.py:55
  36.3 0.0 reduce-scatter.5.cloned.1.call-update
  36.3 5.2 %all-to-all-start.1 = ((bf16[8,640,1024]{2,1,0:T(8,128)(2,1)}), bf16[8,640,1024]{2,1,0:T(8,128)(2,1)}, u32[]{:S(2)}, u32[]{:S(2)}) async-start(bf16[8,640,1024]{2,1,0:T(8,128)(2,1)} %bitcast.30), calls=%async_computation.1 | async-start | bytes 20971520 | tf_op jit(solution)/shard_map/all_to_all | solution.py:43
  41.5 0.0 reduce-scatter.3.cloned.1.call-start
  41.6 120.8 %all_gather.7 = bf16[32,8192]{1,0:T(8,128)(2,1)S(1)} all-gather(bf16[32,1024]{1,0:T(8,128)(2,1)S(1)} %convolution_convert_fusion), channel_id=1, replica_groups=mesh['enc'=4,'roll'=8] {'roll'}, dimensions={1}, use_global_device_ids=true | all-gather | bytes 589824 | tf_op jit(solution)/shard_map/all_gather | solution.py:45
  162.4 0.0 all-to-all-done.1
  162.4 14.9 %copy.14 = bf16[640,8,1024]{0,2,1:T(8,128)(2,1)} copy(bf16[640,8,1024]{2,0,1:T(8,128)(2,1)} %bitcast.5) | data formatting | bytes 20971520 | tf_op jit(solution)/shard_map/all_to_all | solution.py:43
  177.3 5.7 %fusion.1 = bf16[32,640]{1,0:T(8,128)(2,1)S(1)} fusion(bf16[32,8192]{1,0:T(8,128)(2,1)S(1)} %all_gather.7, bf16[640,8192]{0,1:T(8,128)(2,1)} %bitcast.29, bf16[1,32,5120]{2,1,0:T(8,128)(2,1)} %param.8, s32[]{:T(128)S(6)} %select_n.3), kind=kOutput, calls=%fused_computation.5 | convolution fusion | flops 335769600 | bytes 11091972 | tf_op jit(solution)/shard_map/dot_general | solution.py:44
  183.0 0.0 copy-done
  183.0 0.0 copy-start.1
  183.1 4.6 %fusion = bf16[5120,640]{0,1:T(8,128)(2,1)} fusion(bf16[32,640]{1,0:T(8,128)(2,1)S(1)} %fusion.1, bf16[1,32,5120]{2,1,0:T(8,128)(2,1)S(1)} %copy-done), kind=kOutput, calls=%fused_computation.2 | convolution fusion | flops 216268800 | bytes 6922240 | tf_op jit(solution)/shard_map/dot_general | solution.py:61
  187.6 0.0 reduce-scatter.3.cloned.1.call-update
  187.7 26.2 %reduce-scatter.5.cloned.1.call-done = bf16[1280,1024]{1,0:T(8,128)(2,1)} async-done(((bf16[5120,1024]{1,0:T(8,128)(2,1)}), bf16[1280,1024]{1,0:T(8,128)(2,1)}) %reduce-scatter.5.cloned.1.call-update) | async-done | bytes 2621456 | tf_op jit(solution)/shard_map/reduce_scatter | solution.py:70
  213.9 4.7 %convert_element_type.50 = f32[1280,1024]{1,0:T(8,128)} convert(bf16[1280,1024]{1,0:T(8,128)(2,1)} %reduce-scatter.5.cloned.1.call-done) | non-fusion elementwise | flops 1310720 | bytes 7864320 | tf_op jit(solution)/shard_map/convert_element_type | solution.py:72
  218.6 0.0 copy-done.1
  218.7 113.7 %reduce-scatter.3.cloned.1.call-done = bf16[1280,640]{0,1:T(8,128)(2,1)} async-done(((bf16[5120,640]{0,1:T(8,128)(2,1)}), bf16[1280,640]{0,1:T(8,128)(2,1)}) %reduce-scatter.3.cloned.1.call-update) | async-done | bytes 1638416 | tf_op jit(solution)/shard_map/reduce_scatter | solution.py:67
  332.3 3.6 %copy.15 = f32[1280,640]{1,0:T(8,128)} copy(bf16[1280,640]{0,1:T(8,128)(2,1)} %reduce-scatter.3.cloned.1.call-done) | data formatting | bytes 4915200
  (1 shorter events, 0.0 us)
Async XLA Ops:
  7.2 175.9 %copy-start = (bf16[1,32,5120]{2,1,0:T(8,128)(2,1)S(1)}, bf16[1,32,5120]{2,1,0:T(8,128)(2,1)}, u32[]{:S(2)}) copy-start(bf16[1,32,5120]{2,1,0:T(8,128)(2,1)} %param.7) | copy-start | bytes 983044
  9.7 17.2 %all-to-all-start = ((bf16[32,8,1024]{2,0,1:T(8,128)(2,1)}), bf16[32,8,1024]{2,0,1:T(8,128)(2,1)S(1)}, u32[]{:S(2)}, u32[]{:S(2)}) async-start(bf16[32,8,1024]{2,0,1:T(8,128)(2,1)} %copy.13), calls=%async_computation | async-start | bytes 1048576 | tf_op jit(solution)/shard_map/all_to_all | solution.py:22
  14.8 199.1 %reduce-scatter.5.cloned.1.call-start = ((), (), s32[]{:S(2)}) async-start(), calls=%async_computation.5 | async-start | bytes 13107200 | tf_op jit(solution)/shard_map/reduce_scatter | solution.py:70
  36.3 126.1 %all-to-all-start.1 = ((bf16[8,640,1024]{2,1,0:T(8,128)(2,1)}), bf16[8,640,1024]{2,1,0:T(8,128)(2,1)}, u32[]{:S(2)}, u32[]{:S(2)}) async-start(bf16[8,640,1024]{2,1,0:T(8,128)(2,1)} %bitcast.30), calls=%async_computation.1 | async-start | bytes 20971520 | tf_op jit(solution)/shard_map/all_to_all | solution.py:43
  41.5 290.8 %reduce-scatter.3.cloned.1.call-start = ((), (), s32[]{:S(2)}) async-start(), calls=%async_computation.4 | async-start | bytes 8192000 | tf_op jit(solution)/shard_map/reduce_scatter | solution.py:67
  183.0 35.6 %copy-start.1 = (bf16[32,640]{1,0:T(8,128)(2,1)}, bf16[32,640]{1,0:T(8,128)(2,1)S(1)}, u32[]{:S(2)}) copy-start(bf16[32,640]{1,0:T(8,128)(2,1)S(1)} %fusion.1) | copy-start | bytes 122884
Sparse Core Ops, SparseCore 0:
  36.5 177.3 reduce-scatter.4
  216.2 116.0 reduce-scatter.2
where the time goes:
time: 344 us; the launch traced here: 343 us
  waiting for transfers between devices  140 us (41%)
  blocking collectives  130 us (38%)
  local copies, waits for them, and re-layouts  23 us (7%)
  matrix products  19.8 us (6%)
  between operations  14.8 us (4%)
  starting transfers between devices  10.4 us (3%)
  other arithmetic  4.75 us (1%)
    all_gather x1, blocking collectives, body(): lax.all_gather(merged, 'roll', axis=1, tiled=True)  121 us
    reduce_scatter x1, waiting for transfers between devices, body(): lax.psum_scatter(term_first.astype(jnp.bfloat16), 'enc', scatter_dimensio...  114 us
    reduce_scatter x1, waiting for transfers between devices, body(): lax.psum_scatter(term_second.astype(jnp.bfloat16), 'enc', scatter_dimensi...  26.2 us
    all_to_all x1, local copies, waits for them, and re-layouts, body(): lax.all_to_all(w_second, 'roll', split_axis=0, concat_axis=1, tiled=True)  14.9 us
    dot_general x1, matrix products, body(): lax.dot_general(hidden, merged, (((0,), (0,)), ((), ())), preferred_eleme...  9.31 us
    unnamed x1, blocking collectives  9.25 us
    unnamed x9, local copies, waits for them, and re-layouts  7.02 us
  transfers between devices with their start and end apart: 4, of which 2 were waited for; matrix products, arithmetic and copies ran while one was open for 9% of the time, Pallas kernels for 0%

commit v1 on v0

v1 whole, which is shorter than its diff:
```python
import math

import jax
import jax.numpy as jnp
from jax import lax
from jax.sharding import PartitionSpec as P

inv_root_two = 1.0 / math.sqrt(2.0)
inv_root_two_pi = 1.0 / math.sqrt(2.0 * math.pi)


def gelu_slope(values):
    return (
        0.5 * (1.0 + lax.erf(values * inv_root_two))
        + values * jnp.exp(-0.5 * values * values) * inv_root_two_pi
    )


def gather(block, axis):
    copies = jnp.broadcast_to(block[None], (lax.axis_size(axis),) + block.shape)
    return lax.all_to_all(copies, axis, split_axis=0, concat_axis=0, tiled=True)


def body(row_grads, row_dest, merger_in, hidden_pre, w_second):
    slots = row_grads[0]
    slot_count = slots.shape[0]
    merged_count = hidden_pre.shape[1]
    width = hidden_pre.shape[2]
    shards = lax.axis_size("roll")
    groups = lax.axis_size("enc")
    prompts = merged_count // slot_count
    per_prompt = shards // prompts
    columns = slots.shape[1] // shards
    unit_cols = width // shards
    in_cols = width // groups
    shard = lax.axis_index("roll")

    features = jnp.stack([hidden_pre[0], merger_in[0]])
    features = features.reshape(2, merged_count, groups, in_cols).transpose(2, 0, 1, 3)
    features = lax.all_to_all(features, "enc", split_axis=0, concat_axis=0, tiled=True)
    before_all = features[:, 0].reshape(groups * merged_count, in_cols)
    inputs_all = features[:, 1].reshape(groups * merged_count, in_cols)

    local_dest = row_dest[0] - shard // per_prompt * slot_count
    picker = (local_dest[None, :] == jnp.arange(slot_count, dtype=jnp.int32)[:, None]).astype(jnp.bfloat16)
    placed = jnp.einsum(
        "ms,src->rmc", picker, slots.reshape(slot_count, shards, columns),
        preferred_element_type=jnp.float32,
    ).astype(jnp.bfloat16)
    placed = lax.all_to_all(placed, "roll", split_axis=0, concat_axis=0, tiled=True)
    merged = placed.reshape(prompts, per_prompt, slot_count, columns).astype(jnp.float32).sum(1)
    merged = merged.reshape(merged_count, columns).astype(jnp.bfloat16)
    merged_all = gather(merged, "enc").reshape(groups * merged_count, columns)

    partial = jnp.einsum(
        "mc,ruc->rmu", merged, w_second.reshape(shards, unit_cols, columns),
        preferred_element_type=jnp.float32,
    ).astype(jnp.bfloat16)
    partial = lax.all_to_all(partial, "roll", split_axis=0, concat_axis=0, tiled=True)
    units = partial.astype(jnp.float32).sum(0)
    before_part = lax.dynamic_slice_in_dim(hidden_pre[0], shard * unit_cols, unit_cols, 1).astype(jnp.float32)
    grads = (units * gelu_slope(before_part)).astype(jnp.bfloat16)
    grads_all = gather(grads, "enc").reshape(groups * merged_count, unit_cols)

    factor = 1.0 / math.sqrt(merged_count * groups)
    hidden = jax.nn.gelu(before_all.astype(jnp.float32), approximate=False).astype(jnp.bfloat16)
    contract_rows = (((0,), (0,)), ((), ()))
    grad_second = lax.dot_general(hidden, merged_all, contract_rows, preferred_element_type=jnp.float32) * factor
    grad_first = lax.dot_general(inputs_all, grads_all, contract_rows, preferred_element_type=jnp.float32) * factor
    return (grads[None], grad_first, grad_second)


def solution(mesh):
    return jax.shard_map(
        body,
        mesh=mesh,
        in_specs=(
            P("enc", "roll", None),
            P("enc", "roll"),
            P("enc", None, None),
            P("enc", None, None),
            P(None, "roll"),
        ),
        out_specs=(P("enc", None, "roll"), P("enc", "roll"), P("enc", "roll")),
        check_vma=False,
    )
```

time: 344 us -> 83.9 us (0.24)
  blocking collectives: 130 us -> 14.7 us
  waiting for transfers between devices: 140 us -> 32 us
  local copies, waits for them, and re-layouts: 23 us -> 4.17 us
  between operations: 14.8 us -> 0.77 us
  matrix products: 19.8 us -> 14.3 us
  starting transfers between devices: 10.4 us -> 15.1 us
    reduce_scatter x2 -> x0, waiting for transfers between devices: 140 us -> none  [the longest x1 114 us: body(): lax.psum_scatter(term_first.astype(jnp.bfloat16), 'enc', scatter_dimensio...]
    all_gather x1 -> x0, blocking collectives: 121 us -> none  [body(): lax.all_gather(merged, 'roll', axis=1, tiled=True)]
    all_to_all x2 -> x4, waiting for transfers between devices: 0.01 us -> 32 us  [the longest x1 16.3 us: body(): lax.all_to_all(features, 'enc', split_axis=0, concat_axis=0, tiled=True)]
    all_to_all x2 -> x0, local copies, waits for them, and re-layouts: 16 us -> none  [the longest x1 14.9 us: body(): lax.all_to_all(w_second, 'roll', split_axis=0, concat_axis=1, tiled=True)]
    all_to_all x0 -> x1, blocking collectives: none -> 14.7 us  [body(): lax.all_to_all(placed, 'roll', split_axis=0, concat_axis=0, tiled=True)]
    unnamed x1 -> x0, blocking collectives: 9.25 us -> none
    unnamed x9 -> x7, local copies, waits for them, and re-layouts: 7.02 us -> 1.36 us
    dot_general x4, matrix products: 19.8 us -> 14.3 us  [the longest x1 7.95 us: body(): jnp.einsum('mc,ruc->rmu', merged, w_second.reshape(shards, unit_cols, col...]
  transfers between devices with their start and end apart: 4 -> 4, of which waited for: 2 -> 4; matrix products, arithmetic and copies ran while one was open for 9% -> 7% of each run, Pallas kernels for 0% -> 0%
where the time goes in v1:
time: 83.9 us; the launch traced here: 83.3 us
  waiting for transfers between devices  32 us (38%)
  starting transfers between devices  15.1 us (18%)
  blocking collectives  14.7 us (18%)
  matrix products  14.3 us (17%)
  local copies, waits for them, and re-layouts  4.17 us (5%)
  other arithmetic  2.32 us (3%)
    all_to_all x1, waiting for transfers between devices, body(): lax.all_to_all(features, 'enc', split_axis=0, concat_axis=0, tiled=True)  16.3 us
    all_to_all x1, blocking collectives, body(): lax.all_to_all(placed, 'roll', split_axis=0, concat_axis=0, tiled=True)  14.7 us
    all_to_all x2, waiting for transfers between devices, gather(): return lax.all_to_all(copies, axis, split_axis=0, concat_axis=0, tiled=True)  9.69 us
    dot_general x1, matrix products, body(): jnp.einsum('mc,ruc->rmu', merged, w_second.reshape(shards, unit_cols, col...  7.95 us
    all_to_all x2, starting transfers between devices, gather(): return lax.all_to_all(copies, axis, split_axis=0, concat_axis=0, tiled=True)  6.75 us
    all_to_all x1, waiting for transfers between devices, body(): lax.all_to_all(partial, 'roll', split_axis=0, concat_axis=0, tiled=True)  6.07 us
    all_to_all x1, starting transfers between devices, body(): lax.all_to_all(features, 'enc', split_axis=0, concat_axis=0, tiled=True)  4.87 us
    all_to_all x1, starting transfers between devices, body(): lax.all_to_all(partial, 'roll', split_axis=0, concat_axis=0, tiled=True)  3.43 us
  transfers between devices with their start and end apart: 4, of which 4 were waited for; matrix products, arithmetic and copies ran while one was open for 7% of the time, Pallas kernels for 0%

profile of v1, /device:TPU:0, one launch (start us, length us, event | category | flops | bytes accessed | tf_op | source)
XLA Modules:
  0.0 83.3 jit_solution(18361651465188629961)
XLA Ops:
  0.6 1.3 %copy.19 = bf16[4,8,8,1024]{3,2,1,0:T(8,128)(2,1)S(1)} copy(bf16[4,8,8,1024]{3,1,2,0:T(8,128)(2,1)} %bitcast.44) | data formatting | bytes 1048576
  2.0 0.7 subtract_bitcast_fusion
  2.7 0.8 fusion
  3.4 14.7 %all_to_all.25 = bf16[8,32,1024]{2,1,0:T(8,128)(2,1)S(1)} all-to-all(bf16[8,32,1024]{2,1,0:T(8,128)(2,1)S(1)} %fusion), channel_id=1, replica_groups=mesh['enc'=4,'roll'=8] {'roll'}, dimensions={0} | all-to-all | bytes 1048576 | tf_op jit(solution)/shard_map/all_to_all | solution.py:50
  18.1 0.1 reduce_sum.23
  18.2 0.0 copy-start
  18.2 0.0 copy-start.1
  18.2 8.0 %fusion.1 = bf16[8,32,640]{2,1,0:T(8,128)(2,1)} fusion(bf16[8,640,1024]{2,1,0:T(8,128)(2,1)} %bitcast.37, bf16[32,1024]{1,0:T(8,128)(2,1)S(1)} %reduce_sum.23), kind=kOutput, calls=%fused_computation.5 | convolution fusion | flops 335708160 | bytes 10878976 | tf_op jit(solution)/shard_map/mc,ruc->rmu/dot_general | solution.py:55
  26.2 3.4 %all-to-all-start.1 = ((bf16[8,32,640]{2,1,0:T(8,128)(2,1)}), bf16[8,32,640]{2,1,0:T(8,128)(2,1)S(1)}, u32[]{:S(2)}, u32[]{:S(2)}) async-start(bf16[8,32,640]{2,1,0:T(8,128)(2,1)} %fusion.1), calls=%async_computation.1 | async-start | bytes 655360 | tf_op jit(solution)/shard_map/all_to_all | solution.py:59
  29.6 0.0 copy-done
  29.6 0.0 copy-done.1
  29.7 0.1 pad_maximum_fusion
  29.7 0.5 reshape.29
  30.2 0.9 %copy.14 = bf16[4,2,32,1280]{3,2,1,0:T(8,128)(2,1)} copy(bf16[4,2,32,1280]{3,0,2,1:T(4,128)(2,1)S(1)} %bitcast.38) | data formatting | bytes 1310720 | tf_op jit(solution)/shard_map/transpose | solution.py:39
  31.1 6.1 %all-to-all-done.1 = bf16[8,32,640]{2,1,0:T(8,128)(2,1)S(1)} async-done(((bf16[8,32,640]{2,1,0:T(8,128)(2,1)}), bf16[8,32,640]{2,1,0:T(8,128)(2,1)S(1)}, u32[]{:S(2)}, u32[]{:S(2)}) %all-to-all-start.1) | async-done | bytes 327712 | tf_op jit(solution)/shard_map/all_to_all | solution.py:59
  37.2 4.9 %all-to-all-start.2 = ((bf16[4,2,32,1280]{3,2,1,0:T(8,128)(2,1)}), bf16[4,2,32,1280]{3,2,1,0:T(8,128)(2,1)S(1)}, u32[]{:S(2)}, u32[]{:S(2)}) async-start(bf16[4,2,32,1280]{3,2,1,0:T(8,128)(2,1)} %copy.14), calls=%async_computation.2 | async-start | bytes 1310720 | tf_op jit(solution)/shard_map/all_to_all | solution.py:40
  42.1 0.1 fusion.41
  42.1 0.0 copy-start.2
  42.2 16.3 %all-to-all-done.2 = bf16[4,2,32,1280]{3,2,1,0:T(8,128)(2,1)S(1)} async-done(((bf16[4,2,32,1280]{3,2,1,0:T(8,128)(2,1)}), bf16[4,2,32,1280]{3,2,1,0:T(8,128)(2,1)S(1)}, u32[]{:S(2)}, u32[]{:S(2)}) %all-to-all-start.2) | async-done | bytes 655392 | tf_op jit(solution)/shard_map/all_to_all | solution.py:40
  58.4 0.7 broadcast_in_dim.8
  59.2 3.4 %all-to-all-start.4 = ((bf16[4,32,1024]{2,1,0:T(8,128)(2,1)}), bf16[4,32,1024]{2,1,0:T(8,128)(2,1)S(1)}, u32[]{:S(2)}, u32[]{:S(2)}) async-start(bf16[4,32,1024]{2,1,0:T(8,128)(2,1)} %broadcast_in_dim.8), calls=%async_computation.4 | async-start | bytes 524288 | tf_op jit(solution)/shard_map/all_to_all | solution.py:21
  62.6 1.4 %fusion.3 = bf16[4,1,32,1280]{3,2,0,1:T(8,128)(2,1)S(1)} fusion(bf16[4,2,32,1280]{3,2,1,0:T(8,128)(2,1)S(1)} %all-to-all-done.2), kind=kLoop, calls=%fused_computation.10 | loop fusion | flops 10813440 | bytes 655360 | tf_op jit(solution)/shard_map/convert_element_type | solution.py:66
  64.0 6.9 %all-to-all-done.4 = bf16[4,32,1024]{2,1,0:T(8,128)(2,1)S(1)} async-done(((bf16[4,32,1024]{2,1,0:T(8,128)(2,1)}), bf16[4,32,1024]{2,1,0:T(8,128)(2,1)S(1)}, u32[]{:S(2)}, u32[]{:S(2)}) %all-to-all-start.4) | async-done | bytes 262176 | tf_op jit(solution)/shard_map/all_to_all | solution.py:21
  71.0 0.7 broadcast_in_dim.7
  71.7 3.3 %all-to-all-start.3 = ((bf16[4,32,640]{2,1,0:T(8,128)(2,1)}), bf16[4,32,640]{2,1,0:T(8,128)(2,1)S(1)}, u32[]{:S(2)}, u32[]{:S(2)}) async-start(bf16[4,32,640]{2,1,0:T(8,128)(2,1)} %broadcast_in_dim.7), calls=%async_computation.3 | async-start | bytes 327680 | tf_op jit(solution)/shard_map/all_to_all | solution.py:21
  75.0 3.2 %convolution_multiply_fusion = f32[1280,1024]{1,0:T(8,128)} fusion(bf16[128,1280]{1,0:T(8,128)(2,1)S(1)} %bitcast.39, bf16[128,1024]{1,0:T(8,128)(2,1)S(1)} %bitcast.42), kind=kOutput, calls=%fused_computation | convolution fusion | flops 336855040 | bytes 5832704 | tf_op jit(solution)/shard_map/dot_general | solution.py:68
  78.2 0.0 copy-done.2
  78.2 2.7 %all-to-all-done.3 = bf16[4,32,640]{2,1,0:T(8,128)(2,1)S(1)} async-done(((bf16[4,32,640]{2,1,0:T(8,128)(2,1)}), bf16[4,32,640]{2,1,0:T(8,128)(2,1)S(1)}, u32[]{:S(2)}, u32[]{:S(2)}) %all-to-all-start.3) | async-done | bytes 163872 | tf_op jit(solution)/shard_map/all_to_all | solution.py:21
  81.0 2.3 %convolution_multiply_fusion.1 = f32[1280,640]{1,0:T(8,128)} fusion(bf16[128,1280]{1,0:T(8,128)(2,1)S(1)} %bitcast.41, bf16[128,640]{1,0:T(8,128)(2,1)S(1)} %bitcast.43), kind=kOutput, calls=%fused_computation.1 | convolution fusion | flops 210534400 | bytes 3768320 | tf_op jit(solution)/shard_map/dot_general | solution.py:69
  (2 shorter events, 0.1 us)
Async XLA Ops:
  18.2 11.4 %copy-start = (bf16[1,32,5120]{2,1,0:T(8,128)(2,1)S(1)}, bf16[1,32,5120]{2,1,0:T(8,128)(2,1)}, u32[]{:S(2)}) copy-start(bf16[1,32,5120]{2,1,0:T(8,128)(2,1)} %param.8) | copy-start | bytes 983044
  18.2 11.4 %copy-start.1 = (bf16[1,32,5120]{2,1,0:T(8,128)(2,1)S(1)}, bf16[1,32,5120]{2,1,0:T(8,128)(2,1)}, u32[]{:S(2)}) copy-start(bf16[1,32,5120]{2,1,0:T(8,128)(2,1)} %param.7) | copy-start | bytes 983044
  26.2 11.0 %all-to-all-start.1 = ((bf16[8,32,640]{2,1,0:T(8,128)(2,1)}), bf16[8,32,640]{2,1,0:T(8,128)(2,1)S(1)}, u32[]{:S(2)}, u32[]{:S(2)}) async-start(bf16[8,32,640]{2,1,0:T(8,128)(2,1)} %fusion.1), calls=%async_computation.1 | async-start | bytes 655360 | tf_op jit(solution)/shard_map/all_to_all | solution.py:59
  37.2 21.3 %all-to-all-start.2 = ((bf16[4,2,32,1280]{3,2,1,0:T(8,128)(2,1)}), bf16[4,2,32,1280]{3,2,1,0:T(8,128)(2,1)S(1)}, u32[]{:S(2)}, u32[]{:S(2)}) async-start(bf16[4,2,32,1280]{3,2,1,0:T(8,128)(2,1)} %copy.14), calls=%async_computation.2 | async-start | bytes 1310720 | tf_op jit(solution)/shard_map/all_to_all | solution.py:40
  42.1 36.1 %copy-start.2 = (bf16[1,32,640]{2,1,0:T(8,128)(2,1)}, bf16[1,32,640]{2,1,0:T(8,128)(2,1)S(1)}, u32[]{:S(2)}) copy-start(bf16[1,32,640]{2,1,0:T(8,128)(2,1)S(1)} %fusion.41) | copy-start | bytes 122884
  59.2 11.8 %all-to-all-start.4 = ((bf16[4,32,1024]{2,1,0:T(8,128)(2,1)}), bf16[4,32,1024]{2,1,0:T(8,128)(2,1)S(1)}, u32[]{:S(2)}, u32[]{:S(2)}) async-start(bf16[4,32,1024]{2,1,0:T(8,128)(2,1)} %broadcast_in_dim.8), calls=%async_computation.4 | async-start | bytes 524288 | tf_op jit(solution)/shard_map/all_to_all | solution.py:21
  71.7 9.3 %all-to-all-start.3 = ((bf16[4,32,640]{2,1,0:T(8,128)(2,1)}), bf16[4,32,640]{2,1,0:T(8,128)(2,1)S(1)}, u32[]{:S(2)}, u32[]{:S(2)}) async-start(bf16[4,32,640]{2,1,0:T(8,128)(2,1)} %broadcast_in_dim.7), calls=%async_computation.3 | async-start | bytes 327680 | tf_op jit(solution)/shard_map/all_to_all | solution.py:21

commit v2 on v1

v2 whole, which is shorter than its diff:
```python
import functools
import math

import jax
import jax.numpy as jnp
from jax import lax
from jax.experimental import pallas as pl
from jax.experimental.pallas import tpu as pltpu
from jax.sharding import PartitionSpec as P


inv_root_two = 1.0 / math.sqrt(2.0)
inv_root_two_pi = 1.0 / math.sqrt(2.0 * math.pi)
VMEM = pl.BlockSpec(memory_space=pltpu.VMEM)
HBM = pl.BlockSpec(memory_space=pltpu.HBM)
shape = jax.ShapeDtypeStruct


def gelu_slope(values):
    return (
        0.5 * (1.0 + lax.erf(values * inv_root_two))
        + values * jnp.exp(-0.5 * values * values) * inv_root_two_pi
    )


def gelu(values):
    return 0.5 * values * (1.0 + lax.erf(values * inv_root_two))


def call(kernel, outs, args, flops=0, in_specs=None, out_specs=None, scratch=(), limit=4 << 20):
    moved = sum(math.prod(a.shape) * a.dtype.itemsize for a in list(outs) + list(args))
    return pl.pallas_call(
        kernel,
        out_shape=outs,
        in_specs=in_specs or [VMEM] * len(args),
        out_specs=out_specs or [VMEM] * len(outs),
        scratch_shapes=scratch,
        cost_estimate=pl.CostEstimate(flops=flops, bytes_accessed=moved, transcendentals=0),
        compiler_params=pltpu.CompilerParams(vmem_limit_bytes=limit),
    )(*args)


def exchange(block, axis, step):
    pairs = [(i, i ^ step) for i in range(lax.axis_size(axis))]
    return lax.ppermute(block, axis, pairs)


def place_rows(parity, dest_ref, slots_ref, out_ref, held_dest, held, sems):
    halves, merged_count, columns = out_ref.shape
    shard = lax.axis_index("roll")
    dest_copy = pltpu.make_async_copy(dest_ref, held_dest, sems.at[halves])
    dest_copy.start()
    copies = []
    for j in range(halves):
        first = pl.multiple_of((shard ^ (2 * j + parity)) * columns, columns)
        copies.append(pltpu.make_async_copy(slots_ref.at[:, pl.ds(first, columns)], held.at[j], sems.at[j]))
        copies[-1].start()
    dest_copy.wait()
    rows = lax.broadcasted_iota(jnp.int32, (merged_count, held.shape[1]), 0)
    picker = jnp.where(rows == held_dest[...], 1.0, 0.0).astype(jnp.bfloat16)
    for j in range(halves):
        copies[j].wait()
        out_ref[j] = jnp.dot(picker, held[j], preferred_element_type=jnp.float32).astype(jnp.bfloat16)


def pair_sum(kept_ref, came_ref, *out_refs):
    for j, out_ref in enumerate(out_refs):
        out_ref[...] = (kept_ref[j].astype(jnp.float32) + came_ref[j].astype(jnp.float32)).astype(jnp.bfloat16)


def weight_copies(parity, w_ref, held, sems):
    halves, unit_cols, _ = held.shape
    shard = lax.axis_index("roll")
    copies = []
    for j in range(halves):
        first = pl.multiple_of((shard ^ (2 * j + parity)) * unit_cols, unit_cols)
        copies.append(pltpu.make_async_copy(w_ref.at[pl.ds(first, unit_cols), :], held.at[j], sems.at[j]))
        copies[-1].start()
    return copies


def unit_blocks(copies, merged, held, out_ref):
    for j, copy in enumerate(copies):
        copy.wait()
        out_ref[j] = lax.dot_general(
            merged, held[j], (((1,), (1,)), ((), ())), preferred_element_type=jnp.float32
        ).astype(jnp.bfloat16)


def first_units(parity, *refs):
    *piece_refs, w_ref, merged_ref, out_ref, held, sems = refs
    copies = weight_copies(parity, w_ref, held, sems)
    total = piece_refs[0][...].astype(jnp.float32)
    for piece_ref in piece_refs[1:]:
        total = total + piece_ref[...].astype(jnp.float32)
    merged = total.astype(jnp.bfloat16)
    for k in range(merged_ref.shape[0]):
        merged_ref[k] = merged
    unit_blocks(copies, merged, held, out_ref)


def second_units(parity, merged_ref, w_ref, out_ref, held, sems):
    unit_blocks(weight_copies(parity, w_ref, held, sems), merged_ref[0], held, out_ref)


def feature_blocks(before_ref, inputs_ref, *refs):
    *out_refs, held, sems = refs
    rows = before_ref.shape[0]
    columns = out_refs[0].shape[1]
    group = lax.axis_index("enc")
    copies = []
    for k, out_ref in enumerate(out_refs):
        cut = pl.ds(pl.multiple_of((group ^ k) * columns, columns), columns)
        copies.append((
            pltpu.make_async_copy(before_ref.at[:, cut], held.at[k], sems.at[0, k]),
            pltpu.make_async_copy(inputs_ref.at[:, cut], out_ref.at[pl.ds(rows, rows), :], sems.at[1, k]),
        ))
        for copy in copies[-1]:
            copy.start()
    for k, out_ref in enumerate(out_refs):
        copies[k][0].wait()
        out_ref[:rows, :] = gelu(held[k].astype(jnp.float32)).astype(jnp.bfloat16)
    for _, copy in copies:
        copy.wait()


def slope_block(before_ref, out_ref):
    out_ref[...] = gelu_slope(before_ref[...].astype(jnp.float32))


def write_products(left_of, right, factor, out_ref, held, sems):
    size = held.shape[1]
    copies = []
    for j in range(held.shape[0]):
        held[j] = lax.dot_general(
            left_of(j * size, size), right, (((0,), (0,)), ((), ())), preferred_element_type=jnp.float32
        ) * factor
        copies.append(pltpu.make_async_copy(held.at[j], out_ref.at[pl.ds(j * size, size), :], sems.at[j]))
        copies[-1].start()
    for copy in copies:
        copy.wait()


def second_products(factor, groups, *refs):
    feature_refs, (merged_ref, out_ref, held, sems) = refs[:groups], refs[groups:]
    rows = merged_ref.shape[1]
    group = lax.axis_index("enc")

    def left_of(first, size):
        return jnp.concatenate([ref[:rows, first : first + size] for ref in feature_refs], axis=0)

    right = jnp.concatenate([merged_ref[group ^ k] for k in range(groups)], axis=0)
    write_products(left_of, right, factor, out_ref, held, sems)


def first_products(factor, groups, *refs):
    feature_refs, grad_refs, (out_ref, held, sems) = refs[:groups], refs[groups : 2 * groups], refs[2 * groups :]
    rows = grad_refs[0].shape[0]

    def left_of(first, size):
        return jnp.concatenate([ref[rows:, first : first + size] for ref in feature_refs], axis=0)

    right = jnp.concatenate([ref[...] for ref in grad_refs], axis=0)
    write_products(left_of, right, factor, out_ref, held, sems)


def products(kernel, factor, features, rights, columns):
    groups, (rows, in_cols) = len(features), features[0].shape
    size = next((s for s in (256, 128) if in_cols % s == 0), in_cols)
    out = shape((in_cols, columns), jnp.float32)
    (result,) = call(
        functools.partial(kernel, factor, groups), [out], (*features, *rights), groups * rows * in_cols * columns,
        out_specs=[HBM],
        scratch=[pltpu.VMEM((in_cols // size, size, columns), jnp.float32), pltpu.SemaphoreType.DMA((in_cols // size,))],
        limit=(6 << 20) + 4 * in_cols * columns,
    )
    return result


def body(row_grads, row_dest, merger_in, hidden_pre, w_second):
    slots = row_grads[0]
    slot_count = slots.shape[0]
    before, inputs = hidden_pre[0], merger_in[0]
    merged_count, width = before.shape
    slots, row_dest, w_second = (pltpu.with_memory_space_constraint(x, pltpu.HBM) for x in (slots, row_dest, w_second))
    shards = lax.axis_size("roll")
    groups = lax.axis_size("enc")
    halves = shards // 2
    columns = slots.shape[1] // shards
    unit_cols = width // shards
    in_cols = width // groups
    shard = lax.axis_index("roll")
    kind = jnp.bfloat16

    def spread(kept, came):
        blocks = call(pair_sum, [shape(kept.shape[1:], kind)] * halves, (kept, came), kept.size)
        return [blocks[0]] + [exchange(blocks[j], "roll", 2 * j) for j in range(1, halves)]

    if in_cols % 128 == 0:
        outs = [shape((2 * merged_count, in_cols), kind)] * groups
        scratch = [pltpu.VMEM((groups, merged_count, in_cols), kind), pltpu.SemaphoreType.DMA((2, groups))]
        sources = [pltpu.with_memory_space_constraint(x, pltpu.HBM) for x in (before, inputs)]
        blocks = call(feature_blocks, outs, sources, in_specs=[HBM, HBM], scratch=scratch, limit=8 << 20)
    else:
        both = jnp.concatenate([gelu(before.astype(jnp.float32)).astype(kind), inputs], axis=0)
        group = lax.axis_index("enc")
        blocks = [lax.dynamic_slice_in_dim(both, (group ^ k) * in_cols, in_cols, 1) for k in range(groups)]
    features = [blocks[0]] + [exchange(blocks[k], "enc", k) for k in range(1, groups)]

    place = (halves, merged_count, columns)

    def placed(parity):
        scratch = [
            pltpu.VMEM(row_dest.shape, row_dest.dtype),
            pltpu.VMEM((halves, slot_count, columns), kind),
            pltpu.SemaphoreType.DMA((halves + 1,)),
        ]
        return call(
            functools.partial(place_rows, parity), [shape(place, kind)], (row_dest, slots),
            2 * slot_count * math.prod(place), in_specs=[HBM, HBM], scratch=scratch, limit=8 << 20,
        )[0]

    came = exchange(placed(1), "roll", 1)
    pieces = spread(placed(0), came)

    unit_shape = (halves, merged_count, unit_cols)
    flops = 2 * columns * math.prod(unit_shape)
    scratch = [pltpu.VMEM((halves, unit_cols, columns), kind), pltpu.SemaphoreType.DMA((halves,))]
    limit = (8 << 20) + w_second.size
    copies, sent = call(
        functools.partial(first_units, 1),
        [shape((groups, merged_count, columns), kind), shape(unit_shape, kind)],
        (*pieces, w_second), flops, in_specs=[VMEM] * halves + [HBM], scratch=scratch, limit=limit,
    )
    came = exchange(sent, "roll", 1)
    (kept,) = call(
        functools.partial(second_units, 0), [shape(unit_shape, kind)], (copies, w_second), flops,
        in_specs=[VMEM, HBM], scratch=scratch, limit=limit,
    )
    pieces = spread(kept, came)
    merged_all = lax.all_to_all(copies, "enc", split_axis=0, concat_axis=0, tiled=True)
    own = lax.dynamic_slice_in_dim(before, shard * unit_cols, unit_cols, 1)
    (slope,) = call(slope_block, [shape(own.shape, jnp.float32)], (own,))
    grads = (sum(piece.astype(jnp.float32) for piece in pieces) * slope).astype(kind)
    grads_all = [grads] + [exchange(grads, "enc", k) for k in range(1, groups)]

    factor = 1.0 / math.sqrt(merged_count * groups)
    grad_second = products(second_products, factor, features, [merged_all], columns)
    grad_first = products(first_products, factor, features, grads_all, unit_cols)
    return (grads[None], grad_first, grad_second)


def solution(mesh):
    return jax.shard_map(
        body,
        mesh=mesh,
        in_specs=(
            P("enc", "roll", None),
            P("enc", "roll"),
            P("enc", None, None),
            P("enc", None, None),
            P(None, "roll"),
        ),
        out_specs=(P("enc", None, "roll"), P("enc", "roll"), P("enc", "roll")),
        check_vma=False,
    )
```

time: 83.9 us -> 53.9 us (0.64)
  waiting for transfers between devices: 32 us -> 10.2 us
  Pallas kernels: 0 us -> 17.4 us
  blocking collectives: 14.7 us -> 0 us
  matrix products: 14.3 us -> 0 us
  starting transfers between devices: 15.1 us -> 24.3 us
  local copies, waits for them, and re-layouts: 4.17 us -> 0.79 us
  other arithmetic: 2.32 us -> 0.03 us
    all_to_all x4 -> x1, waiting for transfers between devices: 32 us -> 0.01 us  [body(): lax.all_to_all(copies, 'enc', split_axis=0, concat_axis=0, tiled=True)]
    ppermute x0 -> x14, starting transfers between devices: none -> 20.9 us  [exchange(): return lax.ppermute(block, axis, pairs)]
    pallas_call x0 -> x10, Pallas kernels: none -> 17.4 us  [call(): pl.pallas_call(kernel, out_shape=outs, in_specs=in_specs or [VMEM] * len(...]
    all_to_all x1 -> x0, blocking collectives: 14.7 us -> none  [body(): lax.all_to_all(placed, 'roll', split_axis=0, concat_axis=0, tiled=True)]
    dot_general x4 -> x0, matrix products: 14.3 us -> none  [the longest x1 7.95 us: body(): jnp.einsum('mc,ruc->rmu', merged, w_second.reshape(shards, unit_cols, col...]
    all_to_all x4 -> x1, starting transfers between devices: 15.1 us -> 3.41 us  [body(): lax.all_to_all(copies, 'enc', split_axis=0, concat_axis=0, tiled=True)]
    ppermute x0 -> x14, waiting for transfers between devices: none -> 10.2 us  [exchange(): return lax.ppermute(block, axis, pairs)]
    convert_element_type x2 -> x1, other arithmetic: 1.47 us -> 0.03 us  [body(): (sum((piece.astype(jnp.float32) for piece in pieces)) * slope).astype(kind)]
  transfers between devices with their start and end apart: 4 -> 15, of which waited for: 4 -> 5; matrix products, arithmetic and copies ran while one was open for 7% -> 2% of each run, Pallas kernels for 0% -> 18%
where the time goes in v2:
time: 53.9 us; the launch traced here: 53.5 us
  starting transfers between devices  24.3 us (45%)
  Pallas kernels  17.4 us (32%)
  waiting for transfers between devices  10.2 us (19%)
  local copies, waits for them, and re-layouts  0.79 us (1%)
  between operations  0.77 us (1%)
    ppermute x14, starting transfers between devices, exchange(): return lax.ppermute(block, axis, pairs)  20.9 us
    pallas_call x10, Pallas kernels, call(): pl.pallas_call(kernel, out_shape=outs, in_specs=in_specs or [VMEM] * len(...  17.4 us
    ppermute x14, waiting for transfers between devices, exchange(): return lax.ppermute(block, axis, pairs)  10.2 us
    all_to_all x1, starting transfers between devices, body(): lax.all_to_all(copies, 'enc', split_axis=0, concat_axis=0, tiled=True)  3.41 us
  transfers between devices with their start and end apart: 15, of which 5 were waited for; matrix products, arithmetic and copies ran while one was open for 2% of the time, Pallas kernels for 18%

profile of v2, /device:TPU:0, one launch (start us, length us, event | category | flops | bytes accessed | tf_op | source)
XLA Modules:
  0.0 53.5 jit_solution(9670682204812429079)
XLA Ops:
  0.6 1.5 %shard_map.77 = bf16[4,32,1024]{2,1,0:T(8,128)(2,1)S(1)} custom-call(s32[1,32]{1,0:T(1,128)} %dest_ref.3, bf16[32,8192]{1,0:T(8,128)(2,1)} %bitcast.7), custom_call_target="tpu_custom_call" | custom-call | flops 8388608 | bytes 786560 | tf_op jit(solution)/shard_map/pallas_call | solution.py:32
  2.1 0.6 %collective-permute-start = (bf16[4,32,1024]{2,1,0:T(8,128)(2,1)S(1)}, bf16[4,32,1024]{2,1,0:T(8,128)(2,1)S(1)}, u32[]{:S(2)}, u32[]{:S(2)}) collective-permute-start(bf16[4,32,1024]{2,1,0:T(8,128)(2,1)S(1)} %shard_map.77), channel_id=1, source_target_pairs={{0,1},{1,0},{2,3},{3,2},{4,5},{5,4},{6,7},{7,6},{8,9},{9,8},{10,11... | collective-permute-start | bytes 786440 | tf_op jit(solution)/shard_map/ppermute | solution.py:45
  2.7 1.5 %shard_map.76.kept_ref = bf16[4,32,1024]{2,1,0:T(8,128)(2,1)S(1)} custom-call(s32[1,32]{1,0:T(1,128)} %dest_ref.3, bf16[32,8192]{1,0:T(8,128)(2,1)} %bitcast.8), custom_call_target="tpu_custom_call" | custom-call | flops 8388608 | bytes 786560 | tf_op jit(solution)/shard_map/pallas_call | solution.py:32
  4.1 0.1 shard_map.78
  4.2 2.6 %collective-permute-start.1 = (bf16[32,1024]{1,0:T(8,128)(2,1)S(1)}, bf16[32,1024]{1,0:T(8,128)(2,1)S(1)}, u32[]{:S(2)}, u32[]{:S(2)}) collective-permute-start(bf16[32,1024]{1,0:T(8,128)(2,1)S(1)} %get-tuple-element.18), channel_id=1, source_target_pairs={{0,2},{1,3},{2,0},{3,1},{4,6},{5,7},{6,4},{7,5},{8,10},{9,11},{10,... | collective-permute-start | bytes 196616 | tf_op jit(solution)/shard_map/ppermute | solution.py:45
  6.8 1.5 %collective-permute-start.2 = (bf16[32,1024]{1,0:T(8,128)(2,1)S(1)}, bf16[32,1024]{1,0:T(8,128)(2,1)S(1)}, u32[]{:S(2)}, u32[]{:S(2)}) collective-permute-start(bf16[32,1024]{1,0:T(8,128)(2,1)S(1)} %get-tuple-element.19), channel_id=1, source_target_pairs={{0,4},{1,5},{2,6},{3,7},{4,0},{5,1},{6,2},{7,3},{8,12},{9,13},{10,... | collective-permute-start | bytes 196616 | tf_op jit(solution)/shard_map/ppermute | solution.py:45
  8.3 0.0 collective-permute-start.3
  8.3 1.2 %collective-permute-done.1.refs_1_ = bf16[32,1024]{1,0:T(8,128)(2,1)S(1)} collective-permute-done((bf16[32,1024]{1,0:T(8,128)(2,1)S(1)}, bf16[32,1024]{1,0:T(8,128)(2,1)S(1)}, u32[]{:S(2)}, u32[]{:S(2)}) %collective-permute-start.1) | collective-permute-done | bytes 65568 | tf_op jit(solution)/shard_map/ppermute | solution.py:45
  9.5 1.5 %collective-permute-done.2.refs_2_ = bf16[32,1024]{1,0:T(8,128)(2,1)S(1)} collective-permute-done((bf16[32,1024]{1,0:T(8,128)(2,1)S(1)}, bf16[32,1024]{1,0:T(8,128)(2,1)S(1)}, u32[]{:S(2)}, u32[]{:S(2)}) %collective-permute-start.2) | collective-permute-done | bytes 65568 | tf_op jit(solution)/shard_map/ppermute | solution.py:45
  11.1 2.4 %collective-permute-done.3.refs_3_ = bf16[32,1024]{1,0:T(8,128)(2,1)S(1)} collective-permute-done((bf16[32,1024]{1,0:T(8,128)(2,1)S(1)}, bf16[32,1024]{1,0:T(8,128)(2,1)S(1)}, u32[]{:S(2)}, u32[]{:S(2)}) %collective-permute-start.3) | collective-permute-done | bytes 65568 | tf_op jit(solution)/shard_map/ppermute | solution.py:45
  13.5 3.7 %shard_map.79 = (bf16[4,32,1024]{2,1,0:T(8,128)(2,1)}, bf16[4,32,640]{2,1,0:T(8,128)(2,1)S(1)}) custom-call(bf16[32,1024]{1,0:T(8,128)(2,1)S(1)} %get-tuple-element.17.refs_0_, bf16[32,1024]{1,0:T(8,128)(2,1)S(1)} %collective-permute-done.1.refs_1_, bf16[32,1024]{1,0:T(8,128)(2,1)S(1)} %collective-permute-done.2.refs_2_, ...), custom_call_target="tpu_custom_call" | custom-call | flops 167772160 | bytes 11173888 | tf_op jit(solution)/shard_map/pallas_call | solution.py:32
  17.2 0.1 collective-permute-start.4
  17.3 1.3 %shard_map.83 = (bf16[64,1280]{1,0:T(8,128)(2,1)S(1)}, bf16[64,1280]{1,0:T(8,128)(2,1)S(1)}, bf16[64,1280]{1,0:T(8,128)(2,1)S(1)}, bf16[64,1280]{1,0:T(8,128)(2,1)S(1)}) custom-call(bf16[32,5120]{1,0:T(8,128)(2,1)} %bitcast.9, bf16[32,5120]{1,0:T(8,128)(2,1)} %bitcast.10), custom_call_target="tpu_custom_call" | custom-call | bytes 1310720 | tf_op jit(solution)/shard_map/pallas_call | solution.py:32
  18.6 1.6 %collective-permute-start.8 = (bf16[64,1280]{1,0:T(8,128)(2,1)S(1)}, bf16[64,1280]{1,0:T(8,128)(2,1)S(1)}, u32[]{:S(2)}, u32[]{:S(2)}) collective-permute-start(bf16[64,1280]{1,0:T(8,128)(2,1)S(1)} %get-tuple-element.28), channel_id=1, source_target_pairs={{0,8},{8,0},{16,24},{24,16},{1,9},{9,1},{17,25},{25,17},{2,10},{10... | collective-permute-start | bytes 491528 | tf_op jit(solution)/shard_map/ppermute | solution.py:45
  20.2 2.6 %collective-permute-start.9 = (bf16[64,1280]{1,0:T(8,128)(2,1)S(1)}, bf16[64,1280]{1,0:T(8,128)(2,1)S(1)}, u32[]{:S(2)}, u32[]{:S(2)}) collective-permute-start(bf16[64,1280]{1,0:T(8,128)(2,1)S(1)} %get-tuple-element.29), channel_id=1, source_target_pairs={{0,16},{8,24},{16,0},{24,8},{1,17},{9,25},{17,1},{25,9},{2,18},{10... | collective-permute-start | bytes 491528 | tf_op jit(solution)/shard_map/ppermute | solution.py:45
  22.8 3.4 %all-to-all-start = ((bf16[4,32,1024]{2,1,0:T(8,128)(2,1)}), bf16[4,32,1024]{2,1,0:T(8,128)(2,1)S(1)}, u32[]{:S(2)}, u32[]{:S(2)}) async-start(bf16[4,32,1024]{2,1,0:T(8,128)(2,1)} %get-tuple-element.21.merged_ref), calls=%async_computation | async-start | bytes 524288 | tf_op jit(solution)/shard_map/all_to_all | solution.py:241
  26.2 4.6 %shard_map.80.kept_ref = bf16[4,32,640]{2,1,0:T(8,128)(2,1)S(1)} custom-call(bf16[4,32,1024]{2,1,0:T(8,128)(2,1)} %get-tuple-element.21.merged_ref, bf16[5120,1024]{1,0:T(8,128)(2,1)} %w_ref.1), custom_call_target="tpu_custom_call" | custom-call | flops 167772160 | bytes 10911744 | tf_op jit(solution)/shard_map/pallas_call | solution.py:32
  30.8 0.0 collective-permute-done.4.came_ref
  30.9 0.6 %collective-permute-start.5 = (bf16[32,640]{1,0:T(8,128)(2,1)S(1)}, bf16[32,640]{1,0:T(8,128)(2,1)S(1)}, u32[]{:S(2)}, u32[]{:S(2)}) collective-permute-start(bf16[32,640]{1,0:T(8,128)(2,1)S(1)} %get-tuple-element.24), channel_id=1, source_target_pairs={{0,2},{1,3},{2,0},{3,1},{4,6},{5,7},{6,4},{7,5},{8,10},{9,11},{10,... | collective-permute-start | bytes 122888 | tf_op jit(solution)/shard_map/ppermute | solution.py:45
  31.5 0.5 collective-permute-start.6
  32.0 2.5 %collective-permute-start.7 = (bf16[32,640]{1,0:T(8,128)(2,1)S(1)}, bf16[32,640]{1,0:T(8,128)(2,1)S(1)}, u32[]{:S(2)}, u32[]{:S(2)}) collective-permute-start(bf16[32,640]{1,0:T(8,128)(2,1)S(1)} %get-tuple-element.26), channel_id=1, source_target_pairs={{0,6},{1,7},{2,4},{3,5},{4,2},{5,3},{6,0},{7,1},{8,14},{9,15},{10,... | collective-permute-start | bytes 122888 | tf_op jit(solution)/shard_map/ppermute | solution.py:45
  34.4 0.8 %dynamic-slice_bitcast_fusion.before_ref = bf16[32,640]{1,0:T(8,128)(2,1)S(1)} fusion(bf16[1,32,5120]{2,1,0:T(8,128)(2,1)} %param.8, s32[]{:T(128)S(6)} %select_n.3), kind=kLoop, calls=%fused_computation.1 | loop fusion | bytes 81924 | tf_op jit(solution)/shard_map/dynamic_slice | solution.py:242
  35.3 3.9 %collective-permute-start.10 = (bf16[64,1280]{1,0:T(8,128)(2,1)S(1)}, bf16[64,1280]{1,0:T(8,128)(2,1)S(1)}, u32[]{:S(2)}, u32[]{:S(2)}) collective-permute-start(bf16[64,1280]{1,0:T(8,128)(2,1)S(1)} %get-tuple-element.30), channel_id=1, source_target_pairs={{0,24},{8,16},{16,8},{24,0},{1,25},{9,17},{17,9},{25,1},{2,26},{10... | collective-permute-start | bytes 491528 | tf_op jit(solution)/shard_map/ppermute | solution.py:45
  39.1 0.0 collective-permute-done.6
  39.1 0.0 collective-permute-done.7
  39.2 0.0 copy-start
  39.2 1.6 %collective-permute-start.13 = (bf16[32,640]{1,0:T(8,128)(2,1)S(1)}, bf16[32,640]{1,0:T(8,128)(2,1)S(1)}, u32[]{:S(2)}, u32[]{:S(2)}) collective-permute-start(bf16[32,640]{1,0:T(8,128)(2,1)S(1)} %multiply_convert_fusion.refs_4_), channel_id=1, source_target_pairs={{0,24},{8,16},{16,8},{24,0},{1,25},{9,17},{17,9},{25,1},{2,26},{10... | collective-permute-start | bytes 122888 | tf_op jit(solution)/shard_map/ppermute | solution.py:45
  40.8 2.8 %collective-permute-start.11 = (bf16[32,640]{1,0:T(8,128)(2,1)S(1)}, bf16[32,640]{1,0:T(8,128)(2,1)S(1)}, u32[]{:S(2)}, u32[]{:S(2)}) collective-permute-start(bf16[32,640]{1,0:T(8,128)(2,1)S(1)} %multiply_convert_fusion.refs_4_), channel_id=1, source_target_pairs={{0,8},{8,0},{16,24},{24,16},{1,9},{9,1},{17,25},{25,17},{2,10},{10... | collective-permute-start | bytes 122888 | tf_op jit(solution)/shard_map/ppermute | solution.py:45
  43.6 1.5 %collective-permute-done.13.refs_7_ = bf16[32,640]{1,0:T(8,128)(2,1)S(1)} collective-permute-done((bf16[32,640]{1,0:T(8,128)(2,1)S(1)}, bf16[32,640]{1,0:T(8,128)(2,1)S(1)}, u32[]{:S(2)}, u32[]{:S(2)}) %collective-permute-start.13) | collective-permute-done | bytes 40992 | tf_op jit(solution)/shard_map/ppermute | solution.py:45
  45.1 3.5 %collective-permute-done.12.refs_6_ = bf16[32,640]{1,0:T(8,128)(2,1)S(1)} collective-permute-done((bf16[32,640]{1,0:T(8,128)(2,1)S(1)}, bf16[32,640]{1,0:T(8,128)(2,1)S(1)}, u32[]{:S(2)}, u32[]{:S(2)}) %collective-permute-start.12) | collective-permute-done | bytes 40992 | tf_op jit(solution)/shard_map/ppermute | solution.py:45
  48.7 2.0 %shard_map.84 = f32[1280,640]{1,0:T(8,128)} custom-call(bf16[64,1280]{1,0:T(8,128)(2,1)S(1)} %get-tuple-element.27.refs_0_, bf16[64,1280]{1,0:T(8,128)(2,1)S(1)} %collective-permute-done.8.refs_1_, bf16[64,1280]{1,0:T(8,128)(2,1)S(1)} %collective-permute-done.9.refs_2_, bf16[64,1280]{1,0:T(8,128)(2,1)S(1)} %collective-permute-done.10.refs_3_, ...), custom_call_target="tpu_custom_call" | custom-call | flops 209715200 | bytes 4096000 | tf_op jit(solution)/shard_map/pallas_call | solution.py:32
  50.7 2.7 %shard_map.85 = f32[1280,1024]{1,0:T(8,128)} custom-call(bf16[64,1280]{1,0:T(8,128)(2,1)S(1)} %get-tuple-element.27.refs_0_, bf16[64,1280]{1,0:T(8,128)(2,1)S(1)} %collective-permute-done.8.refs_1_, bf16[64,1280]{1,0:T(8,128)(2,1)S(1)} %collective-permute-done.9.refs_2_, bf16[64,1280]{1,0:T(8,128)(2,1)S(1)} %collective-permute-done.10.refs_3_, ...), custom_call_target="tpu_custom_call" | custom-call | flops 335544320 | bytes 6160384 | tf_op jit(solution)/shard_map/pallas_call | solution.py:32
  (12 shorter events, 0.1 us)
Async XLA Ops:
  2.1 2.0 %collective-permute-start = (bf16[4,32,1024]{2,1,0:T(8,128)(2,1)S(1)}, bf16[4,32,1024]{2,1,0:T(8,128)(2,1)S(1)}, u32[]{:S(2)}, u32[]{:S(2)}) collective-permute-start(bf16[4,32,1024]{2,1,0:T(8,128)(2,1)S(1)} %shard_map.77), channel_id=1, source_target_pairs={{0,1},{1,0},{2,3},{3,2},{4,5},{5,4},{6,7},{7,6},{8,9},{9,8},{10,11... | collective-permute-start | bytes 786440 | tf_op jit(solution)/shard_map/ppermute | solution.py:45
  4.2 5.3 %collective-permute-start.1 = (bf16[32,1024]{1,0:T(8,128)(2,1)S(1)}, bf16[32,1024]{1,0:T(8,128)(2,1)S(1)}, u32[]{:S(2)}, u32[]{:S(2)}) collective-permute-start(bf16[32,1024]{1,0:T(8,128)(2,1)S(1)} %get-tuple-element.18), channel_id=1, source_target_pairs={{0,2},{1,3},{2,0},{3,1},{4,6},{5,7},{6,4},{7,5},{8,10},{9,11},{10,... | collective-permute-start | bytes 196616 | tf_op jit(solution)/shard_map/ppermute | solution.py:45
  6.8 4.3 %collective-permute-start.2 = (bf16[32,1024]{1,0:T(8,128)(2,1)S(1)}, bf16[32,1024]{1,0:T(8,128)(2,1)S(1)}, u32[]{:S(2)}, u32[]{:S(2)}) collective-permute-start(bf16[32,1024]{1,0:T(8,128)(2,1)S(1)} %get-tuple-element.19), channel_id=1, source_target_pairs={{0,4},{1,5},{2,6},{3,7},{4,0},{5,1},{6,2},{7,3},{8,12},{9,13},{10,... | collective-permute-start | bytes 196616 | tf_op jit(solution)/shard_map/ppermute | solution.py:45
  8.3 5.2 %collective-permute-start.3 = (bf16[32,1024]{1,0:T(8,128)(2,1)S(1)}, bf16[32,1024]{1,0:T(8,128)(2,1)S(1)}, u32[]{:S(2)}, u32[]{:S(2)}) collective-permute-start(bf16[32,1024]{1,0:T(8,128)(2,1)S(1)} %get-tuple-element.20), channel_id=1, source_target_pairs={{0,6},{1,7},{2,4},{3,5},{4,2},{5,3},{6,0},{7,1},{8,14},{9,15},{10,... | collective-permute-start | bytes 196616 | tf_op jit(solution)/shard_map/ppermute | solution.py:45
  17.2 13.6 %collective-permute-start.4 = (bf16[4,32,640]{2,1,0:T(8,128)(2,1)S(1)}, bf16[4,32,640]{2,1,0:T(8,128)(2,1)S(1)}, u32[]{:S(2)}, u32[]{:S(2)}) collective-permute-start(bf16[4,32,640]{2,1,0:T(8,128)(2,1)S(1)} %get-tuple-element.22), channel_id=1, source_target_pairs={{0,1},{1,0},{2,3},{3,2},{4,5},{5,4},{6,7},{7,6},{8,9},{9,8},{10,11... | collective-permute-start | bytes 491528 | tf_op jit(solution)/shard_map/ppermute | solution.py:45
  18.6 22.2 %collective-permute-start.8 = (bf16[64,1280]{1,0:T(8,128)(2,1)S(1)}, bf16[64,1280]{1,0:T(8,128)(2,1)S(1)}, u32[]{:S(2)}, u32[]{:S(2)}) collective-permute-start(bf16[64,1280]{1,0:T(8,128)(2,1)S(1)} %get-tuple-element.28), channel_id=1, source_target_pairs={{0,8},{8,0},{16,24},{24,16},{1,9},{9,1},{17,25},{25,17},{2,10},{10... | collective-permute-start | bytes 491528 | tf_op jit(solution)/shard_map/ppermute | solution.py:45
  20.2 23.4 %collective-permute-start.9 = (bf16[64,1280]{1,0:T(8,128)(2,1)S(1)}, bf16[64,1280]{1,0:T(8,128)(2,1)S(1)}, u32[]{:S(2)}, u32[]{:S(2)}) collective-permute-start(bf16[64,1280]{1,0:T(8,128)(2,1)S(1)} %get-tuple-element.29), channel_id=1, source_target_pairs={{0,16},{8,24},{16,0},{24,8},{1,17},{9,25},{17,1},{25,9},{2,18},{10... | collective-permute-start | bytes 491528 | tf_op jit(solution)/shard_map/ppermute | solution.py:45
  22.8 27.9 %all-to-all-start = ((bf16[4,32,1024]{2,1,0:T(8,128)(2,1)}), bf16[4,32,1024]{2,1,0:T(8,128)(2,1)S(1)}, u32[]{:S(2)}, u32[]{:S(2)}) async-start(bf16[4,32,1024]{2,1,0:T(8,128)(2,1)} %get-tuple-element.21.merged_ref), calls=%async_computation | async-start | bytes 524288 | tf_op jit(solution)/shard_map/all_to_all | solution.py:241
  30.9 4.4 %collective-permute-start.5 = (bf16[32,640]{1,0:T(8,128)(2,1)S(1)}, bf16[32,640]{1,0:T(8,128)(2,1)S(1)}, u32[]{:S(2)}, u32[]{:S(2)}) collective-permute-start(bf16[32,640]{1,0:T(8,128)(2,1)S(1)} %get-tuple-element.24), channel_id=1, source_target_pairs={{0,2},{1,3},{2,0},{3,1},{4,6},{5,7},{6,4},{7,5},{8,10},{9,11},{10,... | collective-permute-start | bytes 122888 | tf_op jit(solution)/shard_map/ppermute | solution.py:45
  31.5 7.7 %collective-permute-start.6 = (bf16[32,640]{1,0:T(8,128)(2,1)S(1)}, bf16[32,640]{1,0:T(8,128)(2,1)S(1)}, u32[]{:S(2)}, u32[]{:S(2)}) collective-permute-start(bf16[32,640]{1,0:T(8,128)(2,1)S(1)} %get-tuple-element.25), channel_id=1, source_target_pairs={{0,4},{1,5},{2,6},{3,7},{4,0},{5,1},{6,2},{7,3},{8,12},{9,13},{10,... | collective-permute-start | bytes 122888 | tf_op jit(solution)/shard_map/ppermute | solution.py:45
  32.0 7.2 %collective-permute-start.7 = (bf16[32,640]{1,0:T(8,128)(2,1)S(1)}, bf16[32,640]{1,0:T(8,128)(2,1)S(1)}, u32[]{:S(2)}, u32[]{:S(2)}) collective-permute-start(bf16[32,640]{1,0:T(8,128)(2,1)S(1)} %get-tuple-element.26), channel_id=1, source_target_pairs={{0,6},{1,7},{2,4},{3,5},{4,2},{5,3},{6,0},{7,1},{8,14},{9,15},{10,... | collective-permute-start | bytes 122888 | tf_op jit(solution)/shard_map/ppermute | solution.py:45
  35.3 8.4 %collective-permute-start.10 = (bf16[64,1280]{1,0:T(8,128)(2,1)S(1)}, bf16[64,1280]{1,0:T(8,128)(2,1)S(1)}, u32[]{:S(2)}, u32[]{:S(2)}) collective-permute-start(bf16[64,1280]{1,0:T(8,128)(2,1)S(1)} %get-tuple-element.30), channel_id=1, source_target_pairs={{0,24},{8,16},{16,8},{24,0},{1,25},{9,17},{17,9},{25,1},{2,26},{10... | collective-permute-start | bytes 491528 | tf_op jit(solution)/shard_map/ppermute | solution.py:45
  39.2 14.3 %copy-start = (bf16[32,640]{1,0:T(8,128)(2,1)}, bf16[32,640]{1,0:T(8,128)(2,1)S(1)}, u32[]{:S(2)}) copy-start(bf16[32,640]{1,0:T(8,128)(2,1)S(1)} %multiply_convert_fusion.refs_4_) | copy-start | bytes 122884
  39.2 6.0 %collective-permute-start.13 = (bf16[32,640]{1,0:T(8,128)(2,1)S(1)}, bf16[32,640]{1,0:T(8,128)(2,1)S(1)}, u32[]{:S(2)}, u32[]{:S(2)}) collective-permute-start(bf16[32,640]{1,0:T(8,128)(2,1)S(1)} %multiply_convert_fusion.refs_4_), channel_id=1, source_target_pairs={{0,24},{8,16},{16,8},{24,0},{1,25},{9,17},{17,9},{25,1},{2,26},{10... | collective-permute-start | bytes 122888 | tf_op jit(solution)/shard_map/ppermute | solution.py:45
  40.8 7.9 %collective-permute-start.12 = (bf16[32,640]{1,0:T(8,128)(2,1)S(1)}, bf16[32,640]{1,0:T(8,128)(2,1)S(1)}, u32[]{:S(2)}, u32[]{:S(2)}) collective-permute-start(bf16[32,640]{1,0:T(8,128)(2,1)S(1)} %multiply_convert_fusion.refs_4_), channel_id=1, source_target_pairs={{0,16},{8,24},{16,0},{24,8},{1,17},{9,25},{17,1},{25,9},{2,18},{10... | collective-permute-start | bytes 122888 | tf_op jit(solution)/shard_map/ppermute | solution.py:45
  40.8 7.9 %collective-permute-start.11 = (bf16[32,640]{1,0:T(8,128)(2,1)S(1)}, bf16[32,640]{1,0:T(8,128)(2,1)S(1)}, u32[]{:S(2)}, u32[]{:S(2)}) collective-permute-start(bf16[32,640]{1,0:T(8,128)(2,1)S(1)} %multiply_convert_fusion.refs_4_), channel_id=1, source_target_pairs={{0,8},{8,0},{16,24},{24,16},{1,9},{9,1},{17,25},{25,17},{2,10},{10... | collective-permute-start | bytes 122888 | tf_op jit(solution)/shard_map/ppermute | solution.py:45

commit v3 on v2

v3 whole, which is shorter than its diff:
```python
import functools
import math

import jax
import jax.numpy as jnp
from jax import lax
from jax.experimental import pallas as pl
from jax.experimental.pallas import tpu as pltpu
from jax.sharding import PartitionSpec as P


inv_root_two = 1.0 / math.sqrt(2.0)
inv_root_two_pi = 1.0 / math.sqrt(2.0 * math.pi)
VMEM = pl.BlockSpec(memory_space=pltpu.VMEM)
HBM = pl.BlockSpec(memory_space=pltpu.HBM)
shape = jax.ShapeDtypeStruct


def gelu_slope(values):
    return (
        0.5 * (1.0 + lax.erf(values * inv_root_two))
        + values * jnp.exp(-0.5 * values * values) * inv_root_two_pi
    )


def gelu(values):
    return 0.5 * values * (1.0 + lax.erf(values * inv_root_two))


def call(kernel, outs, args, flops=0, in_specs=None, out_specs=None, scratch=(), limit=4 << 20):
    moved = sum(math.prod(a.shape) * a.dtype.itemsize for a in list(outs) + list(args))
    return pl.pallas_call(
        kernel,
        out_shape=outs,
        in_specs=in_specs or [VMEM] * len(args),
        out_specs=out_specs or [VMEM] * len(outs),
        scratch_shapes=scratch,
        cost_estimate=pl.CostEstimate(flops=flops, bytes_accessed=moved, transcendentals=0),
        compiler_params=pltpu.CompilerParams(vmem_limit_bytes=limit),
    )(*args)


def exchange(block, axis, step):
    pairs = [(i, i ^ step) for i in range(lax.axis_size(axis))]
    return lax.ppermute(block, axis, pairs)


def front(halves, groups, aligned, *refs):
    dest_ref, slots_ref, before_ref, inputs_ref = refs[:4]
    placed_refs, rest = refs[4:6], refs[6:]
    feature_refs = rest[: groups * aligned]
    slope_refs = rest[groups * aligned : (groups + 1) * aligned]
    held_dest, held, held_before, held_own, sems = rest[(groups + 1) * aligned :]
    _, merged_count, columns = placed_refs[0].shape
    shard, group = lax.axis_index("roll"), lax.axis_index("enc")
    started = iter(range(sems.shape[0]))

    def fetch(source, target):
        copy = pltpu.make_async_copy(source, target, sems.at[next(started)])
        copy.start()
        return copy

    def cut(index, size):
        return pl.ds(pl.multiple_of(index * size, size), size)

    dest_copy = fetch(dest_ref, held_dest)
    slot_copies = [
        fetch(slots_ref.at[:, cut(shard ^ (2 * j + parity), columns)], held.at[parity, j])
        for parity in (1, 0)
        for j in range(halves)
    ]
    before_copies, input_copies = [], []
    for k, ref in enumerate(feature_refs):
        size = ref.shape[1]
        before_copies.append(fetch(before_ref.at[:, cut(group ^ k, size)], held_before.at[k]))
        input_copies.append(
            fetch(inputs_ref.at[:, cut(group ^ k, size)], ref.at[pl.ds(merged_count, merged_count), :])
        )
    own_copies = [fetch(before_ref.at[:, cut(shard, ref.shape[1])], held_own) for ref in slope_refs]
    dest_copy.wait()
    rows = lax.broadcasted_iota(jnp.int32, (merged_count, held.shape[2]), 0)
    picker = jnp.where(rows == held_dest[...], 1.0, 0.0).astype(jnp.bfloat16)
    slot_copies = iter(slot_copies)
    for parity in (1, 0):
        for j in range(halves):
            next(slot_copies).wait()
            placed_refs[parity][j] = jnp.dot(
                picker, held[parity, j], preferred_element_type=jnp.float32
            ).astype(jnp.bfloat16)
    for k, copy in enumerate(before_copies):
        copy.wait()
        feature_refs[k][:merged_count, :] = gelu(held_before[k].astype(jnp.float32)).astype(jnp.bfloat16)
    for ref, copy in zip(slope_refs, own_copies):
        copy.wait()
        ref[...] = gelu_slope(held_own[...].astype(jnp.float32))
    for copy in input_copies:
        copy.wait()


def load(source_ref, out_ref, sems):
    size = source_ref.shape[0] // sems.shape[0]
    copies = []
    for j in range(sems.shape[0]):
        cut = pl.ds(j * size, size)
        copies.append(pltpu.make_async_copy(source_ref.at[cut, :], out_ref.at[cut, :], sems.at[j]))
        copies[-1].start()
    for copy in copies:
        copy.wait()


def join(*refs):
    *piece_refs, out_ref = refs
    first = 0
    for ref in piece_refs:
        out_ref[first : first + ref.shape[0], :] = ref[...]
        first += ref.shape[0]


def pair_sum(kept_ref, came_ref, *out_refs):
    for j, out_ref in enumerate(out_refs):
        out_ref[...] = (kept_ref[j].astype(jnp.float32) + came_ref[j].astype(jnp.float32)).astype(jnp.bfloat16)


def unit_blocks(parity, merged, w_ref, out_ref):
    shard = lax.axis_index("roll")
    halves, _, unit_cols = out_ref.shape
    for j in range(halves):
        first = pl.multiple_of((shard ^ (2 * j + parity)) * unit_cols, unit_cols)
        out_ref[j] = lax.dot_general(
            merged, w_ref[pl.ds(first, unit_cols), :], (((1,), (1,)), ((), ())), preferred_element_type=jnp.float32
        ).astype(jnp.bfloat16)


def first_units(*refs):
    *piece_refs, w_ref, merged_ref, out_ref = refs
    total = piece_refs[0][...].astype(jnp.float32)
    for piece_ref in piece_refs[1:]:
        total = total + piece_ref[...].astype(jnp.float32)
    merged_ref[...] = total.astype(jnp.bfloat16)
    unit_blocks(1, merged_ref[...], w_ref, out_ref)


def second_units(merged_ref, w_ref, out_ref):
    unit_blocks(0, merged_ref[...], w_ref, out_ref)


def write_products(left_of, right, factor, out_ref, held, sems):
    size = held.shape[1]
    copies = []
    for j in range(held.shape[0]):
        held[j] = lax.dot_general(
            left_of(j * size, size), right, (((0,), (0,)), ((), ())), preferred_element_type=jnp.float32
        ) * factor
        copies.append(pltpu.make_async_copy(held.at[j], out_ref.at[pl.ds(j * size, size), :], sems.at[j]))
        copies[-1].start()
    for copy in copies:
        copy.wait()


def block_products(part, factor, groups, *refs):
    feature_refs, right_refs, (out_ref, held, sems) = refs[:groups], refs[groups:-3], refs[-3:]
    rows = feature_refs[0].shape[0] // 2
    half = slice(part * rows, (part + 1) * rows)

    def left_of(first, size):
        return jnp.concatenate([ref[half, first : first + size] for ref in feature_refs], axis=0)

    right = jnp.concatenate([ref[...] for ref in right_refs], axis=0)
    write_products(left_of, right, factor, out_ref, held, sems)


def products(part, factor, features, rights, columns):
    groups, (rows, in_cols) = len(features), features[0].shape
    size = next((s for s in (256, 128) if in_cols % s == 0), in_cols)
    out = shape((in_cols, columns), jnp.float32)
    (result,) = call(
        functools.partial(block_products, part, factor, groups), [out], (*features, *rights), groups * rows * in_cols * columns,
        out_specs=[HBM],
        scratch=[pltpu.VMEM((in_cols // size, size, columns), jnp.float32), pltpu.SemaphoreType.DMA((in_cols // size,))],
        limit=(6 << 20) + 4 * in_cols * columns,
    )
    return result


def body(row_grads, row_dest, merger_in, hidden_pre, w_second):
    slots = row_grads[0]
    slot_count = slots.shape[0]
    before, inputs = hidden_pre[0], merger_in[0]
    merged_count, width = before.shape
    shards = lax.axis_size("roll")
    groups = lax.axis_size("enc")
    halves = shards // 2
    columns = slots.shape[1] // shards
    unit_cols = width // shards
    in_cols = width // groups
    kind = jnp.bfloat16
    aligned = in_cols % 128 == 0 and unit_cols % 128 == 0

    def spread(kept, came):
        blocks = call(pair_sum, [shape(kept.shape[1:], kind)] * halves, (kept, came), kept.size)
        return [blocks[0]] + [exchange(blocks[j], "roll", 2 * j) for j in range(1, halves)]

    place = (halves, merged_count, columns)
    outs = [shape(place, kind)] * 2
    if aligned:
        outs += [shape((2 * merged_count, in_cols), kind)] * groups + [shape((merged_count, unit_cols), jnp.float32)]
    sources = [pltpu.with_memory_space_constraint(x, pltpu.HBM) for x in (row_dest, slots, before, inputs)]
    scratch = [
        pltpu.VMEM(row_dest.shape, row_dest.dtype),
        pltpu.VMEM((2, halves, slot_count, columns), kind),
        pltpu.VMEM((groups, merged_count, in_cols), kind),
        pltpu.VMEM((merged_count, unit_cols), kind),
        pltpu.SemaphoreType.DMA((2 + 2 * halves + 2 * groups,)),
    ]
    kept, sent, *rest = call(
        functools.partial(front, halves, groups, int(aligned)), outs, sources,
        2 * slot_count * slots.size, in_specs=[HBM] * 4, scratch=scratch, limit=12 << 20,
    )
    if aligned:
        *blocks, slope = rest
    else:
        both = jnp.concatenate([gelu(before.astype(jnp.float32)).astype(kind), inputs], axis=0)
        group = lax.axis_index("enc")
        blocks = [lax.dynamic_slice_in_dim(both, (group ^ k) * in_cols, in_cols, 1) for k in range(groups)]
        own = lax.dynamic_slice_in_dim(before, lax.axis_index("roll") * unit_cols, unit_cols, 1)
        slope = gelu_slope(own.astype(jnp.float32))
    features = [blocks[0]] + [exchange(blocks[k], "enc", k) for k in range(1, groups)]

    pieces = spread(kept, exchange(sent, "roll", 1))
    (weights,) = call(
        load, [shape(w_second.shape, kind)], (pltpu.with_memory_space_constraint(w_second, pltpu.HBM),),
        in_specs=[HBM], scratch=[pltpu.SemaphoreType.DMA((8,))],
    )

    unit_shape = (halves, merged_count, unit_cols)
    flops = 2 * columns * math.prod(unit_shape)
    merged, sent = call(
        first_units, [shape((merged_count, columns), kind), shape(unit_shape, kind)], (*pieces, weights), flops,
    )
    came = exchange(sent, "roll", 1)
    (kept,) = call(second_units, [shape(unit_shape, kind)], (merged, weights), flops)

    merged_all = [merged]
    step = 1
    while step < groups:
        (whole,) = merged_all if step == 1 else call(join, [shape((step * merged_count, columns), kind)], merged_all)
        merged_all = [whole, exchange(whole, "enc", step)]
        step *= 2

    pieces = spread(kept, came)
    grads = (sum(piece.astype(jnp.float32) for piece in pieces) * slope).astype(kind)
    grads_all = [grads] + [exchange(grads, "enc", k) for k in range(1, groups)]

    factor = 1.0 / math.sqrt(merged_count * groups)
    grad_second = products(0, factor, features, merged_all, columns)
    grad_first = products(1, factor, features, grads_all, unit_cols)
    return (grads[None], grad_first, grad_second)


def solution(mesh):
    return jax.shard_map(
        body,
        mesh=mesh,
        in_specs=(
            P("enc", "roll", None),
            P("enc", "roll"),
            P("enc", None, None),
            P("enc", None, None),
            P(None, "roll"),
        ),
        out_specs=(P("enc", None, "roll"), P("enc", "roll"), P("enc", "roll")),
        check_vma=False,
    )
```

time: 53.9 us -> 53.4 us (level)
  waiting for transfers between devices: 10.2 us -> 19 us
  starting transfers between devices: 24.3 us -> 18.8 us
  Pallas kernels: 17.4 us -> 14.6 us
  local copies, waits for them, and re-layouts: 0.79 us -> 0.01 us
    ppermute x14 -> x16, waiting for transfers between devices: 10.2 us -> 19 us  [exchange(): return lax.ppermute(block, axis, pairs)]
    all_to_all x1 -> x0, starting transfers between devices: 3.41 us -> none  [body(): lax.all_to_all(copies, 'enc', split_axis=0, concat_axis=0, tiled=True)]
    pallas_call x10 -> x9, Pallas kernels: 17.4 us -> 14.6 us  [call(): pl.pallas_call(kernel, out_shape=outs, in_specs=in_specs or [VMEM] * len(...]
    ppermute x14 -> x16, starting transfers between devices: 20.9 us -> 18.8 us  [exchange(): return lax.ppermute(block, axis, pairs)]
    dynamic_slice x1 -> x0, local copies, waits for them, and re-layouts: 0.78 us -> none  [body(): own = lax.dynamic_slice_in_dim(before, shard * unit_cols, unit_cols, 1)]
  transfers between devices with their start and end apart: 15 -> 16, of which waited for: 5 -> 5; matrix products, arithmetic and copies ran while one was open for 2% -> 0% of each run, Pallas kernels for 18% -> 16%
where the time goes in v3:
time: 53.4 us; the launch traced here: 53.2 us
  waiting for transfers between devices  19 us (36%)
  starting transfers between devices  18.8 us (35%)
  Pallas kernels  14.6 us (27%)
  between operations  0.76 us (1%)
    ppermute x16, waiting for transfers between devices, exchange(): return lax.ppermute(block, axis, pairs)  19 us
    ppermute x16, starting transfers between devices, exchange(): return lax.ppermute(block, axis, pairs)  18.8 us
    pallas_call x9, Pallas kernels, call(): pl.pallas_call(kernel, out_shape=outs, in_specs=in_specs or [VMEM] * len(...  14.6 us
  transfers between devices with their start and end apart: 16, of which 5 were waited for; matrix products, arithmetic and copies ran while one was open for 0% of the time, Pallas kernels for 16%

profile of v3, /device:TPU:0, one launch (start us, length us, event | category | flops | bytes accessed | tf_op | source)
XLA Modules:
  0.0 53.2 jit_solution(14004528704786905558)
XLA Ops:
  0.6 2.4 %shard_map.76 = (bf16[4,32,1024]{2,1,0:T(8,128)(2,1)S(1)}, bf16[4,32,1024]{2,1,0:T(8,128)(2,1)S(1)}, bf16[64,1280]{1,0:T(8,128)(2,1)S(1)}, bf16[64,1280]{1,0:T(8...) custom-call(s32[1,32]{1,0:T(1,128)} %refs_0_.1, ...), custom_call_target="tpu_custom_call" | custom-call | flops 16777216 | bytes 2441344 | tf_op jit(solution)/shard_map/pallas_call | solution.py:32
  3.0 0.6 %collective-permute-start = (bf16[4,32,1024]{2,1,0:T(8,128)(2,1)S(1)}, bf16[4,32,1024]{2,1,0:T(8,128)(2,1)S(1)}, u32[]{:S(2)}, u32[]{:S(2)}) collective-permute-start(bf16[4,32,1024]{2,1,0:T(8,128)(2,1)S(1)} %get-tuple-element.21), channel_id=1, source_target_pairs={{0,1},{1,0},{2,3},{3,2},{4,5},{5,4},{6,7},{7,6},{8,9},{9,8},{10,11... | collective-permute-start | bytes 786440 | tf_op jit(solution)/shard_map/ppermute | solution.py:45
  3.6 1.2 %collective-permute-done.came_ref = bf16[4,32,1024]{2,1,0:T(8,128)(2,1)S(1)} collective-permute-done((bf16[4,32,1024]{2,1,0:T(8,128)(2,1)S(1)}, bf16[4,32,1024]{2,1,0:T(8,128)(2,1)S(1)}, u32[]{:S(2)}, u32[]{:S(2)}) %collective-permute-start) | collective-permute-done | bytes 262176 | tf_op jit(solution)/shard_map/ppermute | solution.py:45
  4.7 0.1 shard_map.77
  4.8 2.9 %collective-permute-start.1 = (bf16[32,1024]{1,0:T(8,128)(2,1)S(1)}, bf16[32,1024]{1,0:T(8,128)(2,1)S(1)}, u32[]{:S(2)}, u32[]{:S(2)}) collective-permute-start(bf16[32,1024]{1,0:T(8,128)(2,1)S(1)} %get-tuple-element.23), channel_id=1, source_target_pairs={{0,2},{1,3},{2,0},{3,1},{4,6},{5,7},{6,4},{7,5},{8,10},{9,11},{10,... | collective-permute-start | bytes 196616 | tf_op jit(solution)/shard_map/ppermute | solution.py:45
  7.7 1.5 %collective-permute-start.2 = (bf16[32,1024]{1,0:T(8,128)(2,1)S(1)}, bf16[32,1024]{1,0:T(8,128)(2,1)S(1)}, u32[]{:S(2)}, u32[]{:S(2)}) collective-permute-start(bf16[32,1024]{1,0:T(8,128)(2,1)S(1)} %get-tuple-element.24), channel_id=1, source_target_pairs={{0,4},{1,5},{2,6},{3,7},{4,0},{5,1},{6,2},{7,3},{8,12},{9,13},{10,... | collective-permute-start | bytes 196616 | tf_op jit(solution)/shard_map/ppermute | solution.py:45
  9.2 0.0 collective-permute-start.3
  9.3 4.1 %shard_map.78.refs_4_.w_ref = bf16[5120,1024]{1,0:T(8,128)(2,1)S(1)} custom-call(bf16[5120,1024]{1,0:T(8,128)(2,1)} %source_ref.1), custom_call_target="tpu_custom_call" | custom-call | bytes 20971520 | tf_op jit(solution)/shard_map/pallas_call | solution.py:32
  13.4 0.0 collective-permute-done.2.refs_2_
  13.4 1.0 %collective-permute-done.3.refs_3_ = bf16[32,1024]{1,0:T(8,128)(2,1)S(1)} collective-permute-done((bf16[32,1024]{1,0:T(8,128)(2,1)S(1)}, bf16[32,1024]{1,0:T(8,128)(2,1)S(1)}, u32[]{:S(2)}, u32[]{:S(2)}) %collective-permute-start.3) | collective-permute-done | bytes 65568 | tf_op jit(solution)/shard_map/ppermute | solution.py:45
  14.4 1.6 %shard_map.79 = (bf16[32,1024]{1,0:T(8,128)(2,1)S(1)}, bf16[4,32,640]{2,1,0:T(8,128)(2,1)S(1)}) custom-call(bf16[32,1024]{1,0:T(8,128)(2,1)S(1)} %get-tuple-element.22.refs_0_, bf16[32,1024]{1,0:T(8,128)(2,1)S(1)} %collective-permute-done.1.refs_1_, bf16[32,1024]{1,0:T(8,128)(2,1)S(1)} %collective-permute-done.2.refs_2_, ...), custom_call_target="tpu_custom_call" | custom-call | flops 167772160 | bytes 10977280 | tf_op jit(solution)/shard_map/pallas_call | solution.py:32
  16.0 0.0 collective-permute-start.4
  16.1 1.6 %collective-permute-start.14 = (bf16[32,1024]{1,0:T(8,128)(2,1)S(1)}, bf16[32,1024]{1,0:T(8,128)(2,1)S(1)}, u32[]{:S(2)}, u32[]{:S(2)}) collective-permute-start(bf16[32,1024]{1,0:T(8,128)(2,1)S(1)} %get-tuple-element.26.merged_ref.refs_0_), channel_id=1, source_target_pairs={{0,8},{8,0},{16,24},{24,16},{1,9},{9,1},{17,25},{25,17},{2,10},{10... | collective-permute-start | bytes 196616 | tf_op jit(solution)/shard_map/ppermute | solution.py:45
  17.7 1.6 %shard_map.80.kept_ref = bf16[4,32,640]{2,1,0:T(8,128)(2,1)S(1)} custom-call(bf16[32,1024]{1,0:T(8,128)(2,1)S(1)} %get-tuple-element.26.merged_ref.refs_0_, bf16[5120,1024]{1,0:T(8,128)(2,1)S(1)} %shard_map.78.refs_4_.w_ref), custom_call_target="tpu_custom_call" | custom-call | flops 167772160 | bytes 10715136 | tf_op jit(solution)/shard_map/pallas_call | solution.py:32
  19.3 0.0 collective-permute-done.4.came_ref
  19.4 1.0 %collective-permute-start.5 = (bf16[32,640]{1,0:T(8,128)(2,1)S(1)}, bf16[32,640]{1,0:T(8,128)(2,1)S(1)}, u32[]{:S(2)}, u32[]{:S(2)}) collective-permute-start(bf16[32,640]{1,0:T(8,128)(2,1)S(1)} %get-tuple-element.29), channel_id=1, source_target_pairs={{0,2},{1,3},{2,0},{3,1},{4,6},{5,7},{6,4},{7,5},{8,10},{9,11},{10,... | collective-permute-start | bytes 122888 | tf_op jit(solution)/shard_map/ppermute | solution.py:45
  20.4 1.5 %collective-permute-start.6 = (bf16[32,640]{1,0:T(8,128)(2,1)S(1)}, bf16[32,640]{1,0:T(8,128)(2,1)S(1)}, u32[]{:S(2)}, u32[]{:S(2)}) collective-permute-start(bf16[32,640]{1,0:T(8,128)(2,1)S(1)} %get-tuple-element.30), channel_id=1, source_target_pairs={{0,4},{1,5},{2,6},{3,7},{4,0},{5,1},{6,2},{7,3},{8,12},{9,13},{10,... | collective-permute-start | bytes 122888 | tf_op jit(solution)/shard_map/ppermute | solution.py:45
  21.9 1.0 %collective-permute-start.7 = (bf16[32,640]{1,0:T(8,128)(2,1)S(1)}, bf16[32,640]{1,0:T(8,128)(2,1)S(1)}, u32[]{:S(2)}, u32[]{:S(2)}) collective-permute-start(bf16[32,640]{1,0:T(8,128)(2,1)S(1)} %get-tuple-element.31), channel_id=1, source_target_pairs={{0,6},{1,7},{2,4},{3,5},{4,2},{5,3},{6,0},{7,1},{8,14},{9,15},{10,... | collective-permute-start | bytes 122888 | tf_op jit(solution)/shard_map/ppermute | solution.py:45
  23.0 0.4 collective-permute-start.8
  23.4 0.0 collective-permute-done.14.refs_1_
  23.4 2.6 %collective-permute-start.9 = (bf16[64,1280]{1,0:T(8,128)(2,1)S(1)}, bf16[64,1280]{1,0:T(8,128)(2,1)S(1)}, u32[]{:S(2)}, u32[]{:S(2)}) collective-permute-start(bf16[64,1280]{1,0:T(8,128)(2,1)S(1)} %get-tuple-element.35), channel_id=1, source_target_pairs={{0,16},{8,24},{16,0},{24,8},{1,17},{9,25},{17,1},{25,9},{2,18},{10... | collective-permute-start | bytes 491528 | tf_op jit(solution)/shard_map/ppermute | solution.py:45
  26.0 1.4 %collective-permute-start.10 = (bf16[64,1280]{1,0:T(8,128)(2,1)S(1)}, bf16[64,1280]{1,0:T(8,128)(2,1)S(1)}, u32[]{:S(2)}, u32[]{:S(2)}) collective-permute-start(bf16[64,1280]{1,0:T(8,128)(2,1)S(1)} %get-tuple-element.36), channel_id=1, source_target_pairs={{0,24},{8,16},{16,8},{24,0},{1,25},{9,17},{17,9},{25,1},{2,26},{10... | collective-permute-start | bytes 491528 | tf_op jit(solution)/shard_map/ppermute | solution.py:45
  27.4 1.7 %collective-permute-start.15 = (bf16[64,1024]{1,0:T(8,128)(2,1)S(1)}, bf16[64,1024]{1,0:T(8,128)(2,1)S(1)}, u32[]{:S(2)}, u32[]{:S(2)}) collective-permute-start(bf16[64,1024]{1,0:T(8,128)(2,1)S(1)} %shard_map.83.refs_4_), channel_id=1, source_target_pairs={{0,16},{8,24},{16,0},{24,8},{1,17},{9,25},{17,1},{25,9},{2,18},{10... | collective-permute-start | bytes 393224 | tf_op jit(solution)/shard_map/ppermute | solution.py:45
  29.2 0.0 copy-start
  29.2 1.0 %collective-permute-start.13 = (bf16[32,640]{1,0:T(8,128)(2,1)S(1)}, bf16[32,640]{1,0:T(8,128)(2,1)S(1)}, u32[]{:S(2)}, u32[]{:S(2)}) collective-permute-start(bf16[32,640]{1,0:T(8,128)(2,1)S(1)} %multiply_convert_fusion.refs_4_), channel_id=1, source_target_pairs={{0,24},{8,16},{16,8},{24,0},{1,25},{9,17},{17,9},{25,1},{2,26},{10... | collective-permute-start | bytes 122888 | tf_op jit(solution)/shard_map/ppermute | solution.py:45
  30.2 1.3 %collective-permute-done.8.refs_1_ = bf16[64,1280]{1,0:T(8,128)(2,1)S(1)} collective-permute-done((bf16[64,1280]{1,0:T(8,128)(2,1)S(1)}, bf16[64,1280]{1,0:T(8,128)(2,1)S(1)}, u32[]{:S(2)}, u32[]{:S(2)}) %collective-permute-start.8) | collective-permute-done | bytes 163872 | tf_op jit(solution)/shard_map/ppermute | solution.py:45
  31.6 1.1 %collective-permute-start.12 = (bf16[32,640]{1,0:T(8,128)(2,1)S(1)}, bf16[32,640]{1,0:T(8,128)(2,1)S(1)}, u32[]{:S(2)}, u32[]{:S(2)}) collective-permute-start(bf16[32,640]{1,0:T(8,128)(2,1)S(1)} %multiply_convert_fusion.refs_4_), channel_id=1, source_target_pairs={{0,16},{8,24},{16,0},{24,8},{1,17},{9,25},{17,1},{25,9},{2,18},{10... | collective-permute-start | bytes 122888 | tf_op jit(solution)/shard_map/ppermute | solution.py:45
  32.6 9.8 %collective-permute-done.9.refs_2_ = bf16[64,1280]{1,0:T(8,128)(2,1)S(1)} collective-permute-done((bf16[64,1280]{1,0:T(8,128)(2,1)S(1)}, bf16[64,1280]{1,0:T(8,128)(2,1)S(1)}, u32[]{:S(2)}, u32[]{:S(2)}) %collective-permute-start.9) | collective-permute-done | bytes 163872 | tf_op jit(solution)/shard_map/ppermute | solution.py:45
  42.4 0.3 collective-permute-start.11
  42.7 5.7 %collective-permute-done.15.refs_5_ = bf16[64,1024]{1,0:T(8,128)(2,1)S(1)} collective-permute-done((bf16[64,1024]{1,0:T(8,128)(2,1)S(1)}, bf16[64,1024]{1,0:T(8,128)(2,1)S(1)}, u32[]{:S(2)}, u32[]{:S(2)}) %collective-permute-start.15) | collective-permute-done | bytes 131104 | tf_op jit(solution)/shard_map/ppermute | solution.py:45
  48.4 2.7 %shard_map.84 = f32[1280,1024]{1,0:T(8,128)} custom-call(bf16[64,1280]{1,0:T(8,128)(2,1)S(1)} %get-tuple-element.33.refs_0_, bf16[64,1280]{1,0:T(8,128)(2,1)S(1)} %collective-permute-done.8.refs_1_, bf16[64,1280]{1,0:T(8,128)(2,1)S(1)} %collective-permute-done.9.refs_2_, bf16[64,1280]{1,0:T(8,128)(2,1)S(1)} %collective-permute-done.10.refs_3_, ...), custom_call_target="tpu_custom_call" | custom-call | flops 335544320 | bytes 6160384 | tf_op jit(solution)/shard_map/pallas_call | solution.py:32
  51.2 2.0 %shard_map.82 = f32[1280,640]{1,0:T(8,128)} custom-call(bf16[64,1280]{1,0:T(8,128)(2,1)S(1)} %get-tuple-element.33.refs_0_, bf16[64,1280]{1,0:T(8,128)(2,1)S(1)} %collective-permute-done.8.refs_1_, bf16[64,1280]{1,0:T(8,128)(2,1)S(1)} %collective-permute-done.9.refs_2_, bf16[64,1280]{1,0:T(8,128)(2,1)S(1)} %collective-permute-done.10.refs_3_, ...), custom_call_target="tpu_custom_call" | custom-call | flops 209715200 | bytes 4096000 | tf_op jit(solution)/shard_map/pallas_call | solution.py:32
  (12 shorter events, 0.1 us)
Async XLA Ops:
  3.0 1.7 %collective-permute-start = (bf16[4,32,1024]{2,1,0:T(8,128)(2,1)S(1)}, bf16[4,32,1024]{2,1,0:T(8,128)(2,1)S(1)}, u32[]{:S(2)}, u32[]{:S(2)}) collective-permute-start(bf16[4,32,1024]{2,1,0:T(8,128)(2,1)S(1)} %get-tuple-element.21), channel_id=1, source_target_pairs={{0,1},{1,0},{2,3},{3,2},{4,5},{5,4},{6,7},{7,6},{8,9},{9,8},{10,11... | collective-permute-start | bytes 786440 | tf_op jit(solution)/shard_map/ppermute | solution.py:45
  4.8 8.5 %collective-permute-start.1 = (bf16[32,1024]{1,0:T(8,128)(2,1)S(1)}, bf16[32,1024]{1,0:T(8,128)(2,1)S(1)}, u32[]{:S(2)}, u32[]{:S(2)}) collective-permute-start(bf16[32,1024]{1,0:T(8,128)(2,1)S(1)} %get-tuple-element.23), channel_id=1, source_target_pairs={{0,2},{1,3},{2,0},{3,1},{4,6},{5,7},{6,4},{7,5},{8,10},{9,11},{10,... | collective-permute-start | bytes 196616 | tf_op jit(solution)/shard_map/ppermute | solution.py:45
  7.7 5.6 %collective-permute-start.2 = (bf16[32,1024]{1,0:T(8,128)(2,1)S(1)}, bf16[32,1024]{1,0:T(8,128)(2,1)S(1)}, u32[]{:S(2)}, u32[]{:S(2)}) collective-permute-start(bf16[32,1024]{1,0:T(8,128)(2,1)S(1)} %get-tuple-element.24), channel_id=1, source_target_pairs={{0,4},{1,5},{2,6},{3,7},{4,0},{5,1},{6,2},{7,3},{8,12},{9,13},{10,... | collective-permute-start | bytes 196616 | tf_op jit(solution)/shard_map/ppermute | solution.py:45
  9.2 5.2 %collective-permute-start.3 = (bf16[32,1024]{1,0:T(8,128)(2,1)S(1)}, bf16[32,1024]{1,0:T(8,128)(2,1)S(1)}, u32[]{:S(2)}, u32[]{:S(2)}) collective-permute-start(bf16[32,1024]{1,0:T(8,128)(2,1)S(1)} %get-tuple-element.25), channel_id=1, source_target_pairs={{0,6},{1,7},{2,4},{3,5},{4,2},{5,3},{6,0},{7,1},{8,14},{9,15},{10,... | collective-permute-start | bytes 196616 | tf_op jit(solution)/shard_map/ppermute | solution.py:45
  16.0 3.3 %collective-permute-start.4 = (bf16[4,32,640]{2,1,0:T(8,128)(2,1)S(1)}, bf16[4,32,640]{2,1,0:T(8,128)(2,1)S(1)}, u32[]{:S(2)}, u32[]{:S(2)}) collective-permute-start(bf16[4,32,640]{2,1,0:T(8,128)(2,1)S(1)} %get-tuple-element.27), channel_id=1, source_target_pairs={{0,1},{1,0},{2,3},{3,2},{4,5},{5,4},{6,7},{7,6},{8,9},{9,8},{10,11... | collective-permute-start | bytes 491528 | tf_op jit(solution)/shard_map/ppermute | solution.py:45
  16.1 7.3 %collective-permute-start.14 = (bf16[32,1024]{1,0:T(8,128)(2,1)S(1)}, bf16[32,1024]{1,0:T(8,128)(2,1)S(1)}, u32[]{:S(2)}, u32[]{:S(2)}) collective-permute-start(bf16[32,1024]{1,0:T(8,128)(2,1)S(1)} %get-tuple-element.26.merged_ref.refs_0_), channel_id=1, source_target_pairs={{0,8},{8,0},{16,24},{24,16},{1,9},{9,1},{17,25},{25,17},{2,10},{10... | collective-permute-start | bytes 196616 | tf_op jit(solution)/shard_map/ppermute | solution.py:45
  19.4 6.6 %collective-permute-start.5 = (bf16[32,640]{1,0:T(8,128)(2,1)S(1)}, bf16[32,640]{1,0:T(8,128)(2,1)S(1)}, u32[]{:S(2)}, u32[]{:S(2)}) collective-permute-start(bf16[32,640]{1,0:T(8,128)(2,1)S(1)} %get-tuple-element.29), channel_id=1, source_target_pairs={{0,2},{1,3},{2,0},{3,1},{4,6},{5,7},{6,4},{7,5},{8,10},{9,11},{10,... | collective-permute-start | bytes 122888 | tf_op jit(solution)/shard_map/ppermute | solution.py:45
  20.4 7.0 %collective-permute-start.6 = (bf16[32,640]{1,0:T(8,128)(2,1)S(1)}, bf16[32,640]{1,0:T(8,128)(2,1)S(1)}, u32[]{:S(2)}, u32[]{:S(2)}) collective-permute-start(bf16[32,640]{1,0:T(8,128)(2,1)S(1)} %get-tuple-element.30), channel_id=1, source_target_pairs={{0,4},{1,5},{2,6},{3,7},{4,0},{5,1},{6,2},{7,3},{8,12},{9,13},{10,... | collective-permute-start | bytes 122888 | tf_op jit(solution)/shard_map/ppermute | solution.py:45
  21.9 7.2 %collective-permute-start.7 = (bf16[32,640]{1,0:T(8,128)(2,1)S(1)}, bf16[32,640]{1,0:T(8,128)(2,1)S(1)}, u32[]{:S(2)}, u32[]{:S(2)}) collective-permute-start(bf16[32,640]{1,0:T(8,128)(2,1)S(1)} %get-tuple-element.31), channel_id=1, source_target_pairs={{0,6},{1,7},{2,4},{3,5},{4,2},{5,3},{6,0},{7,1},{8,14},{9,15},{10,... | collective-permute-start | bytes 122888 | tf_op jit(solution)/shard_map/ppermute | solution.py:45
  23.0 8.6 %collective-permute-start.8 = (bf16[64,1280]{1,0:T(8,128)(2,1)S(1)}, bf16[64,1280]{1,0:T(8,128)(2,1)S(1)}, u32[]{:S(2)}, u32[]{:S(2)}) collective-permute-start(bf16[64,1280]{1,0:T(8,128)(2,1)S(1)} %get-tuple-element.34), channel_id=1, source_target_pairs={{0,8},{8,0},{16,24},{24,16},{1,9},{9,1},{17,25},{25,17},{2,10},{10... | collective-permute-start | bytes 491528 | tf_op jit(solution)/shard_map/ppermute | solution.py:45
  23.4 19.0 %collective-permute-start.9 = (bf16[64,1280]{1,0:T(8,128)(2,1)S(1)}, bf16[64,1280]{1,0:T(8,128)(2,1)S(1)}, u32[]{:S(2)}, u32[]{:S(2)}) collective-permute-start(bf16[64,1280]{1,0:T(8,128)(2,1)S(1)} %get-tuple-element.35), channel_id=1, source_target_pairs={{0,16},{8,24},{16,0},{24,8},{1,17},{9,25},{17,1},{25,9},{2,18},{10... | collective-permute-start | bytes 491528 | tf_op jit(solution)/shard_map/ppermute | solution.py:45
  26.0 16.7 %collective-permute-start.10 = (bf16[64,1280]{1,0:T(8,128)(2,1)S(1)}, bf16[64,1280]{1,0:T(8,128)(2,1)S(1)}, u32[]{:S(2)}, u32[]{:S(2)}) collective-permute-start(bf16[64,1280]{1,0:T(8,128)(2,1)S(1)} %get-tuple-element.36), channel_id=1, source_target_pairs={{0,24},{8,16},{16,8},{24,0},{1,25},{9,17},{17,9},{25,1},{2,26},{10... | collective-permute-start | bytes 491528 | tf_op jit(solution)/shard_map/ppermute | solution.py:45
  27.4 21.0 %collective-permute-start.15 = (bf16[64,1024]{1,0:T(8,128)(2,1)S(1)}, bf16[64,1024]{1,0:T(8,128)(2,1)S(1)}, u32[]{:S(2)}, u32[]{:S(2)}) collective-permute-start(bf16[64,1024]{1,0:T(8,128)(2,1)S(1)} %shard_map.83.refs_4_), channel_id=1, source_target_pairs={{0,16},{8,24},{16,0},{24,8},{1,17},{9,25},{17,1},{25,9},{2,18},{10... | collective-permute-start | bytes 393224 | tf_op jit(solution)/shard_map/ppermute | solution.py:45
  29.2 24.0 %copy-start = (bf16[32,640]{1,0:T(8,128)(2,1)}, bf16[32,640]{1,0:T(8,128)(2,1)S(1)}, u32[]{:S(2)}) copy-start(bf16[32,640]{1,0:T(8,128)(2,1)S(1)} %multiply_convert_fusion.refs_4_) | copy-start | bytes 122884
  29.2 22.0 %collective-permute-start.13 = (bf16[32,640]{1,0:T(8,128)(2,1)S(1)}, bf16[32,640]{1,0:T(8,128)(2,1)S(1)}, u32[]{:S(2)}, u32[]{:S(2)}) collective-permute-start(bf16[32,640]{1,0:T(8,128)(2,1)S(1)} %multiply_convert_fusion.refs_4_), channel_id=1, source_target_pairs={{0,24},{8,16},{16,8},{24,0},{1,25},{9,17},{17,9},{25,1},{2,26},{10... | collective-permute-start | bytes 122888 | tf_op jit(solution)/shard_map/ppermute | solution.py:45
  31.6 19.6 %collective-permute-start.12 = (bf16[32,640]{1,0:T(8,128)(2,1)S(1)}, bf16[32,640]{1,0:T(8,128)(2,1)S(1)}, u32[]{:S(2)}, u32[]{:S(2)}) collective-permute-start(bf16[32,640]{1,0:T(8,128)(2,1)S(1)} %multiply_convert_fusion.refs_4_), channel_id=1, source_target_pairs={{0,16},{8,24},{16,0},{24,8},{1,17},{9,25},{17,1},{25,9},{2,18},{10... | collective-permute-start | bytes 122888 | tf_op jit(solution)/shard_map/ppermute | solution.py:45
  42.4 8.8 %collective-permute-start.11 = (bf16[32,640]{1,0:T(8,128)(2,1)S(1)}, bf16[32,640]{1,0:T(8,128)(2,1)S(1)}, u32[]{:S(2)}, u32[]{:S(2)}) collective-permute-start(bf16[32,640]{1,0:T(8,128)(2,1)S(1)} %multiply_convert_fusion.refs_4_), channel_id=1, source_target_pairs={{0,8},{8,0},{16,24},{24,16},{1,9},{9,1},{17,25},{25,17},{2,10},{10... | collective-permute-start | bytes 122888 | tf_op jit(solution)/shard_map/ppermute | solution.py:45

commit v4 on v3

--- a/solution.py
+++ b/solution.py
@@ -45,12 +45,18 @@
     return lax.ppermute(block, axis, pairs)
 
 
+def feature_cuts(groups):
+    lane = lax.axis_index("roll") % 2
+    return [(0, None)] + [(k + lane, None) for k in range(1, groups - 1, 2)] + [(groups - 1, lane)]
+
+
 def front(halves, groups, aligned, *refs):
     dest_ref, slots_ref, before_ref, inputs_ref = refs[:4]
     placed_refs, rest = refs[4:6], refs[6:]
-    feature_refs = rest[: groups * aligned]
-    slope_refs = rest[groups * aligned : (groups + 1) * aligned]
-    held_dest, held, held_before, held_own, sems = rest[(groups + 1) * aligned :]
+    count = groups // 2 + 1
+    feature_refs = rest[: count * aligned]
+    slope_refs = rest[count * aligned : (count + 1) * aligned]
+    held_dest, held, held_own, sems = rest[(count + 1) * aligned :]
     _, merged_count, columns = placed_refs[0].shape
     shard, group = lax.axis_index("roll"), lax.axis_index("enc")
     started = iter(range(sems.shape[0]))
@@ -64,36 +70,29 @@
         return pl.ds(pl.multiple_of(index * size, size), size)
 
     dest_copy = fetch(dest_ref, held_dest)
+    spots = [2 * j + parity for parity in (1, 0) for j in range(halves)]
     slot_copies = [
-        fetch(slots_ref.at[:, cut(shard ^ (2 * j + parity), columns)], held.at[parity, j])
-        for parity in (1, 0)
-        for j in range(halves)
+        fetch(slots_ref.at[:, cut(shard ^ k, columns)], held.at[:, pl.ds(i * columns, columns)]) for i, k in enumerate(spots)
     ]
     before_copies, input_copies = [], []
-    for k, ref in enumerate(feature_refs):
-        size = ref.shape[1]
-        before_copies.append(fetch(before_ref.at[:, cut(group ^ k, size)], held_before.at[k]))
-        input_copies.append(
-            fetch(inputs_ref.at[:, cut(group ^ k, size)], ref.at[pl.ds(merged_count, merged_count), :])
-        )
+    for ref, (distance, half) in zip(feature_refs, feature_cuts(groups)):
+        index = group ^ distance
+        source = cut(index if half is None else 2 * index + half, ref.shape[1])
+        before_copies.append(fetch(before_ref.at[:, source], ref.at[pl.ds(0, merged_count), :]))
+        input_copies.append(fetch(inputs_ref.at[:, source], ref.at[pl.ds(merged_count, merged_count), :]))
     own_copies = [fetch(before_ref.at[:, cut(shard, ref.shape[1])], held_own) for ref in slope_refs]
     dest_copy.wait()
-    rows = lax.broadcasted_iota(jnp.int32, (merged_count, held.shape[2]), 0)
+    rows = lax.broadcasted_iota(jnp.int32, (merged_count, held.shape[0]), 0)
     picker = jnp.where(rows == held_dest[...], 1.0, 0.0).astype(jnp.bfloat16)
-    slot_copies = iter(slot_copies)
-    for parity in (1, 0):
-        for j in range(halves):
-            next(slot_copies).wait()
-            placed_refs[parity][j] = jnp.dot(
-                picker, held[parity, j], preferred_element_type=jnp.float32
-            ).astype(jnp.bfloat16)
-    for k, copy in enumerate(before_copies):
-        copy.wait()
-        feature_refs[k][:merged_count, :] = gelu(held_before[k].astype(jnp.float32)).astype(jnp.bfloat16)
+    for copy in slot_copies:
+        copy.wait()
+    placed = jnp.dot(picker, held[...], preferred_element_type=jnp.float32).astype(jnp.bfloat16)
+    for i, k in enumerate(spots):
+        placed_refs[k % 2][k // 2] = placed[:, i * columns : (i + 1) * columns]
     for ref, copy in zip(slope_refs, own_copies):
         copy.wait()
         ref[...] = gelu_slope(held_own[...].astype(jnp.float32))
-    for copy in input_copies:
+    for copy in before_copies + input_copies:
         copy.wait()
 
 
@@ -157,25 +156,41 @@
         copy.wait()
 
 
-def block_products(part, factor, groups, *refs):
-    feature_refs, right_refs, (out_ref, held, sems) = refs[:groups], refs[groups:-3], refs[-3:]
-    rows = feature_refs[0].shape[0] // 2
-    half = slice(part * rows, (part + 1) * rows)
+def block_products(part, factor, places, *refs):
+    groups = len(places)
+    feature_refs, right_refs, (out_ref, held, sems) = refs[: groups + 1], refs[groups + 1 : -3], refs[-3:]
+    *whole_refs, mine_ref, came_ref = feature_refs
+    rows = mine_ref.shape[0] // 2
+    rows_cut = slice(part * rows, (part + 1) * rows)
+    half_cols = mine_ref.shape[1]
+    lane = lax.axis_index("roll") % 2
 
     def left_of(first, size):
-        return jnp.concatenate([ref[half, first : first + size] for ref in feature_refs], axis=0)
-
-    right = jnp.concatenate([ref[...] for ref in right_refs], axis=0)
-    write_products(left_of, right, factor, out_ref, held, sems)
-
-
-def products(part, factor, features, rights, columns):
-    groups, (rows, in_cols) = len(features), features[0].shape
-    size = next((s for s in (256, 128) if in_cols % s == 0), in_cols)
+        half, start = divmod(first, half_cols)
+        pieces = [ref[rows_cut, first : first + size] for ref in whole_refs]
+        mine, came = (ref[rows_cut, start : start + size] for ref in (mine_ref, came_ref))
+        left = jnp.concatenate(pieces + [jnp.where(lane == half, mine, came)], axis=0)
+        return left if part else gelu(left.astype(jnp.float32)).astype(jnp.bfloat16)
+
+    right = [right_refs[index][start : start + rows, :] for index, start in places]
+    for k in range(1, groups - 1, 2):
+        right[k], right[k + 1] = (
+            jnp.where(lane == 0, right[k], right[k + 1]),
+            jnp.where(lane == 0, right[k + 1], right[k]),
+        )
+    write_products(left_of, jnp.concatenate(right, axis=0), factor, out_ref, held, sems)
+
+
+def products(part, factor, features, rights, order):
+    rows = features[0].shape[0] // 2
+    in_cols, columns = features[0].shape[1], rights[0].shape[1]
+    spots = [(i, first) for i, right in enumerate(rights) for first in range(0, right.shape[0], rows)]
+    places = [spots[order.index(k)] for k in range(len(order))]
+    size = 128 if in_cols % 256 == 0 else in_cols // 2
     out = shape((in_cols, columns), jnp.float32)
     (result,) = call(
-        functools.partial(block_products, part, factor, groups), [out], (*features, *rights), groups * rows * in_cols * columns,
-        out_specs=[HBM],
+        functools.partial(block_products, part, factor, places), [out], (*features, *rights),
+        2 * len(order) * rows * in_cols * columns, out_specs=[HBM],
         scratch=[pltpu.VMEM((in_cols // size, size, columns), jnp.float32), pltpu.SemaphoreType.DMA((in_cols // size,))],
         limit=(6 << 20) + 4 * in_cols * columns,
     )
@@ -194,7 +209,7 @@
     unit_cols = width // shards
     in_cols = width // groups
     kind = jnp.bfloat16
-    aligned = in_cols % 128 == 0 and unit_cols % 128 == 0
+    aligned = in_cols % 256 == 0 and unit_cols % 128 == 0
 
     def spread(kept, came):
         blocks = call(pair_sum, [shape(kept.shape[1:], kind)] * halves, (kept, came), kept.size)
@@ -203,14 +218,14 @@
     place = (halves, merged_count, columns)
     outs = [shape(place, kind)] * 2
     if aligned:
-        outs += [shape((2 * merged_count, in_cols), kind)] * groups + [shape((merged_count, unit_cols), jnp.float32)]
+        outs += [shape((2 * merged_count, in_cols), kind)] * (groups // 2)
+        outs += [shape((2 * merged_count, in_cols // 2), kind), shape((merged_count, unit_cols), jnp.float32)]
     sources = [pltpu.with_memory_space_constraint(x, pltpu.HBM) for x in (row_dest, slots, before, inputs)]
     scratch = [
         pltpu.VMEM(row_dest.shape, row_dest.dtype),
-        pltpu.VMEM((2, halves, slot_count, columns), kind),
-        pltpu.VMEM((groups, merged_count, in_cols), kind),
+        pltpu.VMEM(slots.shape, kind),
         pltpu.VMEM((merged_count, unit_cols), kind),
-        pltpu.SemaphoreType.DMA((2 + 2 * halves + 2 * groups,)),
+        pltpu.SemaphoreType.DMA((4 + 2 * halves + groups,)),
     ]
     kept, sent, *rest = call(
         functools.partial(front, halves, groups, int(aligned)), outs, sources,
@@ -219,12 +234,24 @@
     if aligned:
         *blocks, slope = rest
     else:
-        both = jnp.concatenate([gelu(before.astype(jnp.float32)).astype(kind), inputs], axis=0)
+        both = jnp.concatenate([before, inputs], axis=0)
         group = lax.axis_index("enc")
-        blocks = [lax.dynamic_slice_in_dim(both, (group ^ k) * in_cols, in_cols, 1) for k in range(groups)]
+        blocks = []
+        for distance, half in feature_cuts(groups):
+            size = in_cols if half is None else in_cols // 2
+            first = (group ^ distance) * in_cols + (0 if half is None else half * size)
+            blocks.append(lax.dynamic_slice_in_dim(both, first, size, 1))
         own = lax.dynamic_slice_in_dim(before, lax.axis_index("roll") * unit_cols, unit_cols, 1)
         slope = gelu_slope(own.astype(jnp.float32))
-    features = [blocks[0]] + [exchange(blocks[k], "enc", k) for k in range(1, groups)]
+
+    features = [blocks[0]]
+    for block, k in zip(blocks[1:], range(1, groups, 2)):
+        last = k == groups - 1
+        pairs = [
+            (e * shards + r, (e ^ (k if last else k + r % 2)) * shards + r) for e in range(groups) for r in range(shards)
+        ]
+        came = lax.ppermute(block, ("enc", "roll"), pairs)
+        features += [came, exchange(came, "roll", 1)]
 
     pieces = spread(kept, exchange(sent, "roll", 1))
     (weights,) = call(
@@ -240,20 +267,22 @@
     came = exchange(sent, "roll", 1)
     (kept,) = call(second_units, [shape(unit_shape, kind)], (merged, weights), flops)
 
-    merged_all = [merged]
-    step = 1
-    while step < groups:
-        (whole,) = merged_all if step == 1 else call(join, [shape((step * merged_count, columns), kind)], merged_all)
+    merged_all, order, step = [merged], [0], groups // 2
+    while step:
+        (whole,) = (
+            merged_all if len(order) == 1 else call(join, [shape((len(order) * merged_count, columns), kind)], merged_all)
+        )
         merged_all = [whole, exchange(whole, "enc", step)]
-        step *= 2
+        order += [k ^ step for k in order]
+        step //= 2
 
     pieces = spread(kept, came)
     grads = (sum(piece.astype(jnp.float32) for piece in pieces) * slope).astype(kind)
     grads_all = [grads] + [exchange(grads, "enc", k) for k in range(1, groups)]
 
     factor = 1.0 / math.sqrt(merged_count * groups)
-    grad_second = products(0, factor, features, merged_all, columns)
-    grad_first = products(1, factor, features, grads_all, unit_cols)
+    grad_second = products(0, factor, features, merged_all, order)
+    grad_first = products(1, factor, features, grads_all, list(range(groups)))
     return (grads[None], grad_first, grad_second)
 
 

time: 53.4 us -> 41.9 us (0.78)
  waiting for transfers between devices: 19 us -> 8.49 us
  Pallas kernels: 14.6 us -> 13.7 us
    ppermute x16 -> x15, waiting for transfers between devices: 19 us -> 5.94 us  [exchange(): return lax.ppermute(block, axis, pairs)]
    ppermute x16 -> x15, starting transfers between devices: 18.8 us -> 14.6 us  [exchange(): return lax.ppermute(block, axis, pairs)]
    ppermute x0 -> x2, starting transfers between devices: none -> 4.12 us  [body(): came = lax.ppermute(block, ('enc', 'roll'), pairs)]
    ppermute x0 -> x2, waiting for transfers between devices: none -> 2.55 us  [body(): came = lax.ppermute(block, ('enc', 'roll'), pairs)]
    pallas_call x9, Pallas kernels: 14.6 us -> 13.7 us  [call(): pl.pallas_call(kernel, out_shape=outs, in_specs=in_specs or [VMEM] * len(...]
  transfers between devices with their start and end apart: 16 -> 17, of which waited for: 5 -> 7; matrix products, arithmetic and copies ran while one was open for 0% -> 0% of each run, Pallas kernels for 16% -> 20%
where the time goes in v4:
time: 41.9 us; the launch traced here: 41.7 us
  starting transfers between devices  18.7 us (45%)
  Pallas kernels  13.7 us (33%)
  waiting for transfers between devices  8.49 us (20%)
  between operations  0.76 us (2%)
    ppermute x15, starting transfers between devices, exchange(): return lax.ppermute(block, axis, pairs)  14.6 us
    pallas_call x9, Pallas kernels, call(): pl.pallas_call(kernel, out_shape=outs, in_specs=in_specs or [VMEM] * len(...  13.7 us
    ppermute x15, waiting for transfers between devices, exchange(): return lax.ppermute(block, axis, pairs)  5.94 us
    ppermute x2, starting transfers between devices, body(): came = lax.ppermute(block, ('enc', 'roll'), pairs)  4.12 us
    ppermute x2, waiting for transfers between devices, body(): came = lax.ppermute(block, ('enc', 'roll'), pairs)  2.55 us
  transfers between devices with their start and end apart: 17, of which 7 were waited for; matrix products, arithmetic and copies ran while one was open for 0% of the time, Pallas kernels for 20%

profile of v4, /device:TPU:0, one launch (start us, length us, event | category | flops | bytes accessed | tf_op | source)
XLA Modules:
  0.0 41.7 jit_solution(63081721502599503)
XLA Ops:
  0.6 1.5 %shard_map.76 = (bf16[4,32,1024]{2,1,0:T(8,128)(2,1)S(1)}, bf16[4,32,1024]{2,1,0:T(8,128)(2,1)S(1)}, bf16[64,1280]{1,0:T(8,128)(2,1)S(1)}, bf16[64,1280]{1,0:T(8...) custom-call(s32[1,32]{1,0:T(1,128)} %refs_0_.1, bf16[32,8192]{1,0:T(8,128)(2,1)} %bitcast.5, ...), custom_call_target="tpu_custom_call" | custom-call | flops 16777216 | bytes 2195584 | tf_op jit(solution)/shard_map/pallas_call | solution.py:32
  2.2 0.6 %collective-permute-start = (bf16[4,32,1024]{2,1,0:T(8,128)(2,1)S(1)}, bf16[4,32,1024]{2,1,0:T(8,128)(2,1)S(1)}, u32[]{:S(2)}, u32[]{:S(2)}) collective-permute-start(bf16[4,32,1024]{2,1,0:T(8,128)(2,1)S(1)} %get-tuple-element.20), channel_id=1, source_target_pairs={{0,1},{1,0},{2,3},{3,2},{4,5},{5,4},{6,7},{7,6},{8,9},{9,8},{10,11... | collective-permute-start | bytes 786440 | tf_op jit(solution)/shard_map/ppermute | solution.py:45
  2.7 1.2 %collective-permute-done.came_ref = bf16[4,32,1024]{2,1,0:T(8,128)(2,1)S(1)} collective-permute-done((bf16[4,32,1024]{2,1,0:T(8,128)(2,1)S(1)}, bf16[4,32,1024]{2,1,0:T(8,128)(2,1)S(1)}, u32[]{:S(2)}, u32[]{:S(2)}) %collective-permute-start) | collective-permute-done | bytes 262176 | tf_op jit(solution)/shard_map/ppermute | solution.py:45
  3.9 0.1 shard_map.77
  4.0 2.9 %collective-permute-start.1 = (bf16[32,1024]{1,0:T(8,128)(2,1)S(1)}, bf16[32,1024]{1,0:T(8,128)(2,1)S(1)}, u32[]{:S(2)}, u32[]{:S(2)}) collective-permute-start(bf16[32,1024]{1,0:T(8,128)(2,1)S(1)} %get-tuple-element.22), channel_id=1, source_target_pairs={{0,2},{1,3},{2,0},{3,1},{4,6},{5,7},{6,4},{7,5},{8,10},{9,11},{10,... | collective-permute-start | bytes 196616 | tf_op jit(solution)/shard_map/ppermute | solution.py:45
  6.9 1.5 %collective-permute-start.2 = (bf16[32,1024]{1,0:T(8,128)(2,1)S(1)}, bf16[32,1024]{1,0:T(8,128)(2,1)S(1)}, u32[]{:S(2)}, u32[]{:S(2)}) collective-permute-start(bf16[32,1024]{1,0:T(8,128)(2,1)S(1)} %get-tuple-element.23), channel_id=1, source_target_pairs={{0,4},{1,5},{2,6},{3,7},{4,0},{5,1},{6,2},{7,3},{8,12},{9,13},{10,... | collective-permute-start | bytes 196616 | tf_op jit(solution)/shard_map/ppermute | solution.py:45
  8.4 0.0 collective-permute-start.3
  8.4 4.1 %shard_map.78.refs_4_.w_ref = bf16[5120,1024]{1,0:T(8,128)(2,1)S(1)} custom-call(bf16[5120,1024]{1,0:T(8,128)(2,1)} %source_ref.1), custom_call_target="tpu_custom_call" | custom-call | bytes 20971520 | tf_op jit(solution)/shard_map/pallas_call | solution.py:32
  12.6 1.0 %collective-permute-done.3.refs_3_ = bf16[32,1024]{1,0:T(8,128)(2,1)S(1)} collective-permute-done((bf16[32,1024]{1,0:T(8,128)(2,1)S(1)}, bf16[32,1024]{1,0:T(8,128)(2,1)S(1)}, u32[]{:S(2)}, u32[]{:S(2)}) %collective-permute-start.3) | collective-permute-done | bytes 65568 | tf_op jit(solution)/shard_map/ppermute | solution.py:45
  13.6 1.6 %shard_map.79 = (bf16[32,1024]{1,0:T(8,128)(2,1)S(1)}, bf16[4,32,640]{2,1,0:T(8,128)(2,1)S(1)}) custom-call(bf16[32,1024]{1,0:T(8,128)(2,1)S(1)} %get-tuple-element.21.refs_0_, bf16[32,1024]{1,0:T(8,128)(2,1)S(1)} %collective-permute-done.1.refs_1_, bf16[32,1024]{1,0:T(8,128)(2,1)S(1)} %collective-permute-done.2.refs_2_, ...), custom_call_target="tpu_custom_call" | custom-call | flops 167772160 | bytes 10977280 | tf_op jit(solution)/shard_map/pallas_call | solution.py:32
  15.2 0.0 collective-permute-start.4
  15.3 1.7 %collective-permute-start.8 = (bf16[64,1280]{1,0:T(8,128)(2,1)S(1)}, bf16[64,1280]{1,0:T(8,128)(2,1)S(1)}, u32[]{:S(2)}, u32[]{:S(2)}) collective-permute-start(bf16[64,1280]{1,0:T(8,128)(2,1)S(1)} %get-tuple-element.33), channel_id=1, source_target_pairs={{0,8},{1,17},{2,10},{3,19},{4,12},{5,21},{6,14},{7,23},{8,0},{9,25... | collective-permute-start | bytes 491528 | tf_op jit(solution)/shard_map/ppermute | solution.py:253
  16.9 2.5 %collective-permute-start.10 = (bf16[64,640]{1,0:T(8,128)(2,1)S(1)}, bf16[64,640]{1,0:T(8,128)(2,1)S(1)}, u32[]{:S(2)}, u32[]{:S(2)}) collective-permute-start(bf16[64,640]{1,0:T(8,128)(2,1)S(1)} %get-tuple-element.34), channel_id=1, source_target_pairs={{0,24},{1,25},{2,26},{3,27},{4,28},{5,29},{6,30},{7,31},{8,16},{9,... | collective-permute-start | bytes 245768 | tf_op jit(solution)/shard_map/ppermute | solution.py:253
  19.4 0.1 collective-permute-start.15
  19.5 1.6 %shard_map.80.kept_ref = bf16[4,32,640]{2,1,0:T(8,128)(2,1)S(1)} custom-call(bf16[32,1024]{1,0:T(8,128)(2,1)S(1)} %get-tuple-element.25.merged_ref.refs_0_, bf16[5120,1024]{1,0:T(8,128)(2,1)S(1)} %shard_map.78.refs_4_.w_ref), custom_call_target="tpu_custom_call" | custom-call | flops 167772160 | bytes 10715136 | tf_op jit(solution)/shard_map/pallas_call | solution.py:32
  21.1 0.0 collective-permute-done.4.came_ref
  21.2 2.0 %collective-permute-start.7 = (bf16[32,640]{1,0:T(8,128)(2,1)S(1)}, bf16[32,640]{1,0:T(8,128)(2,1)S(1)}, u32[]{:S(2)}, u32[]{:S(2)}) collective-permute-start(bf16[32,640]{1,0:T(8,128)(2,1)S(1)} %get-tuple-element.30), channel_id=1, source_target_pairs={{0,6},{1,7},{2,4},{3,5},{4,2},{5,3},{6,0},{7,1},{8,14},{9,15},{10,... | collective-permute-start | bytes 122888 | tf_op jit(solution)/shard_map/ppermute | solution.py:45
  23.1 0.5 %collective-permute-start.6 = (bf16[32,640]{1,0:T(8,128)(2,1)S(1)}, bf16[32,640]{1,0:T(8,128)(2,1)S(1)}, u32[]{:S(2)}, u32[]{:S(2)}) collective-permute-start(bf16[32,640]{1,0:T(8,128)(2,1)S(1)} %get-tuple-element.29), channel_id=1, source_target_pairs={{0,4},{1,5},{2,6},{3,7},{4,0},{5,1},{6,2},{7,3},{8,12},{9,13},{10,... | collective-permute-start | bytes 122888 | tf_op jit(solution)/shard_map/ppermute | solution.py:45
  23.6 2.5 %collective-permute-done.10.refs_3_ = bf16[64,640]{1,0:T(8,128)(2,1)S(1)} collective-permute-done((bf16[64,640]{1,0:T(8,128)(2,1)S(1)}, bf16[64,640]{1,0:T(8,128)(2,1)S(1)}, u32[]{:S(2)}, u32[]{:S(2)}) %collective-permute-start.10) | collective-permute-done | bytes 81952 | tf_op jit(solution)/shard_map/ppermute | solution.py:253
  26.2 0.9 %collective-permute-start.5 = (bf16[32,640]{1,0:T(8,128)(2,1)S(1)}, bf16[32,640]{1,0:T(8,128)(2,1)S(1)}, u32[]{:S(2)}, u32[]{:S(2)}) collective-permute-start(bf16[32,640]{1,0:T(8,128)(2,1)S(1)} %get-tuple-element.28), channel_id=1, source_target_pairs={{0,2},{1,3},{2,0},{3,1},{4,6},{5,7},{6,4},{7,5},{8,10},{9,11},{10,... | collective-permute-start | bytes 122888 | tf_op jit(solution)/shard_map/ppermute | solution.py:45
  27.1 1.3 %collective-permute-done.15.refs_1_ = bf16[32,1024]{1,0:T(8,128)(2,1)S(1)} collective-permute-done((bf16[32,1024]{1,0:T(8,128)(2,1)S(1)}, bf16[32,1024]{1,0:T(8,128)(2,1)S(1)}, u32[]{:S(2)}, u32[]{:S(2)}) %collective-permute-start.15) | collective-permute-done | bytes 65568 | tf_op jit(solution)/shard_map/ppermute | solution.py:45
  28.4 0.5 %collective-permute-start.9 = (bf16[64,1280]{1,0:T(8,128)(2,1)S(1)}, bf16[64,1280]{1,0:T(8,128)(2,1)S(1)}, u32[]{:S(2)}, u32[]{:S(2)}) collective-permute-start(bf16[64,1280]{1,0:T(8,128)(2,1)S(1)} %collective-permute-done.8.refs_1_), channel_id=1, source_target_pairs={{0,1},{1,0},{2,3},{3,2},{4,5},{5,4},{6,7},{7,6},{8,9},{9,8},{10,11... | collective-permute-start | bytes 491528 | tf_op jit(solution)/shard_map/ppermute | solution.py:45
  29.0 1.1 %collective-permute-start.16 = (bf16[64,1024]{1,0:T(8,128)(2,1)S(1)}, bf16[64,1024]{1,0:T(8,128)(2,1)S(1)}, u32[]{:S(2)}, u32[]{:S(2)}) collective-permute-start(bf16[64,1024]{1,0:T(8,128)(2,1)S(1)} %shard_map.83.refs_5_), channel_id=1, source_target_pairs={{0,8},{8,0},{16,24},{24,16},{1,9},{9,1},{17,25},{25,17},{2,10},{10... | collective-permute-start | bytes 393224 | tf_op jit(solution)/shard_map/ppermute | solution.py:45
  30.0 0.2 collective-permute-done.5
  30.2 0.0 copy-start
  30.2 1.5 %collective-permute-start.12 = (bf16[32,640]{1,0:T(8,128)(2,1)S(1)}, bf16[32,640]{1,0:T(8,128)(2,1)S(1)}, u32[]{:S(2)}, u32[]{:S(2)}) collective-permute-start(bf16[32,640]{1,0:T(8,128)(2,1)S(1)} %multiply_convert_fusion.refs_5_), channel_id=1, source_target_pairs={{0,8},{8,0},{16,24},{24,16},{1,9},{9,1},{17,25},{25,17},{2,10},{10... | collective-permute-start | bytes 122888 | tf_op jit(solution)/shard_map/ppermute | solution.py:45
  31.7 2.1 %collective-permute-start.13 = (bf16[32,640]{1,0:T(8,128)(2,1)S(1)}, bf16[32,640]{1,0:T(8,128)(2,1)S(1)}, u32[]{:S(2)}, u32[]{:S(2)}) collective-permute-start(bf16[32,640]{1,0:T(8,128)(2,1)S(1)} %multiply_convert_fusion.refs_5_), channel_id=1, source_target_pairs={{0,16},{8,24},{16,0},{24,8},{1,17},{9,25},{17,1},{25,9},{2,18},{10... | collective-permute-start | bytes 122888 | tf_op jit(solution)/shard_map/ppermute | solution.py:45
  33.8 0.9 %collective-permute-start.14 = (bf16[32,640]{1,0:T(8,128)(2,1)S(1)}, bf16[32,640]{1,0:T(8,128)(2,1)S(1)}, u32[]{:S(2)}, u32[]{:S(2)}) collective-permute-start(bf16[32,640]{1,0:T(8,128)(2,1)S(1)} %multiply_convert_fusion.refs_5_), channel_id=1, source_target_pairs={{0,24},{8,16},{16,8},{24,0},{1,25},{9,17},{17,9},{25,1},{2,26},{10... | collective-permute-start | bytes 122888 | tf_op jit(solution)/shard_map/ppermute | solution.py:45
  34.7 0.2 collective-permute-done.16.refs_6_
  34.9 2.7 %shard_map.84 = f32[1280,1024]{1,0:T(8,128)} custom-call(bf16[64,1280]{1,0:T(8,128)(2,1)S(1)} %get-tuple-element.32.refs_0_, bf16[64,1280]{1,0:T(8,128)(2,1)S(1)} %collective-permute-done.8.refs_1_, bf16[64,1280]{1,0:T(8,128)(2,1)S(1)} %collective-permute-done.9.refs_2_, bf16[64,640]{1,0:T(8,128)(2,1)S(1)} %collective-permute-done.10.refs_3_, ...), custom_call_target="tpu_custom_call" | custom-call | flops 335544320 | bytes 6160384 | tf_op jit(solution)/shard_map/pallas_call | solution.py:32
  37.6 2.1 %collective-permute-done.14.refs_8_ = bf16[32,640]{1,0:T(8,128)(2,1)S(1)} collective-permute-done((bf16[32,640]{1,0:T(8,128)(2,1)S(1)}, bf16[32,640]{1,0:T(8,128)(2,1)S(1)}, u32[]{:S(2)}, u32[]{:S(2)}) %collective-permute-start.14) | collective-permute-done | bytes 40992 | tf_op jit(solution)/shard_map/ppermute | solution.py:45
  39.7 2.0 %shard_map.82 = f32[1280,640]{1,0:T(8,128)} custom-call(bf16[64,1280]{1,0:T(8,128)(2,1)S(1)} %get-tuple-element.32.refs_0_, bf16[64,1280]{1,0:T(8,128)(2,1)S(1)} %collective-permute-done.8.refs_1_, bf16[64,1280]{1,0:T(8,128)(2,1)S(1)} %collective-permute-done.9.refs_2_, bf16[64,640]{1,0:T(8,128)(2,1)S(1)} %collective-permute-done.10.refs_3_, ...), custom_call_target="tpu_custom_call" | custom-call | flops 209715200 | bytes 4096000 | tf_op jit(solution)/shard_map/pallas_call | solution.py:32
  (14 shorter events, 0.1 us)
Async XLA Ops:
  2.2 1.7 %collective-permute-start = (bf16[4,32,1024]{2,1,0:T(8,128)(2,1)S(1)}, bf16[4,32,1024]{2,1,0:T(8,128)(2,1)S(1)}, u32[]{:S(2)}, u32[]{:S(2)}) collective-permute-start(bf16[4,32,1024]{2,1,0:T(8,128)(2,1)S(1)} %get-tuple-element.20), channel_id=1, source_target_pairs={{0,1},{1,0},{2,3},{3,2},{4,5},{5,4},{6,7},{7,6},{8,9},{9,8},{10,11... | collective-permute-start | bytes 786440 | tf_op jit(solution)/shard_map/ppermute | solution.py:45
  4.0 8.6 %collective-permute-start.1 = (bf16[32,1024]{1,0:T(8,128)(2,1)S(1)}, bf16[32,1024]{1,0:T(8,128)(2,1)S(1)}, u32[]{:S(2)}, u32[]{:S(2)}) collective-permute-start(bf16[32,1024]{1,0:T(8,128)(2,1)S(1)} %get-tuple-element.22), channel_id=1, source_target_pairs={{0,2},{1,3},{2,0},{3,1},{4,6},{5,7},{6,4},{7,5},{8,10},{9,11},{10,... | collective-permute-start | bytes 196616 | tf_op jit(solution)/shard_map/ppermute | solution.py:45
  6.9 5.6 %collective-permute-start.2 = (bf16[32,1024]{1,0:T(8,128)(2,1)S(1)}, bf16[32,1024]{1,0:T(8,128)(2,1)S(1)}, u32[]{:S(2)}, u32[]{:S(2)}) collective-permute-start(bf16[32,1024]{1,0:T(8,128)(2,1)S(1)} %get-tuple-element.23), channel_id=1, source_target_pairs={{0,4},{1,5},{2,6},{3,7},{4,0},{5,1},{6,2},{7,3},{8,12},{9,13},{10,... | collective-permute-start | bytes 196616 | tf_op jit(solution)/shard_map/ppermute | solution.py:45
  8.4 5.2 %collective-permute-start.3 = (bf16[32,1024]{1,0:T(8,128)(2,1)S(1)}, bf16[32,1024]{1,0:T(8,128)(2,1)S(1)}, u32[]{:S(2)}, u32[]{:S(2)}) collective-permute-start(bf16[32,1024]{1,0:T(8,128)(2,1)S(1)} %get-tuple-element.24), channel_id=1, source_target_pairs={{0,6},{1,7},{2,4},{3,5},{4,2},{5,3},{6,0},{7,1},{8,14},{9,15},{10,... | collective-permute-start | bytes 196616 | tf_op jit(solution)/shard_map/ppermute | solution.py:45
  15.2 5.9 %collective-permute-start.4 = (bf16[4,32,640]{2,1,0:T(8,128)(2,1)S(1)}, bf16[4,32,640]{2,1,0:T(8,128)(2,1)S(1)}, u32[]{:S(2)}, u32[]{:S(2)}) collective-permute-start(bf16[4,32,640]{2,1,0:T(8,128)(2,1)S(1)} %get-tuple-element.26), channel_id=1, source_target_pairs={{0,1},{1,0},{2,3},{3,2},{4,5},{5,4},{6,7},{7,6},{8,9},{9,8},{10,11... | collective-permute-start | bytes 491528 | tf_op jit(solution)/shard_map/ppermute | solution.py:45
  15.3 11.9 %collective-permute-start.8 = (bf16[64,1280]{1,0:T(8,128)(2,1)S(1)}, bf16[64,1280]{1,0:T(8,128)(2,1)S(1)}, u32[]{:S(2)}, u32[]{:S(2)}) collective-permute-start(bf16[64,1280]{1,0:T(8,128)(2,1)S(1)} %get-tuple-element.33), channel_id=1, source_target_pairs={{0,8},{1,17},{2,10},{3,19},{4,12},{5,21},{6,14},{7,23},{8,0},{9,25... | collective-permute-start | bytes 491528 | tf_op jit(solution)/shard_map/ppermute | solution.py:253
  16.9 9.3 %collective-permute-start.10 = (bf16[64,640]{1,0:T(8,128)(2,1)S(1)}, bf16[64,640]{1,0:T(8,128)(2,1)S(1)}, u32[]{:S(2)}, u32[]{:S(2)}) collective-permute-start(bf16[64,640]{1,0:T(8,128)(2,1)S(1)} %get-tuple-element.34), channel_id=1, source_target_pairs={{0,24},{1,25},{2,26},{3,27},{4,28},{5,29},{6,30},{7,31},{8,16},{9,... | collective-permute-start | bytes 245768 | tf_op jit(solution)/shard_map/ppermute | solution.py:253
  19.4 9.1 %collective-permute-start.15 = (bf16[32,1024]{1,0:T(8,128)(2,1)S(1)}, bf16[32,1024]{1,0:T(8,128)(2,1)S(1)}, u32[]{:S(2)}, u32[]{:S(2)}) collective-permute-start(bf16[32,1024]{1,0:T(8,128)(2,1)S(1)} %get-tuple-element.25.merged_ref.refs_0_), channel_id=1, source_target_pairs={{0,16},{8,24},{16,0},{24,8},{1,17},{9,25},{17,1},{25,9},{2,18},{10... | collective-permute-start | bytes 196616 | tf_op jit(solution)/shard_map/ppermute | solution.py:45
  21.2 7.8 %collective-permute-start.7 = (bf16[32,640]{1,0:T(8,128)(2,1)S(1)}, bf16[32,640]{1,0:T(8,128)(2,1)S(1)}, u32[]{:S(2)}, u32[]{:S(2)}) collective-permute-start(bf16[32,640]{1,0:T(8,128)(2,1)S(1)} %get-tuple-element.30), channel_id=1, source_target_pairs={{0,6},{1,7},{2,4},{3,5},{4,2},{5,3},{6,0},{7,1},{8,14},{9,15},{10,... | collective-permute-start | bytes 122888 | tf_op jit(solution)/shard_map/ppermute | solution.py:45
  23.1 6.9 %collective-permute-start.6 = (bf16[32,640]{1,0:T(8,128)(2,1)S(1)}, bf16[32,640]{1,0:T(8,128)(2,1)S(1)}, u32[]{:S(2)}, u32[]{:S(2)}) collective-permute-start(bf16[32,640]{1,0:T(8,128)(2,1)S(1)} %get-tuple-element.29), channel_id=1, source_target_pairs={{0,4},{1,5},{2,6},{3,7},{4,0},{5,1},{6,2},{7,3},{8,12},{9,13},{10,... | collective-permute-start | bytes 122888 | tf_op jit(solution)/shard_map/ppermute | solution.py:45
  26.2 4.0 %collective-permute-start.5 = (bf16[32,640]{1,0:T(8,128)(2,1)S(1)}, bf16[32,640]{1,0:T(8,128)(2,1)S(1)}, u32[]{:S(2)}, u32[]{:S(2)}) collective-permute-start(bf16[32,640]{1,0:T(8,128)(2,1)S(1)} %get-tuple-element.28), channel_id=1, source_target_pairs={{0,2},{1,3},{2,0},{3,1},{4,6},{5,7},{6,4},{7,5},{8,10},{9,11},{10,... | collective-permute-start | bytes 122888 | tf_op jit(solution)/shard_map/ppermute | solution.py:45
  27.1 6.7 %collective-permute-start.11 = (bf16[64,640]{1,0:T(8,128)(2,1)S(1)}, bf16[64,640]{1,0:T(8,128)(2,1)S(1)}, u32[]{:S(2)}, u32[]{:S(2)}) collective-permute-start(bf16[64,640]{1,0:T(8,128)(2,1)S(1)} %collective-permute-done.10.refs_3_), channel_id=1, source_target_pairs={{0,1},{1,0},{2,3},{3,2},{4,5},{5,4},{6,7},{7,6},{8,9},{9,8},{10,11... | collective-permute-start | bytes 245768 | tf_op jit(solution)/shard_map/ppermute | solution.py:45
  28.4 6.3 %collective-permute-start.9 = (bf16[64,1280]{1,0:T(8,128)(2,1)S(1)}, bf16[64,1280]{1,0:T(8,128)(2,1)S(1)}, u32[]{:S(2)}, u32[]{:S(2)}) collective-permute-start(bf16[64,1280]{1,0:T(8,128)(2,1)S(1)} %collective-permute-done.8.refs_1_), channel_id=1, source_target_pairs={{0,1},{1,0},{2,3},{3,2},{4,5},{5,4},{6,7},{7,6},{8,9},{9,8},{10,11... | collective-permute-start | bytes 491528 | tf_op jit(solution)/shard_map/ppermute | solution.py:45
  29.0 5.9 %collective-permute-start.16 = (bf16[64,1024]{1,0:T(8,128)(2,1)S(1)}, bf16[64,1024]{1,0:T(8,128)(2,1)S(1)}, u32[]{:S(2)}, u32[]{:S(2)}) collective-permute-start(bf16[64,1024]{1,0:T(8,128)(2,1)S(1)} %shard_map.83.refs_5_), channel_id=1, source_target_pairs={{0,8},{8,0},{16,24},{24,16},{1,9},{9,1},{17,25},{25,17},{2,10},{10... | collective-permute-start | bytes 393224 | tf_op jit(solution)/shard_map/ppermute | solution.py:45
  30.2 11.5 %copy-start = (bf16[32,640]{1,0:T(8,128)(2,1)}, bf16[32,640]{1,0:T(8,128)(2,1)S(1)}, u32[]{:S(2)}) copy-start(bf16[32,640]{1,0:T(8,128)(2,1)S(1)} %multiply_convert_fusion.refs_5_) | copy-start | bytes 122884
  30.2 7.4 %collective-permute-start.12 = (bf16[32,640]{1,0:T(8,128)(2,1)S(1)}, bf16[32,640]{1,0:T(8,128)(2,1)S(1)}, u32[]{:S(2)}, u32[]{:S(2)}) collective-permute-start(bf16[32,640]{1,0:T(8,128)(2,1)S(1)} %multiply_convert_fusion.refs_5_), channel_id=1, source_target_pairs={{0,8},{8,0},{16,24},{24,16},{1,9},{9,1},{17,25},{25,17},{2,10},{10... | collective-permute-start | bytes 122888 | tf_op jit(solution)/shard_map/ppermute | solution.py:45
  31.7 5.9 %collective-permute-start.13 = (bf16[32,640]{1,0:T(8,128)(2,1)S(1)}, bf16[32,640]{1,0:T(8,128)(2,1)S(1)}, u32[]{:S(2)}, u32[]{:S(2)}) collective-permute-start(bf16[32,640]{1,0:T(8,128)(2,1)S(1)} %multiply_convert_fusion.refs_5_), channel_id=1, source_target_pairs={{0,16},{8,24},{16,0},{24,8},{1,17},{9,25},{17,1},{25,9},{2,18},{10... | collective-permute-start | bytes 122888 | tf_op jit(solution)/shard_map/ppermute | solution.py:45
  33.8 5.9 %collective-permute-start.14 = (bf16[32,640]{1,0:T(8,128)(2,1)S(1)}, bf16[32,640]{1,0:T(8,128)(2,1)S(1)}, u32[]{:S(2)}, u32[]{:S(2)}) collective-permute-start(bf16[32,640]{1,0:T(8,128)(2,1)S(1)} %multiply_convert_fusion.refs_5_), channel_id=1, source_target_pairs={{0,24},{8,16},{16,8},{24,0},{1,25},{9,17},{17,9},{25,1},{2,26},{10... | collective-permute-start | bytes 122888 | tf_op jit(solution)/shard_map/ppermute | solution.py:45

commit v5 on v4

--- a/solution.py
+++ b/solution.py
@@ -55,8 +55,7 @@
     placed_refs, rest = refs[4:6], refs[6:]
     count = groups // 2 + 1
     feature_refs = rest[: count * aligned]
-    slope_refs = rest[count * aligned : (count + 1) * aligned]
-    held_dest, held, held_own, sems = rest[(count + 1) * aligned :]
+    held_dest, held, sems = rest[count * aligned :]
     _, merged_count, columns = placed_refs[0].shape
     shard, group = lax.axis_index("roll"), lax.axis_index("enc")
     started = iter(range(sems.shape[0]))
@@ -80,7 +79,6 @@
         source = cut(index if half is None else 2 * index + half, ref.shape[1])
         before_copies.append(fetch(before_ref.at[:, source], ref.at[pl.ds(0, merged_count), :]))
         input_copies.append(fetch(inputs_ref.at[:, source], ref.at[pl.ds(merged_count, merged_count), :]))
-    own_copies = [fetch(before_ref.at[:, cut(shard, ref.shape[1])], held_own) for ref in slope_refs]
     dest_copy.wait()
     rows = lax.broadcasted_iota(jnp.int32, (merged_count, held.shape[0]), 0)
     picker = jnp.where(rows == held_dest[...], 1.0, 0.0).astype(jnp.bfloat16)
@@ -89,21 +87,7 @@
     placed = jnp.dot(picker, held[...], preferred_element_type=jnp.float32).astype(jnp.bfloat16)
     for i, k in enumerate(spots):
         placed_refs[k % 2][k // 2] = placed[:, i * columns : (i + 1) * columns]
-    for ref, copy in zip(slope_refs, own_copies):
-        copy.wait()
-        ref[...] = gelu_slope(held_own[...].astype(jnp.float32))
     for copy in before_copies + input_copies:
-        copy.wait()
-
-
-def load(source_ref, out_ref, sems):
-    size = source_ref.shape[0] // sems.shape[0]
-    copies = []
-    for j in range(sems.shape[0]):
-        cut = pl.ds(j * size, size)
-        copies.append(pltpu.make_async_copy(source_ref.at[cut, :], out_ref.at[cut, :], sems.at[j]))
-        copies[-1].start()
-    for copy in copies:
         copy.wait()
 
 
@@ -113,6 +97,15 @@
     for ref in piece_refs:
         out_ref[first : first + ref.shape[0], :] = ref[...]
         first += ref.shape[0]
+
+
+def own_slope(before_ref, out_ref, held, sem):
+    size = out_ref.shape[1]
+    first = pl.multiple_of(lax.axis_index("roll") * size, size)
+    copy = pltpu.make_async_copy(before_ref.at[:, pl.ds(first, size)], held, sem)
+    copy.start()
+    copy.wait()
+    out_ref[...] = gelu_slope(held[...].astype(jnp.float32))
 
 
 def pair_sum(kept_ref, came_ref, *out_refs):
@@ -212,27 +205,30 @@
     aligned = in_cols % 256 == 0 and unit_cols % 128 == 0
 
     def spread(kept, came):
-        blocks = call(pair_sum, [shape(kept.shape[1:], kind)] * halves, (kept, came), kept.size)
+        blocks = call(pair_sum, [shape(kept.shape[1:], kind)] * halves, (kept, came), 20_000_000_000)
         return [blocks[0]] + [exchange(blocks[j], "roll", 2 * j) for j in range(1, halves)]
 
     place = (halves, merged_count, columns)
     outs = [shape(place, kind)] * 2
     if aligned:
         outs += [shape((2 * merged_count, in_cols), kind)] * (groups // 2)
-        outs += [shape((2 * merged_count, in_cols // 2), kind), shape((merged_count, unit_cols), jnp.float32)]
+        outs += [shape((2 * merged_count, in_cols // 2), kind)]
     sources = [pltpu.with_memory_space_constraint(x, pltpu.HBM) for x in (row_dest, slots, before, inputs)]
     scratch = [
         pltpu.VMEM(row_dest.shape, row_dest.dtype),
         pltpu.VMEM(slots.shape, kind),
-        pltpu.VMEM((merged_count, unit_cols), kind),
-        pltpu.SemaphoreType.DMA((4 + 2 * halves + groups,)),
+        pltpu.SemaphoreType.DMA((3 + 2 * halves + groups,)),
     ]
     kept, sent, *rest = call(
         functools.partial(front, halves, groups, int(aligned)), outs, sources,
         2 * slot_count * slots.size, in_specs=[HBM] * 4, scratch=scratch, limit=12 << 20,
     )
     if aligned:
-        *blocks, slope = rest
+        blocks = rest
+        (slope,) = call(
+            own_slope, [shape((merged_count, unit_cols), jnp.float32)], (sources[2],), in_specs=[HBM],
+            scratch=[pltpu.VMEM((merged_count, unit_cols), kind), pltpu.SemaphoreType.DMA],
+        )
     else:
         both = jnp.concatenate([before, inputs], axis=0)
         group = lax.axis_index("enc")
@@ -254,10 +250,7 @@
         features += [came, exchange(came, "roll", 1)]
 
     pieces = spread(kept, exchange(sent, "roll", 1))
-    (weights,) = call(
-        load, [shape(w_second.shape, kind)], (pltpu.with_memory_space_constraint(w_second, pltpu.HBM),),
-        in_specs=[HBM], scratch=[pltpu.SemaphoreType.DMA((8,))],
-    )
+    weights = w_second
 
     unit_shape = (halves, merged_count, unit_cols)
     flops = 2 * columns * math.prod(unit_shape)

time: 41.9 us -> 42.4 us (1.012)
  waiting for transfers between devices: 8.49 us -> 13.5 us
  Pallas kernels: 13.7 us -> 10.4 us
  starting transfers between devices: 18.7 us -> 17.4 us
    ppermute x15, waiting for transfers between devices: 5.94 us -> 9.57 us  [exchange(): return lax.ppermute(block, axis, pairs)]
    pallas_call x9, Pallas kernels: 13.7 us -> 10.4 us  [call(): pl.pallas_call(kernel, out_shape=outs, in_specs=in_specs or [VMEM] * len(...]
    ppermute x2, waiting for transfers between devices: 2.55 us -> 3.88 us  [body(): came = lax.ppermute(block, ('enc', 'roll'), pairs)]
    ppermute x15, starting transfers between devices: 14.6 us -> 13.4 us  [exchange(): return lax.ppermute(block, axis, pairs)]
  transfers between devices with their start and end apart: 17 -> 17, of which waited for: 7 -> 8; matrix products, arithmetic and copies ran while one was open for 0% -> 0% of each run, Pallas kernels for 20% -> 12%
where the time goes in v5:
time: 42.4 us; the launch traced here: 42.1 us
  starting transfers between devices  17.4 us (41%)
  waiting for transfers between devices  13.5 us (32%)
  Pallas kernels  10.4 us (25%)
  between operations  0.77 us (2%)
    ppermute x15, starting transfers between devices, exchange(): return lax.ppermute(block, axis, pairs)  13.4 us
    pallas_call x9, Pallas kernels, call(): pl.pallas_call(kernel, out_shape=outs, in_specs=in_specs or [VMEM] * len(...  10.4 us
    ppermute x15, waiting for transfers between devices, exchange(): return lax.ppermute(block, axis, pairs)  9.57 us
    ppermute x2, starting transfers between devices, body(): came = lax.ppermute(block, ('enc', 'roll'), pairs)  4.09 us
    ppermute x2, waiting for transfers between devices, body(): came = lax.ppermute(block, ('enc', 'roll'), pairs)  3.88 us
  transfers between devices with their start and end apart: 17, of which 8 were waited for; matrix products, arithmetic and copies ran while one was open for 0% of the time, Pallas kernels for 12%

profile of v5, /device:TPU:0, one launch (start us, length us, event | category | flops | bytes accessed | tf_op | source)
XLA Modules:
  0.0 42.1 jit_solution(17453911835641004391)
XLA Ops:
  0.6 1.5 %shard_map.76 = (bf16[4,32,1024]{2,1,0:T(8,128)(2,1)S(1)}, bf16[4,32,1024]{2,1,0:T(8,128)(2,1)S(1)}, bf16[64,1280]{1,0:T(8,128)(2,1)S(1)}, bf16[64,1280]{1,0:T(8,128)(2,1)S(1)}, bf16[64,640]{1,0:T(8,128)(2,1)S(1)}) custom-call(s32[1,32]{1,0:T(1,128)} %refs_0_.1, bf16[32,8192]{1,0:T(8,128)(2,1)} %bitcast.9, bf16[32,5120]{1,0:T(8,128)(2,1)} %bitcast.7, ...), custom_call_target="tpu_custom_call" | custom-call | flops 16777216 | bytes 2113664 | tf_op jit(solution)/shard_map/pallas_call | solution.py:32
  2.1 0.6 %collective-permute-start = (bf16[4,32,1024]{2,1,0:T(8,128)(2,1)S(1)}, bf16[4,32,1024]{2,1,0:T(8,128)(2,1)S(1)}, u32[]{:S(2)}, u32[]{:S(2)}) collective-permute-start(bf16[4,32,1024]{2,1,0:T(8,128)(2,1)S(1)} %get-tuple-element.19), channel_id=1, source_target_pairs={{0,1},{1,0},{2,3},{3,2},{4,5},{5,4},{6,7},{7,6},{8,9},{9,8},{10,11... | collective-permute-start | bytes 786440 | tf_op jit(solution)/shard_map/ppermute | solution.py:45
  2.7 1.2 %collective-permute-done.came_ref = bf16[4,32,1024]{2,1,0:T(8,128)(2,1)S(1)} collective-permute-done((bf16[4,32,1024]{2,1,0:T(8,128)(2,1)S(1)}, bf16[4,32,1024]{2,1,0:T(8,128)(2,1)S(1)}, u32[]{:S(2)}, u32[]{:S(2)}) %collective-permute-start) | collective-permute-done | bytes 262176 | tf_op jit(solution)/shard_map/ppermute | solution.py:45
  3.9 0.1 shard_map.77
  3.9 2.9 %collective-permute-start.1 = (bf16[32,1024]{1,0:T(8,128)(2,1)S(1)}, bf16[32,1024]{1,0:T(8,128)(2,1)S(1)}, u32[]{:S(2)}, u32[]{:S(2)}) collective-permute-start(bf16[32,1024]{1,0:T(8,128)(2,1)S(1)} %get-tuple-element.21), channel_id=1, source_target_pairs={{0,2},{1,3},{2,0},{3,1},{4,6},{5,7},{6,4},{7,5},{8,10},{9,11},{10,... | collective-permute-start | bytes 196616 | tf_op jit(solution)/shard_map/ppermute | solution.py:45
  6.8 1.5 %collective-permute-start.2 = (bf16[32,1024]{1,0:T(8,128)(2,1)S(1)}, bf16[32,1024]{1,0:T(8,128)(2,1)S(1)}, u32[]{:S(2)}, u32[]{:S(2)}) collective-permute-start(bf16[32,1024]{1,0:T(8,128)(2,1)S(1)} %get-tuple-element.22), channel_id=1, source_target_pairs={{0,4},{1,5},{2,6},{3,7},{4,0},{5,1},{6,2},{7,3},{8,12},{9,13},{10,... | collective-permute-start | bytes 196616 | tf_op jit(solution)/shard_map/ppermute | solution.py:45
  8.4 0.9 %collective-permute-done.1.refs_1_ = bf16[32,1024]{1,0:T(8,128)(2,1)S(1)} collective-permute-done((bf16[32,1024]{1,0:T(8,128)(2,1)S(1)}, bf16[32,1024]{1,0:T(8,128)(2,1)S(1)}, u32[]{:S(2)}, u32[]{:S(2)}) %collective-permute-start.1) | collective-permute-done | bytes 65568 | tf_op jit(solution)/shard_map/ppermute | solution.py:45
  9.2 1.9 %collective-permute-done.2.refs_2_ = bf16[32,1024]{1,0:T(8,128)(2,1)S(1)} collective-permute-done((bf16[32,1024]{1,0:T(8,128)(2,1)S(1)}, bf16[32,1024]{1,0:T(8,128)(2,1)S(1)}, u32[]{:S(2)}, u32[]{:S(2)}) %collective-permute-start.2) | collective-permute-done | bytes 65568 | tf_op jit(solution)/shard_map/ppermute | solution.py:45
  11.1 2.4 %collective-permute-done.3.refs_3_ = bf16[32,1024]{1,0:T(8,128)(2,1)S(1)} collective-permute-done((bf16[32,1024]{1,0:T(8,128)(2,1)S(1)}, bf16[32,1024]{1,0:T(8,128)(2,1)S(1)}, u32[]{:S(2)}, u32[]{:S(2)}) %collective-permute-start.3) | collective-permute-done | bytes 65568 | tf_op jit(solution)/shard_map/ppermute | solution.py:45
  13.6 1.6 %shard_map.78 = (bf16[32,1024]{1,0:T(8,128)(2,1)S(1)}, bf16[4,32,640]{2,1,0:T(8,128)(2,1)S(1)}) custom-call(bf16[32,1024]{1,0:T(8,128)(2,1)S(1)} %get-tuple-element.20.refs_0_, bf16[32,1024]{1,0:T(8,128)(2,1)S(1)} %collective-permute-done.1.refs_1_, bf16[32,1024]{1,0:T(8,128)(2,1)S(1)} %collective-permute-done.2.refs_2_, ...), custom_call_target="tpu_custom_call" | custom-call | flops 167772160 | bytes 10977280 | tf_op jit(solution)/shard_map/pallas_call | solution.py:32
  15.2 0.0 collective-permute-start.4
  15.2 1.6 %collective-permute-start.8 = (bf16[64,1280]{1,0:T(8,128)(2,1)S(1)}, bf16[64,1280]{1,0:T(8,128)(2,1)S(1)}, u32[]{:S(2)}, u32[]{:S(2)}) collective-permute-start(bf16[64,1280]{1,0:T(8,128)(2,1)S(1)} %get-tuple-element.31), channel_id=1, source_target_pairs={{0,8},{1,17},{2,10},{3,19},{4,12},{5,21},{6,14},{7,23},{8,0},{9,25... | collective-permute-start | bytes 491528 | tf_op jit(solution)/shard_map/ppermute | solution.py:249
  16.9 2.5 %collective-permute-start.10 = (bf16[64,640]{1,0:T(8,128)(2,1)S(1)}, bf16[64,640]{1,0:T(8,128)(2,1)S(1)}, u32[]{:S(2)}, u32[]{:S(2)}) collective-permute-start(bf16[64,640]{1,0:T(8,128)(2,1)S(1)} %get-tuple-element.32), channel_id=1, source_target_pairs={{0,24},{1,25},{2,26},{3,27},{4,28},{5,29},{6,30},{7,31},{8,16},{9,... | collective-permute-start | bytes 245768 | tf_op jit(solution)/shard_map/ppermute | solution.py:249
  19.3 0.1 collective-permute-start.15
  19.5 1.6 %shard_map.79.kept_ref = bf16[4,32,640]{2,1,0:T(8,128)(2,1)S(1)} custom-call(bf16[32,1024]{1,0:T(8,128)(2,1)S(1)} %get-tuple-element.24.merged_ref.refs_0_, bf16[5120,1024]{1,0:T(8,128)(2,1)S(1)} %bitcast.5), custom_call_target="tpu_custom_call" | custom-call | flops 167772160 | bytes 10715136 | tf_op jit(solution)/shard_map/pallas_call | solution.py:32
  21.1 0.0 collective-permute-done.4.came_ref
  21.2 0.6 %collective-permute-start.5 = (bf16[32,640]{1,0:T(8,128)(2,1)S(1)}, bf16[32,640]{1,0:T(8,128)(2,1)S(1)}, u32[]{:S(2)}, u32[]{:S(2)}) collective-permute-start(bf16[32,640]{1,0:T(8,128)(2,1)S(1)} %get-tuple-element.27), channel_id=1, source_target_pairs={{0,2},{1,3},{2,0},{3,1},{4,6},{5,7},{6,4},{7,5},{8,10},{9,11},{10,... | collective-permute-start | bytes 122888 | tf_op jit(solution)/shard_map/ppermute | solution.py:45
  21.8 0.5 %collective-permute-start.6 = (bf16[32,640]{1,0:T(8,128)(2,1)S(1)}, bf16[32,640]{1,0:T(8,128)(2,1)S(1)}, u32[]{:S(2)}, u32[]{:S(2)}) collective-permute-start(bf16[32,640]{1,0:T(8,128)(2,1)S(1)} %get-tuple-element.28), channel_id=1, source_target_pairs={{0,4},{1,5},{2,6},{3,7},{4,0},{5,1},{6,2},{7,3},{8,12},{9,13},{10,... | collective-permute-start | bytes 122888 | tf_op jit(solution)/shard_map/ppermute | solution.py:45
  22.3 3.9 %collective-permute-done.10.refs_3_ = bf16[64,640]{1,0:T(8,128)(2,1)S(1)} collective-permute-done((bf16[64,640]{1,0:T(8,128)(2,1)S(1)}, bf16[64,640]{1,0:T(8,128)(2,1)S(1)}, u32[]{:S(2)}, u32[]{:S(2)}) %collective-permute-start.10) | collective-permute-done | bytes 81952 | tf_op jit(solution)/shard_map/ppermute | solution.py:249
  26.1 0.5 %collective-permute-start.7 = (bf16[32,640]{1,0:T(8,128)(2,1)S(1)}, bf16[32,640]{1,0:T(8,128)(2,1)S(1)}, u32[]{:S(2)}, u32[]{:S(2)}) collective-permute-start(bf16[32,640]{1,0:T(8,128)(2,1)S(1)} %get-tuple-element.29), channel_id=1, source_target_pairs={{0,6},{1,7},{2,4},{3,5},{4,2},{5,3},{6,0},{7,1},{8,14},{9,15},{10,... | collective-permute-start | bytes 122888 | tf_op jit(solution)/shard_map/ppermute | solution.py:45
  26.6 0.8 %shard_map.81 = f32[32,640]{1,0:T(8,128)S(1)} custom-call(bf16[32,5120]{1,0:T(8,128)(2,1)} %bitcast.8), custom_call_target="tpu_custom_call" | custom-call | bytes 409600 | tf_op jit(solution)/shard_map/pallas_call | solution.py:32
  27.5 0.1 collective-permute-start.11
  27.6 0.8 %collective-permute-done.15.refs_1_ = bf16[32,1024]{1,0:T(8,128)(2,1)S(1)} collective-permute-done((bf16[32,1024]{1,0:T(8,128)(2,1)S(1)}, bf16[32,1024]{1,0:T(8,128)(2,1)S(1)}, u32[]{:S(2)}, u32[]{:S(2)}) %collective-permute-start.15) | collective-permute-done | bytes 65568 | tf_op jit(solution)/shard_map/ppermute | solution.py:45
  28.4 0.5 %collective-permute-start.9 = (bf16[64,1280]{1,0:T(8,128)(2,1)S(1)}, bf16[64,1280]{1,0:T(8,128)(2,1)S(1)}, u32[]{:S(2)}, u32[]{:S(2)}) collective-permute-start(bf16[64,1280]{1,0:T(8,128)(2,1)S(1)} %collective-permute-done.8.refs_1_), channel_id=1, source_target_pairs={{0,1},{1,0},{2,3},{3,2},{4,5},{5,4},{6,7},{7,6},{8,9},{9,8},{10,11... | collective-permute-start | bytes 491528 | tf_op jit(solution)/shard_map/ppermute | solution.py:45
  28.9 1.5 %collective-permute-start.16 = (bf16[64,1024]{1,0:T(8,128)(2,1)S(1)}, bf16[64,1024]{1,0:T(8,128)(2,1)S(1)}, u32[]{:S(2)}, u32[]{:S(2)}) collective-permute-start(bf16[64,1024]{1,0:T(8,128)(2,1)S(1)} %shard_map.83.refs_5_), channel_id=1, source_target_pairs={{0,8},{8,0},{16,24},{24,16},{1,9},{9,1},{17,25},{25,17},{2,10},{10... | collective-permute-start | bytes 393224 | tf_op jit(solution)/shard_map/ppermute | solution.py:45
  30.5 0.6 %collective-permute-done.7 = bf16[32,640]{1,0:T(8,128)(2,1)S(1)} collective-permute-done((bf16[32,640]{1,0:T(8,128)(2,1)S(1)}, bf16[32,640]{1,0:T(8,128)(2,1)S(1)}, u32[]{:S(2)}, u32[]{:S(2)}) %collective-permute-start.7) | collective-permute-done | bytes 40992 | tf_op jit(solution)/shard_map/ppermute | solution.py:45
  31.1 1.5 %collective-permute-start.12 = (bf16[32,640]{1,0:T(8,128)(2,1)S(1)}, bf16[32,640]{1,0:T(8,128)(2,1)S(1)}, u32[]{:S(2)}, u32[]{:S(2)}) collective-permute-start(bf16[32,640]{1,0:T(8,128)(2,1)S(1)} %multiply_convert_fusion.refs_5_), channel_id=1, source_target_pairs={{0,8},{8,0},{16,24},{24,16},{1,9},{9,1},{17,25},{25,17},{2,10},{10... | collective-permute-start | bytes 122888 | tf_op jit(solution)/shard_map/ppermute | solution.py:45
  32.6 1.7 %collective-permute-start.13 = (bf16[32,640]{1,0:T(8,128)(2,1)S(1)}, bf16[32,640]{1,0:T(8,128)(2,1)S(1)}, u32[]{:S(2)}, u32[]{:S(2)}) collective-permute-start(bf16[32,640]{1,0:T(8,128)(2,1)S(1)} %multiply_convert_fusion.refs_5_), channel_id=1, source_target_pairs={{0,16},{8,24},{16,0},{24,8},{1,17},{9,25},{17,1},{25,9},{2,18},{10... | collective-permute-start | bytes 122888 | tf_op jit(solution)/shard_map/ppermute | solution.py:45
  34.2 1.3 %collective-permute-start.14 = (bf16[32,640]{1,0:T(8,128)(2,1)S(1)}, bf16[32,640]{1,0:T(8,128)(2,1)S(1)}, u32[]{:S(2)}, u32[]{:S(2)}) collective-permute-start(bf16[32,640]{1,0:T(8,128)(2,1)S(1)} %multiply_convert_fusion.refs_5_), channel_id=1, source_target_pairs={{0,24},{8,16},{16,8},{24,0},{1,25},{9,17},{17,9},{25,1},{2,26},{10... | collective-permute-start | bytes 122888 | tf_op jit(solution)/shard_map/ppermute | solution.py:45
  35.6 2.7 %shard_map.84 = f32[1280,1024]{1,0:T(8,128)} custom-call(bf16[64,1280]{1,0:T(8,128)(2,1)S(1)} %get-tuple-element.30.refs_0_, bf16[64,1280]{1,0:T(8,128)(2,1)S(1)} %collective-permute-done.8.refs_1_, bf16[64,1280]{1,0:T(8,128)(2,1)S(1)} %collective-permute-done.9.refs_2_, bf16[64,640]{1,0:T(8,128)(2,1)S(1)} %collective-permute-done.10.refs_3_, ...), custom_call_target="tpu_custom_call" | custom-call | flops 335544320 | bytes 6160384 | tf_op jit(solution)/shard_map/pallas_call | solution.py:32
  38.3 1.8 %collective-permute-done.14.refs_8_ = bf16[32,640]{1,0:T(8,128)(2,1)S(1)} collective-permute-done((bf16[32,640]{1,0:T(8,128)(2,1)S(1)}, bf16[32,640]{1,0:T(8,128)(2,1)S(1)}, u32[]{:S(2)}, u32[]{:S(2)}) %collective-permute-start.14) | collective-permute-done | bytes 40992 | tf_op jit(solution)/shard_map/ppermute | solution.py:45
  40.1 2.0 %shard_map.82 = f32[1280,640]{1,0:T(8,128)} custom-call(bf16[64,1280]{1,0:T(8,128)(2,1)S(1)} %get-tuple-element.30.refs_0_, bf16[64,1280]{1,0:T(8,128)(2,1)S(1)} %collective-permute-done.8.refs_1_, bf16[64,1280]{1,0:T(8,128)(2,1)S(1)} %collective-permute-done.9.refs_2_, bf16[64,640]{1,0:T(8,128)(2,1)S(1)} %collective-permute-done.10.refs_3_, ...), custom_call_target="tpu_custom_call" | custom-call | flops 209715200 | bytes 4096000 | tf_op jit(solution)/shard_map/pallas_call | solution.py:32
  (21 shorter events, 0.1 us)
Async XLA Ops:
  2.1 1.7 %collective-permute-start = (bf16[4,32,1024]{2,1,0:T(8,128)(2,1)S(1)}, bf16[4,32,1024]{2,1,0:T(8,128)(2,1)S(1)}, u32[]{:S(2)}, u32[]{:S(2)}) collective-permute-start(bf16[4,32,1024]{2,1,0:T(8,128)(2,1)S(1)} %get-tuple-element.19), channel_id=1, source_target_pairs={{0,1},{1,0},{2,3},{3,2},{4,5},{5,4},{6,7},{7,6},{8,9},{9,8},{10,11... | collective-permute-start | bytes 786440 | tf_op jit(solution)/shard_map/ppermute | solution.py:45
  3.9 9.7 %slice-start = ((s8[10485760]{0:T(1024)(128)(4,1)}), s8[4194304]{0:T(1024)(128)(4,1)S(1)}, s32[]{:S(2)}) async-start(s8[10485760]{0:T(1024)(128)(4,1)} %bitcast.4), calls=%async_computation | async-start | bytes 8388608
  3.9 9.7 %slice-start.1 = ((s8[10485760]{0:T(1024)(128)(4,1)}), s8[4194304]{0:T(1024)(128)(4,1)S(1)}, s32[]{:S(2)}) async-start(s8[10485760]{0:T(1024)(128)(4,1)} %bitcast.4), calls=%async_computation.1 | async-start | bytes 8388608
  3.9 9.7 %slice-start.2 = ((s8[10485760]{0:T(1024)(128)(4,1)}), s8[2097152]{0:T(1024)(128)(4,1)S(1)}, s32[]{:S(2)}) async-start(s8[10485760]{0:T(1024)(128)(4,1)} %bitcast.4), calls=%async_computation.2 | async-start | bytes 4194304
  3.9 5.3 %collective-permute-start.1 = (bf16[32,1024]{1,0:T(8,128)(2,1)S(1)}, bf16[32,1024]{1,0:T(8,128)(2,1)S(1)}, u32[]{:S(2)}, u32[]{:S(2)}) collective-permute-start(bf16[32,1024]{1,0:T(8,128)(2,1)S(1)} %get-tuple-element.21), channel_id=1, source_target_pairs={{0,2},{1,3},{2,0},{3,1},{4,6},{5,7},{6,4},{7,5},{8,10},{9,11},{10,... | collective-permute-start | bytes 196616 | tf_op jit(solution)/shard_map/ppermute | solution.py:45
  6.8 4.3 %collective-permute-start.2 = (bf16[32,1024]{1,0:T(8,128)(2,1)S(1)}, bf16[32,1024]{1,0:T(8,128)(2,1)S(1)}, u32[]{:S(2)}, u32[]{:S(2)}) collective-permute-start(bf16[32,1024]{1,0:T(8,128)(2,1)S(1)} %get-tuple-element.22), channel_id=1, source_target_pairs={{0,4},{1,5},{2,6},{3,7},{4,0},{5,1},{6,2},{7,3},{8,12},{9,13},{10,... | collective-permute-start | bytes 196616 | tf_op jit(solution)/shard_map/ppermute | solution.py:45
  8.4 5.2 %collective-permute-start.3 = (bf16[32,1024]{1,0:T(8,128)(2,1)S(1)}, bf16[32,1024]{1,0:T(8,128)(2,1)S(1)}, u32[]{:S(2)}, u32[]{:S(2)}) collective-permute-start(bf16[32,1024]{1,0:T(8,128)(2,1)S(1)} %get-tuple-element.23), channel_id=1, source_target_pairs={{0,6},{1,7},{2,4},{3,5},{4,2},{5,3},{6,0},{7,1},{8,14},{9,15},{10,... | collective-permute-start | bytes 196616 | tf_op jit(solution)/shard_map/ppermute | solution.py:45
  15.2 5.9 %collective-permute-start.4 = (bf16[4,32,640]{2,1,0:T(8,128)(2,1)S(1)}, bf16[4,32,640]{2,1,0:T(8,128)(2,1)S(1)}, u32[]{:S(2)}, u32[]{:S(2)}) collective-permute-start(bf16[4,32,640]{2,1,0:T(8,128)(2,1)S(1)} %get-tuple-element.25), channel_id=1, source_target_pairs={{0,1},{1,0},{2,3},{3,2},{4,5},{5,4},{6,7},{7,6},{8,9},{9,8},{10,11... | collective-permute-start | bytes 491528 | tf_op jit(solution)/shard_map/ppermute | solution.py:45
  15.2 12.2 %collective-permute-start.8 = (bf16[64,1280]{1,0:T(8,128)(2,1)S(1)}, bf16[64,1280]{1,0:T(8,128)(2,1)S(1)}, u32[]{:S(2)}, u32[]{:S(2)}) collective-permute-start(bf16[64,1280]{1,0:T(8,128)(2,1)S(1)} %get-tuple-element.31), channel_id=1, source_target_pairs={{0,8},{1,17},{2,10},{3,19},{4,12},{5,21},{6,14},{7,23},{8,0},{9,25... | collective-permute-start | bytes 491528 | tf_op jit(solution)/shard_map/ppermute | solution.py:249
  16.9 9.3 %collective-permute-start.10 = (bf16[64,640]{1,0:T(8,128)(2,1)S(1)}, bf16[64,640]{1,0:T(8,128)(2,1)S(1)}, u32[]{:S(2)}, u32[]{:S(2)}) collective-permute-start(bf16[64,640]{1,0:T(8,128)(2,1)S(1)} %get-tuple-element.32), channel_id=1, source_target_pairs={{0,24},{1,25},{2,26},{3,27},{4,28},{5,29},{6,30},{7,31},{8,16},{9,... | collective-permute-start | bytes 245768 | tf_op jit(solution)/shard_map/ppermute | solution.py:249
  19.3 9.1 %collective-permute-start.15 = (bf16[32,1024]{1,0:T(8,128)(2,1)S(1)}, bf16[32,1024]{1,0:T(8,128)(2,1)S(1)}, u32[]{:S(2)}, u32[]{:S(2)}) collective-permute-start(bf16[32,1024]{1,0:T(8,128)(2,1)S(1)} %get-tuple-element.24.merged_ref.refs_0_), channel_id=1, source_target_pairs={{0,16},{8,24},{16,0},{24,8},{1,17},{9,25},{17,1},{25,9},{2,18},{10... | collective-permute-start | bytes 196616 | tf_op jit(solution)/shard_map/ppermute | solution.py:45
  21.2 7.8 %collective-permute-start.5 = (bf16[32,640]{1,0:T(8,128)(2,1)S(1)}, bf16[32,640]{1,0:T(8,128)(2,1)S(1)}, u32[]{:S(2)}, u32[]{:S(2)}) collective-permute-start(bf16[32,640]{1,0:T(8,128)(2,1)S(1)} %get-tuple-element.27), channel_id=1, source_target_pairs={{0,2},{1,3},{2,0},{3,1},{4,6},{5,7},{6,4},{7,5},{8,10},{9,11},{10,... | collective-permute-start | bytes 122888 | tf_op jit(solution)/shard_map/ppermute | solution.py:45
  21.8 8.7 %collective-permute-start.6 = (bf16[32,640]{1,0:T(8,128)(2,1)S(1)}, bf16[32,640]{1,0:T(8,128)(2,1)S(1)}, u32[]{:S(2)}, u32[]{:S(2)}) collective-permute-start(bf16[32,640]{1,0:T(8,128)(2,1)S(1)} %get-tuple-element.28), channel_id=1, source_target_pairs={{0,4},{1,5},{2,6},{3,7},{4,0},{5,1},{6,2},{7,3},{8,12},{9,13},{10,... | collective-permute-start | bytes 122888 | tf_op jit(solution)/shard_map/ppermute | solution.py:45
  26.1 4.9 %collective-permute-start.7 = (bf16[32,640]{1,0:T(8,128)(2,1)S(1)}, bf16[32,640]{1,0:T(8,128)(2,1)S(1)}, u32[]{:S(2)}, u32[]{:S(2)}) collective-permute-start(bf16[32,640]{1,0:T(8,128)(2,1)S(1)} %get-tuple-element.29), channel_id=1, source_target_pairs={{0,6},{1,7},{2,4},{3,5},{4,2},{5,3},{6,0},{7,1},{8,14},{9,15},{10,... | collective-permute-start | bytes 122888 | tf_op jit(solution)/shard_map/ppermute | solution.py:45
  27.5 6.8 %collective-permute-start.11 = (bf16[64,640]{1,0:T(8,128)(2,1)S(1)}, bf16[64,640]{1,0:T(8,128)(2,1)S(1)}, u32[]{:S(2)}, u32[]{:S(2)}) collective-permute-start(bf16[64,640]{1,0:T(8,128)(2,1)S(1)} %collective-permute-done.10.refs_3_), channel_id=1, source_target_pairs={{0,1},{1,0},{2,3},{3,2},{4,5},{5,4},{6,7},{7,6},{8,9},{9,8},{10,11... | collective-permute-start | bytes 245768 | tf_op jit(solution)/shard_map/ppermute | solution.py:45
  28.4 7.2 %collective-permute-start.9 = (bf16[64,1280]{1,0:T(8,128)(2,1)S(1)}, bf16[64,1280]{1,0:T(8,128)(2,1)S(1)}, u32[]{:S(2)}, u32[]{:S(2)}) collective-permute-start(bf16[64,1280]{1,0:T(8,128)(2,1)S(1)} %collective-permute-done.8.refs_1_), channel_id=1, source_target_pairs={{0,1},{1,0},{2,3},{3,2},{4,5},{5,4},{6,7},{7,6},{8,9},{9,8},{10,11... | collective-permute-start | bytes 491528 | tf_op jit(solution)/shard_map/ppermute | solution.py:45
  28.9 6.6 %collective-permute-start.16 = (bf16[64,1024]{1,0:T(8,128)(2,1)S(1)}, bf16[64,1024]{1,0:T(8,128)(2,1)S(1)}, u32[]{:S(2)}, u32[]{:S(2)}) collective-permute-start(bf16[64,1024]{1,0:T(8,128)(2,1)S(1)} %shard_map.83.refs_5_), channel_id=1, source_target_pairs={{0,8},{8,0},{16,24},{24,16},{1,9},{9,1},{17,25},{25,17},{2,10},{10... | collective-permute-start | bytes 393224 | tf_op jit(solution)/shard_map/ppermute | solution.py:45
  31.1 11.1 %copy-start = (bf16[32,640]{1,0:T(8,128)(2,1)}, bf16[32,640]{1,0:T(8,128)(2,1)S(1)}, u32[]{:S(2)}) copy-start(bf16[32,640]{1,0:T(8,128)(2,1)S(1)} %multiply_convert_fusion.refs_5_) | copy-start | bytes 122884
  31.1 7.2 %collective-permute-start.12 = (bf16[32,640]{1,0:T(8,128)(2,1)S(1)}, bf16[32,640]{1,0:T(8,128)(2,1)S(1)}, u32[]{:S(2)}, u32[]{:S(2)}) collective-permute-start(bf16[32,640]{1,0:T(8,128)(2,1)S(1)} %multiply_convert_fusion.refs_5_), channel_id=1, source_target_pairs={{0,8},{8,0},{16,24},{24,16},{1,9},{9,1},{17,25},{25,17},{2,10},{10... | collective-permute-start | bytes 122888 | tf_op jit(solution)/shard_map/ppermute | solution.py:45
  32.6 5.7 %collective-permute-start.13 = (bf16[32,640]{1,0:T(8,128)(2,1)S(1)}, bf16[32,640]{1,0:T(8,128)(2,1)S(1)}, u32[]{:S(2)}, u32[]{:S(2)}) collective-permute-start(bf16[32,640]{1,0:T(8,128)(2,1)S(1)} %multiply_convert_fusion.refs_5_), channel_id=1, source_target_pairs={{0,16},{8,24},{16,0},{24,8},{1,17},{9,25},{17,1},{25,9},{2,18},{10... | collective-permute-start | bytes 122888 | tf_op jit(solution)/shard_map/ppermute | solution.py:45
  34.2 5.8 %collective-permute-start.14 = (bf16[32,640]{1,0:T(8,128)(2,1)S(1)}, bf16[32,640]{1,0:T(8,128)(2,1)S(1)}, u32[]{:S(2)}, u32[]{:S(2)}) collective-permute-start(bf16[32,640]{1,0:T(8,128)(2,1)S(1)} %multiply_convert_fusion.refs_5_), channel_id=1, source_target_pairs={{0,24},{8,16},{16,8},{24,0},{1,25},{9,17},{17,9},{25,1},{2,26},{10... | collective-permute-start | bytes 122888 | tf_op jit(solution)/shard_map/ppermute | solution.py:45

commit v6 on v5

--- a/solution.py
+++ b/solution.py
@@ -116,11 +116,12 @@
 def unit_blocks(parity, merged, w_ref, out_ref):
     shard = lax.axis_index("roll")
     halves, _, unit_cols = out_ref.shape
+    turned = merged.T
     for j in range(halves):
         first = pl.multiple_of((shard ^ (2 * j + parity)) * unit_cols, unit_cols)
         out_ref[j] = lax.dot_general(
-            merged, w_ref[pl.ds(first, unit_cols), :], (((1,), (1,)), ((), ())), preferred_element_type=jnp.float32
-        ).astype(jnp.bfloat16)
+            w_ref[pl.ds(first, unit_cols), :], turned, (((1,), (0,)), ((), ())), preferred_element_type=jnp.float32
+        ).T.astype(jnp.bfloat16)
 
 
 def first_units(*refs):
@@ -136,12 +137,12 @@
     unit_blocks(0, merged_ref[...], w_ref, out_ref)
 
 
-def write_products(left_of, right, factor, out_ref, held, sems):
+def write_products(left_of, right, left_dim, factor, out_ref, held, sems):
     size = held.shape[1]
     copies = []
     for j in range(held.shape[0]):
         held[j] = lax.dot_general(
-            left_of(j * size, size), right, (((0,), (0,)), ((), ())), preferred_element_type=jnp.float32
+            left_of(j * size, size), right, (((left_dim,), (0,)), ((), ())), preferred_element_type=jnp.float32
         ) * factor
         copies.append(pltpu.make_async_copy(held.at[j], out_ref.at[pl.ds(j * size, size), :], sems.at[j]))
         copies[-1].start()
@@ -149,45 +150,61 @@
         copy.wait()
 
 
-def block_products(part, factor, places, *refs):
+def right_blocks(places, rows, refs):
     groups = len(places)
-    feature_refs, right_refs, (out_ref, held, sems) = refs[: groups + 1], refs[groups + 1 : -3], refs[-3:]
-    *whole_refs, mine_ref, came_ref = feature_refs
-    rows = mine_ref.shape[0] // 2
-    rows_cut = slice(part * rows, (part + 1) * rows)
-    half_cols = mine_ref.shape[1]
     lane = lax.axis_index("roll") % 2
-
-    def left_of(first, size):
-        half, start = divmod(first, half_cols)
-        pieces = [ref[rows_cut, first : first + size] for ref in whole_refs]
-        mine, came = (ref[rows_cut, start : start + size] for ref in (mine_ref, came_ref))
-        left = jnp.concatenate(pieces + [jnp.where(lane == half, mine, came)], axis=0)
-        return left if part else gelu(left.astype(jnp.float32)).astype(jnp.bfloat16)
-
-    right = [right_refs[index][start : start + rows, :] for index, start in places]
+    right = [refs[index][start : start + rows, :] for index, start in places]
     for k in range(1, groups - 1, 2):
         right[k], right[k + 1] = (
             jnp.where(lane == 0, right[k], right[k + 1]),
             jnp.where(lane == 0, right[k + 1], right[k]),
         )
-    write_products(left_of, jnp.concatenate(right, axis=0), factor, out_ref, held, sems)
-
-
-def products(part, factor, features, rights, order):
-    rows = features[0].shape[0] // 2
-    in_cols, columns = features[0].shape[1], rights[0].shape[1]
+    return jnp.concatenate(right, axis=0)
+
+
+def second_products(factor, places, *refs):
+    groups = len(places)
+    feature_refs, right_refs, (out_ref, turned_ref, held, sems) = refs[: groups + 1], refs[groups + 1 : -4], refs[-4:]
+    *whole_refs, mine_ref, came_ref = feature_refs
+    rows, half_cols = mine_ref.shape[0] // 2, mine_ref.shape[1]
+    lane = lax.axis_index("roll") % 2
+
+    def features_of(part, first, size):
+        rows_cut = slice(part * rows, (part + 1) * rows)
+        half, start = divmod(first, half_cols)
+        pieces = [ref[rows_cut, first : first + size] for ref in whole_refs]
+        mine, came = (ref[rows_cut, start : start + size] for ref in (mine_ref, came_ref))
+        return jnp.concatenate(pieces + [jnp.where(lane == half, mine, came)], axis=0)
+
+    def left_of(first, size):
+        turned_ref[first : first + size, :] = features_of(1, first, size).T
+        return gelu(features_of(0, first, size).astype(jnp.float32)).astype(jnp.bfloat16)
+
+    write_products(left_of, right_blocks(places, rows, right_refs), 0, factor, out_ref, held, sems)
+
+
+def first_products(factor, places, turned_ref, *refs):
+    right_refs, (out_ref, held, sems) = refs[:-3], refs[-3:]
+    rows = turned_ref.shape[1] // len(places)
+
+    def left_of(first, size):
+        return turned_ref[first : first + size, :]
+
+    write_products(left_of, right_blocks(places, rows, right_refs), 1, factor, out_ref, held, sems)
+
+
+def products(kernel, factor, lefts, rights, order, in_cols, rows, extra):
+    columns = rights[0].shape[1]
     spots = [(i, first) for i, right in enumerate(rights) for first in range(0, right.shape[0], rows)]
     places = [spots[order.index(k)] for k in range(len(order))]
     size = 128 if in_cols % 256 == 0 else in_cols // 2
     out = shape((in_cols, columns), jnp.float32)
-    (result,) = call(
-        functools.partial(block_products, part, factor, places), [out], (*features, *rights),
-        2 * len(order) * rows * in_cols * columns, out_specs=[HBM],
+    return call(
+        functools.partial(kernel, factor, places), [out, *extra], (*lefts, *rights),
+        2 * len(order) * rows * in_cols * columns, out_specs=[HBM] + [VMEM] * len(extra),
         scratch=[pltpu.VMEM((in_cols // size, size, columns), jnp.float32), pltpu.SemaphoreType.DMA((in_cols // size,))],
         limit=(6 << 20) + 4 * in_cols * columns,
     )
-    return result
 
 
 def body(row_grads, row_dest, merger_in, hidden_pre, w_second):
@@ -250,15 +267,13 @@
         features += [came, exchange(came, "roll", 1)]
 
     pieces = spread(kept, exchange(sent, "roll", 1))
-    weights = w_second
-
     unit_shape = (halves, merged_count, unit_cols)
     flops = 2 * columns * math.prod(unit_shape)
     merged, sent = call(
-        first_units, [shape((merged_count, columns), kind), shape(unit_shape, kind)], (*pieces, weights), flops,
+        first_units, [shape((merged_count, columns), kind), shape(unit_shape, kind)], (*pieces, w_second), flops,
     )
     came = exchange(sent, "roll", 1)
-    (kept,) = call(second_units, [shape(unit_shape, kind)], (merged, weights), flops)
+    (kept,) = call(second_units, [shape(unit_shape, kind)], (merged, w_second), flops)
 
     merged_all, order, step = [merged], [0], groups // 2
     while step:
@@ -274,8 +289,13 @@
     grads_all = [grads] + [exchange(grads, "enc", k) for k in range(1, groups)]
 
     factor = 1.0 / math.sqrt(merged_count * groups)
-    grad_second = products(0, factor, features, merged_all, order)
-    grad_first = products(1, factor, features, grads_all, list(range(groups)))
+    turned = shape((in_cols, groups * merged_count), kind)
+    grad_second, turned = products(
+        second_products, factor, features, merged_all, order, in_cols, merged_count, [turned]
+    )
+    (grad_first,) = products(
+        first_products, factor, [turned], grads_all, list(range(groups)), in_cols, merged_count, []
+    )
     return (grads[None], grad_first, grad_second)
 
 

time: 42.4 us -> 39.6 us (0.934)
  waiting for transfers between devices: 13.5 us -> 7.53 us
  starting transfers between devices: 17.4 us -> 20.7 us
    ppermute x2, waiting for transfers between devices: 3.88 us -> 0.13 us  [body(): came = lax.ppermute(block, ('enc', 'roll'), pairs)]
    ppermute x15, starting transfers between devices: 13.4 us -> 17.1 us  [exchange(): return lax.ppermute(block, axis, pairs)]
    ppermute x15, waiting for transfers between devices: 9.57 us -> 7.39 us  [exchange(): return lax.ppermute(block, axis, pairs)]
    ppermute x2, starting transfers between devices: 4.09 us -> 3.65 us  [body(): came = lax.ppermute(block, ('enc', 'roll'), pairs)]
  transfers between devices with their start and end apart: 17 -> 17, of which waited for: 8 -> 7; matrix products, arithmetic and copies ran while one was open for 0% -> 0% of each run, Pallas kernels for 12% -> 13%
where the time goes in v6:
time: 39.6 us; the launch traced here: 39.3 us
  starting transfers between devices  20.7 us (52%)
  Pallas kernels  10.3 us (26%)
  waiting for transfers between devices  7.53 us (19%)
  between operations  0.78 us (2%)
    ppermute x15, starting transfers between devices, exchange(): return lax.ppermute(block, axis, pairs)  17.1 us
    pallas_call x9, Pallas kernels, call(): pl.pallas_call(kernel, out_shape=outs, in_specs=in_specs or [VMEM] * len(...  10.3 us
    ppermute x15, waiting for transfers between devices, exchange(): return lax.ppermute(block, axis, pairs)  7.39 us
    ppermute x2, starting transfers between devices, body(): came = lax.ppermute(block, ('enc', 'roll'), pairs)  3.65 us
  transfers between devices with their start and end apart: 17, of which 7 were waited for; matrix products, arithmetic and copies ran while one was open for 0% of the time, Pallas kernels for 13%

profile of v6, /device:TPU:0, one launch (start us, length us, event | category | flops | bytes accessed | tf_op | source)
XLA Modules:
  0.0 39.3 jit_solution(6389377548517790172)
XLA Ops:
  0.6 1.5 %shard_map.76 = (bf16[4,32,1024]{2,1,0:T(8,128)(2,1)S(1)}, bf16[4,32,1024]{2,1,0:T(8,128)(2,1)S(1)}, bf16[64,1280]{1,0:T(8,128)(2,1)S(1)}, bf16[64,1280]{1,0:T(8,128)(2,1)S(1)}, bf16[64,640]{1,0:T(8,128)(2,1)S(1)}) custom-call(s32[1,32]{1,0:T(1,128)} %refs_0_.1, bf16[32,8192]{1,0:T(8,128)(2,1)} %bitcast.9, bf16[32,5120]{1,0:T(8,128)(2,1)} %bitcast.7, ...), custom_call_target="tpu_custom_call" | custom-call | flops 16777216 | bytes 2113664 | tf_op jit(solution)/shard_map/pallas_call | solution.py:32
  2.1 0.6 %collective-permute-start = (bf16[4,32,1024]{2,1,0:T(8,128)(2,1)S(1)}, bf16[4,32,1024]{2,1,0:T(8,128)(2,1)S(1)}, u32[]{:S(2)}, u32[]{:S(2)}) collective-permute-start(bf16[4,32,1024]{2,1,0:T(8,128)(2,1)S(1)} %get-tuple-element.21), channel_id=1, source_target_pairs={{0,1},{1,0},{2,3},{3,2},{4,5},{5,4},{6,7},{7,6},{8,9},{9,8},{10,11... | collective-permute-start | bytes 786440 | tf_op jit(solution)/shard_map/ppermute | solution.py:45
  2.7 1.2 %collective-permute-done.came_ref = bf16[4,32,1024]{2,1,0:T(8,128)(2,1)S(1)} collective-permute-done((bf16[4,32,1024]{2,1,0:T(8,128)(2,1)S(1)}, bf16[4,32,1024]{2,1,0:T(8,128)(2,1)S(1)}, u32[]{:S(2)}, u32[]{:S(2)}) %collective-permute-start) | collective-permute-done | bytes 262176 | tf_op jit(solution)/shard_map/ppermute | solution.py:45
  3.9 0.1 shard_map.77
  3.9 2.9 %collective-permute-start.1 = (bf16[32,1024]{1,0:T(8,128)(2,1)S(1)}, bf16[32,1024]{1,0:T(8,128)(2,1)S(1)}, u32[]{:S(2)}, u32[]{:S(2)}) collective-permute-start(bf16[32,1024]{1,0:T(8,128)(2,1)S(1)} %get-tuple-element.23), channel_id=1, source_target_pairs={{0,2},{1,3},{2,0},{3,1},{4,6},{5,7},{6,4},{7,5},{8,10},{9,11},{10,... | collective-permute-start | bytes 196616 | tf_op jit(solution)/shard_map/ppermute | solution.py:45
  6.8 1.5 %collective-permute-start.2 = (bf16[32,1024]{1,0:T(8,128)(2,1)S(1)}, bf16[32,1024]{1,0:T(8,128)(2,1)S(1)}, u32[]{:S(2)}, u32[]{:S(2)}) collective-permute-start(bf16[32,1024]{1,0:T(8,128)(2,1)S(1)} %get-tuple-element.24), channel_id=1, source_target_pairs={{0,4},{1,5},{2,6},{3,7},{4,0},{5,1},{6,2},{7,3},{8,12},{9,13},{10,... | collective-permute-start | bytes 196616 | tf_op jit(solution)/shard_map/ppermute | solution.py:45
  8.4 0.0 collective-permute-start.3
  8.4 0.9 %collective-permute-done.1.refs_1_ = bf16[32,1024]{1,0:T(8,128)(2,1)S(1)} collective-permute-done((bf16[32,1024]{1,0:T(8,128)(2,1)S(1)}, bf16[32,1024]{1,0:T(8,128)(2,1)S(1)}, u32[]{:S(2)}, u32[]{:S(2)}) %collective-permute-start.1) | collective-permute-done | bytes 65568 | tf_op jit(solution)/shard_map/ppermute | solution.py:45
  9.2 1.9 %collective-permute-done.2.refs_2_ = bf16[32,1024]{1,0:T(8,128)(2,1)S(1)} collective-permute-done((bf16[32,1024]{1,0:T(8,128)(2,1)S(1)}, bf16[32,1024]{1,0:T(8,128)(2,1)S(1)}, u32[]{:S(2)}, u32[]{:S(2)}) %collective-permute-start.2) | collective-permute-done | bytes 65568 | tf_op jit(solution)/shard_map/ppermute | solution.py:45
  11.1 2.4 %collective-permute-done.3.refs_3_ = bf16[32,1024]{1,0:T(8,128)(2,1)S(1)} collective-permute-done((bf16[32,1024]{1,0:T(8,128)(2,1)S(1)}, bf16[32,1024]{1,0:T(8,128)(2,1)S(1)}, u32[]{:S(2)}, u32[]{:S(2)}) %collective-permute-start.3) | collective-permute-done | bytes 65568 | tf_op jit(solution)/shard_map/ppermute | solution.py:45
  13.6 1.6 %shard_map.78 = (bf16[32,1024]{1,0:T(8,128)(2,1)S(1)}, bf16[4,32,640]{2,1,0:T(8,128)(2,1)S(1)}) custom-call(bf16[32,1024]{1,0:T(8,128)(2,1)S(1)} %get-tuple-element.22.refs_0_, bf16[32,1024]{1,0:T(8,128)(2,1)S(1)} %collective-permute-done.1.refs_1_, bf16[32,1024]{1,0:T(8,128)(2,1)S(1)} %collective-permute-done.2.refs_2_, ...), custom_call_target="tpu_custom_call" | custom-call | flops 167772160 | bytes 10977280 | tf_op jit(solution)/shard_map/pallas_call | solution.py:32
  15.1 0.1 collective-permute-start.4
  15.2 3.6 %collective-permute-start.10 = (bf16[64,640]{1,0:T(8,128)(2,1)S(1)}, bf16[64,640]{1,0:T(8,128)(2,1)S(1)}, u32[]{:S(2)}, u32[]{:S(2)}) collective-permute-start(bf16[64,640]{1,0:T(8,128)(2,1)S(1)} %get-tuple-element.34), channel_id=1, source_target_pairs={{0,24},{1,25},{2,26},{3,27},{4,28},{5,29},{6,30},{7,31},{8,16},{9,... | collective-permute-start | bytes 245768 | tf_op jit(solution)/shard_map/ppermute | solution.py:266
  18.9 0.8 %collective-permute-start.12 = (bf16[32,1024]{1,0:T(8,128)(2,1)S(1)}, bf16[32,1024]{1,0:T(8,128)(2,1)S(1)}, u32[]{:S(2)}, u32[]{:S(2)}) collective-permute-start(bf16[32,1024]{1,0:T(8,128)(2,1)S(1)} %get-tuple-element.26.merged_ref.refs_0_), channel_id=1, source_target_pairs={{0,16},{8,24},{16,0},{24,8},{1,17},{9,25},{17,1},{25,9},{2,18},{10... | collective-permute-start | bytes 196616 | tf_op jit(solution)/shard_map/ppermute | solution.py:45
  19.7 1.6 %shard_map.79.kept_ref = bf16[4,32,640]{2,1,0:T(8,128)(2,1)S(1)} custom-call(bf16[32,1024]{1,0:T(8,128)(2,1)S(1)} %get-tuple-element.26.merged_ref.refs_0_, bf16[5120,1024]{1,0:T(8,128)(2,1)S(1)} %bitcast.5), custom_call_target="tpu_custom_call" | custom-call | flops 167772160 | bytes 10715136 | tf_op jit(solution)/shard_map/pallas_call | solution.py:32
  21.3 0.6 %collective-permute-start.5 = (bf16[32,640]{1,0:T(8,128)(2,1)S(1)}, bf16[32,640]{1,0:T(8,128)(2,1)S(1)}, u32[]{:S(2)}, u32[]{:S(2)}) collective-permute-start(bf16[32,640]{1,0:T(8,128)(2,1)S(1)} %get-tuple-element.29), channel_id=1, source_target_pairs={{0,2},{1,3},{2,0},{3,1},{4,6},{5,7},{6,4},{7,5},{8,10},{9,11},{10,... | collective-permute-start | bytes 122888 | tf_op jit(solution)/shard_map/ppermute | solution.py:45
  21.9 0.4 %collective-permute-start.6 = (bf16[32,640]{1,0:T(8,128)(2,1)S(1)}, bf16[32,640]{1,0:T(8,128)(2,1)S(1)}, u32[]{:S(2)}, u32[]{:S(2)}) collective-permute-start(bf16[32,640]{1,0:T(8,128)(2,1)S(1)} %get-tuple-element.30), channel_id=1, source_target_pairs={{0,4},{1,5},{2,6},{3,7},{4,0},{5,1},{6,2},{7,3},{8,12},{9,13},{10,... | collective-permute-start | bytes 122888 | tf_op jit(solution)/shard_map/ppermute | solution.py:45
  22.3 0.1 collective-permute-done.10.refs_3_
  22.4 2.4 %collective-permute-start.7 = (bf16[32,640]{1,0:T(8,128)(2,1)S(1)}, bf16[32,640]{1,0:T(8,128)(2,1)S(1)}, u32[]{:S(2)}, u32[]{:S(2)}) collective-permute-start(bf16[32,640]{1,0:T(8,128)(2,1)S(1)} %get-tuple-element.31), channel_id=1, source_target_pairs={{0,6},{1,7},{2,4},{3,5},{4,2},{5,3},{6,0},{7,1},{8,14},{9,15},{10,... | collective-permute-start | bytes 122888 | tf_op jit(solution)/shard_map/ppermute | solution.py:45
  24.8 0.8 %shard_map.81 = f32[32,640]{1,0:T(8,128)S(1)} custom-call(bf16[32,5120]{1,0:T(8,128)(2,1)} %bitcast.8), custom_call_target="tpu_custom_call" | custom-call | bytes 409600 | tf_op jit(solution)/shard_map/pallas_call | solution.py:32
  25.7 2.6 %collective-permute-start.11 = (bf16[64,640]{1,0:T(8,128)(2,1)S(1)}, bf16[64,640]{1,0:T(8,128)(2,1)S(1)}, u32[]{:S(2)}, u32[]{:S(2)}) collective-permute-start(bf16[64,640]{1,0:T(8,128)(2,1)S(1)} %collective-permute-done.10.refs_3_), channel_id=1, source_target_pairs={{0,1},{1,0},{2,3},{3,2},{4,5},{5,4},{6,7},{7,6},{8,9},{9,8},{10,11... | collective-permute-start | bytes 245768 | tf_op jit(solution)/shard_map/ppermute | solution.py:45
  28.2 0.7 %collective-permute-start.9 = (bf16[64,1280]{1,0:T(8,128)(2,1)S(1)}, bf16[64,1280]{1,0:T(8,128)(2,1)S(1)}, u32[]{:S(2)}, u32[]{:S(2)}) collective-permute-start(bf16[64,1280]{1,0:T(8,128)(2,1)S(1)} %collective-permute-done.8.refs_1_), channel_id=1, source_target_pairs={{0,1},{1,0},{2,3},{3,2},{4,5},{5,4},{6,7},{7,6},{8,9},{9,8},{10,11... | collective-permute-start | bytes 491528 | tf_op jit(solution)/shard_map/ppermute | solution.py:45
  29.0 0.1 collective-permute-start.13
  29.1 0.0 copy-start
  29.1 2.5 %collective-permute-start.16 = (bf16[32,640]{1,0:T(8,128)(2,1)S(1)}, bf16[32,640]{1,0:T(8,128)(2,1)S(1)}, u32[]{:S(2)}, u32[]{:S(2)}) collective-permute-start(bf16[32,640]{1,0:T(8,128)(2,1)S(1)} %multiply_convert_fusion.refs_0_), channel_id=1, source_target_pairs={{0,24},{8,16},{16,8},{24,0},{1,25},{9,17},{17,9},{25,1},{2,26},{10... | collective-permute-start | bytes 122888 | tf_op jit(solution)/shard_map/ppermute | solution.py:45
  31.7 1.0 %collective-permute-start.15 = (bf16[32,640]{1,0:T(8,128)(2,1)S(1)}, bf16[32,640]{1,0:T(8,128)(2,1)S(1)}, u32[]{:S(2)}, u32[]{:S(2)}) collective-permute-start(bf16[32,640]{1,0:T(8,128)(2,1)S(1)} %multiply_convert_fusion.refs_0_), channel_id=1, source_target_pairs={{0,16},{8,24},{16,0},{24,8},{1,17},{9,25},{17,1},{25,9},{2,18},{10... | collective-permute-start | bytes 122888 | tf_op jit(solution)/shard_map/ppermute | solution.py:45
  32.6 0.9 %collective-permute-start.14 = (bf16[32,640]{1,0:T(8,128)(2,1)S(1)}, bf16[32,640]{1,0:T(8,128)(2,1)S(1)}, u32[]{:S(2)}, u32[]{:S(2)}) collective-permute-start(bf16[32,640]{1,0:T(8,128)(2,1)S(1)} %multiply_convert_fusion.refs_0_), channel_id=1, source_target_pairs={{0,8},{8,0},{16,24},{24,16},{1,9},{9,1},{17,25},{25,17},{2,10},{10... | collective-permute-start | bytes 122888 | tf_op jit(solution)/shard_map/ppermute | solution.py:45
  33.6 0.9 %collective-permute-done.13.refs_6_ = bf16[64,1024]{1,0:T(8,128)(2,1)S(1)} collective-permute-done((bf16[64,1024]{1,0:T(8,128)(2,1)S(1)}, bf16[64,1024]{1,0:T(8,128)(2,1)S(1)}, u32[]{:S(2)}, u32[]{:S(2)}) %collective-permute-start.13) | collective-permute-done | bytes 131104 | tf_op jit(solution)/shard_map/ppermute | solution.py:45
  34.5 2.7 %shard_map.83 = (f32[1280,1024]{1,0:T(8,128)}, bf16[1280,128]{1,0:T(8,128)(2,1)S(1)}) custom-call(bf16[64,1280]{1,0:T(8,128)(2,1)S(1)} %get-tuple-element.32.refs_0_, bf16[64,1280]{1,0:T(8,128)(2,1)S(1)} %collective-permute-done.8.refs_1_, bf16[64,1280]{1,0:T(8,128)(2,1)S(1)} %collective-permute-done.9.refs_2_, ...), custom_call_target="tpu_custom_call" | custom-call | flops 335544320 | bytes 6488064 | tf_op jit(solution)/shard_map/pallas_call | solution.py:32
  37.2 0.1 collective-permute-done.15.refs_2_
  37.3 0.0 collective-permute-done.14.refs_1_
  37.4 2.0 %shard_map.84 = f32[1280,640]{1,0:T(8,128)} custom-call(bf16[1280,128]{1,0:T(8,128)(2,1)S(1)} %get-tuple-element.35.turned_ref, bf16[32,640]{1,0:T(8,128)(2,1)S(1)} %multiply_convert_fusion.refs_0_, bf16[32,640]{1,0:T(8,128)(2,1)S(1)} %collective-permute-done.14.refs_1_, bf16[32,640]{1,0:T(8,128)(2,1)S(1)} %collective-permute-done.15.refs_2_, ...), custom_call_target="tpu_custom_call" | custom-call | flops 209715200 | bytes 3768320 | tf_op jit(solution)/shard_map/pallas_call | solution.py:32
  (21 shorter events, 0.1 us)
Async XLA Ops:
  2.1 1.7 %collective-permute-start = (bf16[4,32,1024]{2,1,0:T(8,128)(2,1)S(1)}, bf16[4,32,1024]{2,1,0:T(8,128)(2,1)S(1)}, u32[]{:S(2)}, u32[]{:S(2)}) collective-permute-start(bf16[4,32,1024]{2,1,0:T(8,128)(2,1)S(1)} %get-tuple-element.21), channel_id=1, source_target_pairs={{0,1},{1,0},{2,3},{3,2},{4,5},{5,4},{6,7},{7,6},{8,9},{9,8},{10,11... | collective-permute-start | bytes 786440 | tf_op jit(solution)/shard_map/ppermute | solution.py:45
  3.9 9.7 %slice-start = ((s8[10485760]{0:T(1024)(128)(4,1)}), s8[4194304]{0:T(1024)(128)(4,1)S(1)}, s32[]{:S(2)}) async-start(s8[10485760]{0:T(1024)(128)(4,1)} %bitcast.4), calls=%async_computation | async-start | bytes 8388608
  3.9 9.7 %slice-start.1 = ((s8[10485760]{0:T(1024)(128)(4,1)}), s8[4194304]{0:T(1024)(128)(4,1)S(1)}, s32[]{:S(2)}) async-start(s8[10485760]{0:T(1024)(128)(4,1)} %bitcast.4), calls=%async_computation.1 | async-start | bytes 8388608
  3.9 9.7 %slice-start.2 = ((s8[10485760]{0:T(1024)(128)(4,1)}), s8[2097152]{0:T(1024)(128)(4,1)S(1)}, s32[]{:S(2)}) async-start(s8[10485760]{0:T(1024)(128)(4,1)} %bitcast.4), calls=%async_computation.2 | async-start | bytes 4194304
  3.9 5.3 %collective-permute-start.1 = (bf16[32,1024]{1,0:T(8,128)(2,1)S(1)}, bf16[32,1024]{1,0:T(8,128)(2,1)S(1)}, u32[]{:S(2)}, u32[]{:S(2)}) collective-permute-start(bf16[32,1024]{1,0:T(8,128)(2,1)S(1)} %get-tuple-element.23), channel_id=1, source_target_pairs={{0,2},{1,3},{2,0},{3,1},{4,6},{5,7},{6,4},{7,5},{8,10},{9,11},{10,... | collective-permute-start | bytes 196616 | tf_op jit(solution)/shard_map/ppermute | solution.py:45
  6.8 4.3 %collective-permute-start.2 = (bf16[32,1024]{1,0:T(8,128)(2,1)S(1)}, bf16[32,1024]{1,0:T(8,128)(2,1)S(1)}, u32[]{:S(2)}, u32[]{:S(2)}) collective-permute-start(bf16[32,1024]{1,0:T(8,128)(2,1)S(1)} %get-tuple-element.24), channel_id=1, source_target_pairs={{0,4},{1,5},{2,6},{3,7},{4,0},{5,1},{6,2},{7,3},{8,12},{9,13},{10,... | collective-permute-start | bytes 196616 | tf_op jit(solution)/shard_map/ppermute | solution.py:45
  8.4 5.2 %collective-permute-start.3 = (bf16[32,1024]{1,0:T(8,128)(2,1)S(1)}, bf16[32,1024]{1,0:T(8,128)(2,1)S(1)}, u32[]{:S(2)}, u32[]{:S(2)}) collective-permute-start(bf16[32,1024]{1,0:T(8,128)(2,1)S(1)} %get-tuple-element.25), channel_id=1, source_target_pairs={{0,6},{1,7},{2,4},{3,5},{4,2},{5,3},{6,0},{7,1},{8,14},{9,15},{10,... | collective-permute-start | bytes 196616 | tf_op jit(solution)/shard_map/ppermute | solution.py:45
  15.1 6.1 %collective-permute-start.4 = (bf16[4,32,640]{2,1,0:T(8,128)(2,1)S(1)}, bf16[4,32,640]{2,1,0:T(8,128)(2,1)S(1)}, u32[]{:S(2)}, u32[]{:S(2)}) collective-permute-start(bf16[4,32,640]{2,1,0:T(8,128)(2,1)S(1)} %get-tuple-element.27), channel_id=1, source_target_pairs={{0,1},{1,0},{2,3},{3,2},{4,5},{5,4},{6,7},{7,6},{8,9},{9,8},{10,11... | collective-permute-start | bytes 491528 | tf_op jit(solution)/shard_map/ppermute | solution.py:45
  15.2 7.2 %collective-permute-start.10 = (bf16[64,640]{1,0:T(8,128)(2,1)S(1)}, bf16[64,640]{1,0:T(8,128)(2,1)S(1)}, u32[]{:S(2)}, u32[]{:S(2)}) collective-permute-start(bf16[64,640]{1,0:T(8,128)(2,1)S(1)} %get-tuple-element.34), channel_id=1, source_target_pairs={{0,24},{1,25},{2,26},{3,27},{4,28},{5,29},{6,30},{7,31},{8,16},{9,... | collective-permute-start | bytes 245768 | tf_op jit(solution)/shard_map/ppermute | solution.py:266
  18.9 6.8 %collective-permute-start.8 = (bf16[64,1280]{1,0:T(8,128)(2,1)S(1)}, bf16[64,1280]{1,0:T(8,128)(2,1)S(1)}, u32[]{:S(2)}, u32[]{:S(2)}) collective-permute-start(bf16[64,1280]{1,0:T(8,128)(2,1)S(1)} %get-tuple-element.33), channel_id=1, source_target_pairs={{0,8},{1,17},{2,10},{3,19},{4,12},{5,21},{6,14},{7,23},{8,0},{9,25... | collective-permute-start | bytes 491528 | tf_op jit(solution)/shard_map/ppermute | solution.py:266
  18.9 9.4 %collective-permute-start.12 = (bf16[32,1024]{1,0:T(8,128)(2,1)S(1)}, bf16[32,1024]{1,0:T(8,128)(2,1)S(1)}, u32[]{:S(2)}, u32[]{:S(2)}) collective-permute-start(bf16[32,1024]{1,0:T(8,128)(2,1)S(1)} %get-tuple-element.26.merged_ref.refs_0_), channel_id=1, source_target_pairs={{0,16},{8,24},{16,0},{24,8},{1,17},{9,25},{17,1},{25,9},{2,18},{10... | collective-permute-start | bytes 196616 | tf_op jit(solution)/shard_map/ppermute | solution.py:45
  21.3 7.7 %collective-permute-start.5 = (bf16[32,640]{1,0:T(8,128)(2,1)S(1)}, bf16[32,640]{1,0:T(8,128)(2,1)S(1)}, u32[]{:S(2)}, u32[]{:S(2)}) collective-permute-start(bf16[32,640]{1,0:T(8,128)(2,1)S(1)} %get-tuple-element.29), channel_id=1, source_target_pairs={{0,2},{1,3},{2,0},{3,1},{4,6},{5,7},{6,4},{7,5},{8,10},{9,11},{10,... | collective-permute-start | bytes 122888 | tf_op jit(solution)/shard_map/ppermute | solution.py:45
  21.9 7.2 %collective-permute-start.6 = (bf16[32,640]{1,0:T(8,128)(2,1)S(1)}, bf16[32,640]{1,0:T(8,128)(2,1)S(1)}, u32[]{:S(2)}, u32[]{:S(2)}) collective-permute-start(bf16[32,640]{1,0:T(8,128)(2,1)S(1)} %get-tuple-element.30), channel_id=1, source_target_pairs={{0,4},{1,5},{2,6},{3,7},{4,0},{5,1},{6,2},{7,3},{8,12},{9,13},{10,... | collective-permute-start | bytes 122888 | tf_op jit(solution)/shard_map/ppermute | solution.py:45
  22.4 6.6 %collective-permute-start.7 = (bf16[32,640]{1,0:T(8,128)(2,1)S(1)}, bf16[32,640]{1,0:T(8,128)(2,1)S(1)}, u32[]{:S(2)}, u32[]{:S(2)}) collective-permute-start(bf16[32,640]{1,0:T(8,128)(2,1)S(1)} %get-tuple-element.31), channel_id=1, source_target_pairs={{0,6},{1,7},{2,4},{3,5},{4,2},{5,3},{6,0},{7,1},{8,14},{9,15},{10,... | collective-permute-start | bytes 122888 | tf_op jit(solution)/shard_map/ppermute | solution.py:45
  25.7 7.0 %collective-permute-start.11 = (bf16[64,640]{1,0:T(8,128)(2,1)S(1)}, bf16[64,640]{1,0:T(8,128)(2,1)S(1)}, u32[]{:S(2)}, u32[]{:S(2)}) collective-permute-start(bf16[64,640]{1,0:T(8,128)(2,1)S(1)} %collective-permute-done.10.refs_3_), channel_id=1, source_target_pairs={{0,1},{1,0},{2,3},{3,2},{4,5},{5,4},{6,7},{7,6},{8,9},{9,8},{10,11... | collective-permute-start | bytes 245768 | tf_op jit(solution)/shard_map/ppermute | solution.py:45
  28.2 5.3 %collective-permute-start.9 = (bf16[64,1280]{1,0:T(8,128)(2,1)S(1)}, bf16[64,1280]{1,0:T(8,128)(2,1)S(1)}, u32[]{:S(2)}, u32[]{:S(2)}) collective-permute-start(bf16[64,1280]{1,0:T(8,128)(2,1)S(1)} %collective-permute-done.8.refs_1_), channel_id=1, source_target_pairs={{0,1},{1,0},{2,3},{3,2},{4,5},{5,4},{6,7},{7,6},{8,9},{9,8},{10,11... | collective-permute-start | bytes 491528 | tf_op jit(solution)/shard_map/ppermute | solution.py:45
  29.0 5.5 %collective-permute-start.13 = (bf16[64,1024]{1,0:T(8,128)(2,1)S(1)}, bf16[64,1024]{1,0:T(8,128)(2,1)S(1)}, u32[]{:S(2)}, u32[]{:S(2)}) collective-permute-start(bf16[64,1024]{1,0:T(8,128)(2,1)S(1)} %shard_map.82.refs_5_), channel_id=1, source_target_pairs={{0,8},{8,0},{16,24},{24,16},{1,9},{9,1},{17,25},{25,17},{2,10},{10... | collective-permute-start | bytes 393224 | tf_op jit(solution)/shard_map/ppermute | solution.py:45
  29.1 10.2 %copy-start = (bf16[32,640]{1,0:T(8,128)(2,1)}, bf16[32,640]{1,0:T(8,128)(2,1)S(1)}, u32[]{:S(2)}) copy-start(bf16[32,640]{1,0:T(8,128)(2,1)S(1)} %multiply_convert_fusion.refs_0_) | copy-start | bytes 122884
  29.1 8.1 %collective-permute-start.16 = (bf16[32,640]{1,0:T(8,128)(2,1)S(1)}, bf16[32,640]{1,0:T(8,128)(2,1)S(1)}, u32[]{:S(2)}, u32[]{:S(2)}) collective-permute-start(bf16[32,640]{1,0:T(8,128)(2,1)S(1)} %multiply_convert_fusion.refs_0_), channel_id=1, source_target_pairs={{0,24},{8,16},{16,8},{24,0},{1,25},{9,17},{17,9},{25,1},{2,26},{10... | collective-permute-start | bytes 122888 | tf_op jit(solution)/shard_map/ppermute | solution.py:45
  31.7 5.7 %collective-permute-start.15 = (bf16[32,640]{1,0:T(8,128)(2,1)S(1)}, bf16[32,640]{1,0:T(8,128)(2,1)S(1)}, u32[]{:S(2)}, u32[]{:S(2)}) collective-permute-start(bf16[32,640]{1,0:T(8,128)(2,1)S(1)} %multiply_convert_fusion.refs_0_), channel_id=1, source_target_pairs={{0,16},{8,24},{16,0},{24,8},{1,17},{9,25},{17,1},{25,9},{2,18},{10... | collective-permute-start | bytes 122888 | tf_op jit(solution)/shard_map/ppermute | solution.py:45
  32.6 4.7 %collective-permute-start.14 = (bf16[32,640]{1,0:T(8,128)(2,1)S(1)}, bf16[32,640]{1,0:T(8,128)(2,1)S(1)}, u32[]{:S(2)}, u32[]{:S(2)}) collective-permute-start(bf16[32,640]{1,0:T(8,128)(2,1)S(1)} %multiply_convert_fusion.refs_0_), channel_id=1, source_target_pairs={{0,8},{8,0},{16,24},{24,16},{1,9},{9,1},{17,25},{25,17},{2,10},{10... | collective-permute-start | bytes 122888 | tf_op jit(solution)/shard_map/ppermute | solution.py:45

commit v7 on v6

--- a/solution.py
+++ b/solution.py
@@ -119,9 +119,13 @@
     turned = merged.T
     for j in range(halves):
         first = pl.multiple_of((shard ^ (2 * j + parity)) * unit_cols, unit_cols)
-        out_ref[j] = lax.dot_general(
-            w_ref[pl.ds(first, unit_cols), :], turned, (((1,), (0,)), ((), ())), preferred_element_type=jnp.float32
-        ).T.astype(jnp.bfloat16)
+        rows = w_ref[pl.ds(first, unit_cols), :]
+        if j % 2:
+            out_ref[j] = lax.dot_general(
+                merged, rows, (((1,), (1,)), ((), ())), preferred_element_type=jnp.float32
+            ).astype(jnp.bfloat16)
+        else:
+            out_ref[j] = jnp.dot(rows, turned, preferred_element_type=jnp.float32).T.astype(jnp.bfloat16)
 
 
 def first_units(*refs):

time: 39.6 us -> 39.5 us (level)
  no operation moved by 1% of the time
where the time goes in v7:
time: 39.5 us; the launch traced here: 39.3 us
  starting transfers between devices  20.7 us (52%)
  Pallas kernels  10.2 us (26%)
  waiting for transfers between devices  7.58 us (19%)
  between operations  0.78 us (2%)
    ppermute x15, starting transfers between devices, exchange(): return lax.ppermute(block, axis, pairs)  17.1 us
    pallas_call x9, Pallas kernels, call(): pl.pallas_call(kernel, out_shape=outs, in_specs=in_specs or [VMEM] * len(...  10.2 us
    ppermute x15, waiting for transfers between devices, exchange(): return lax.ppermute(block, axis, pairs)  7.39 us
    ppermute x2, starting transfers between devices, body(): came = lax.ppermute(block, ('enc', 'roll'), pairs)  3.65 us
  transfers between devices with their start and end apart: 17, of which 7 were waited for; matrix products, arithmetic and copies ran while one was open for 0% of the time, Pallas kernels for 13%

profile of v7, /device:TPU:0, one launch (start us, length us, event | category | flops | bytes accessed | tf_op | source)
XLA Modules:
  0.0 39.3 jit_solution(6618180834017338724)
XLA Ops:
  0.6 1.5 %shard_map.76 = (bf16[4,32,1024]{2,1,0:T(8,128)(2,1)S(1)}, bf16[4,32,1024]{2,1,0:T(8,128)(2,1)S(1)}, bf16[64,1280]{1,0:T(8,128)(2,1)S(1)}, bf16[64,1280]{1,0:T(8,128)(2,1)S(1)}, bf16[64,640]{1,0:T(8,128)(2,1)S(1)}) custom-call(s32[1,32]{1,0:T(1,128)} %refs_0_.1, bf16[32,8192]{1,0:T(8,128)(2,1)} %bitcast.9, bf16[32,5120]{1,0:T(8,128)(2,1)} %bitcast.7, ...), custom_call_target="tpu_custom_call" | custom-call | flops 16777216 | bytes 2113664 | tf_op jit(solution)/shard_map/pallas_call | solution.py:32
  2.1 0.6 %collective-permute-start = (bf16[4,32,1024]{2,1,0:T(8,128)(2,1)S(1)}, bf16[4,32,1024]{2,1,0:T(8,128)(2,1)S(1)}, u32[]{:S(2)}, u32[]{:S(2)}) collective-permute-start(bf16[4,32,1024]{2,1,0:T(8,128)(2,1)S(1)} %get-tuple-element.21), channel_id=1, source_target_pairs={{0,1},{1,0},{2,3},{3,2},{4,5},{5,4},{6,7},{7,6},{8,9},{9,8},{10,11... | collective-permute-start | bytes 786440 | tf_op jit(solution)/shard_map/ppermute | solution.py:45
  2.7 1.2 %collective-permute-done.came_ref = bf16[4,32,1024]{2,1,0:T(8,128)(2,1)S(1)} collective-permute-done((bf16[4,32,1024]{2,1,0:T(8,128)(2,1)S(1)}, bf16[4,32,1024]{2,1,0:T(8,128)(2,1)S(1)}, u32[]{:S(2)}, u32[]{:S(2)}) %collective-permute-start) | collective-permute-done | bytes 262176 | tf_op jit(solution)/shard_map/ppermute | solution.py:45
  3.9 0.1 shard_map.77
  3.9 2.9 %collective-permute-start.1 = (bf16[32,1024]{1,0:T(8,128)(2,1)S(1)}, bf16[32,1024]{1,0:T(8,128)(2,1)S(1)}, u32[]{:S(2)}, u32[]{:S(2)}) collective-permute-start(bf16[32,1024]{1,0:T(8,128)(2,1)S(1)} %get-tuple-element.23), channel_id=1, source_target_pairs={{0,2},{1,3},{2,0},{3,1},{4,6},{5,7},{6,4},{7,5},{8,10},{9,11},{10,... | collective-permute-start | bytes 196616 | tf_op jit(solution)/shard_map/ppermute | solution.py:45
  6.8 1.5 %collective-permute-start.2 = (bf16[32,1024]{1,0:T(8,128)(2,1)S(1)}, bf16[32,1024]{1,0:T(8,128)(2,1)S(1)}, u32[]{:S(2)}, u32[]{:S(2)}) collective-permute-start(bf16[32,1024]{1,0:T(8,128)(2,1)S(1)} %get-tuple-element.24), channel_id=1, source_target_pairs={{0,4},{1,5},{2,6},{3,7},{4,0},{5,1},{6,2},{7,3},{8,12},{9,13},{10,... | collective-permute-start | bytes 196616 | tf_op jit(solution)/shard_map/ppermute | solution.py:45
  8.4 0.0 collective-permute-start.3
  8.4 0.9 %collective-permute-done.1.refs_1_ = bf16[32,1024]{1,0:T(8,128)(2,1)S(1)} collective-permute-done((bf16[32,1024]{1,0:T(8,128)(2,1)S(1)}, bf16[32,1024]{1,0:T(8,128)(2,1)S(1)}, u32[]{:S(2)}, u32[]{:S(2)}) %collective-permute-start.1) | collective-permute-done | bytes 65568 | tf_op jit(solution)/shard_map/ppermute | solution.py:45
  9.2 1.9 %collective-permute-done.2.refs_2_ = bf16[32,1024]{1,0:T(8,128)(2,1)S(1)} collective-permute-done((bf16[32,1024]{1,0:T(8,128)(2,1)S(1)}, bf16[32,1024]{1,0:T(8,128)(2,1)S(1)}, u32[]{:S(2)}, u32[]{:S(2)}) %collective-permute-start.2) | collective-permute-done | bytes 65568 | tf_op jit(solution)/shard_map/ppermute | solution.py:45
  11.1 2.4 %collective-permute-done.3.refs_3_ = bf16[32,1024]{1,0:T(8,128)(2,1)S(1)} collective-permute-done((bf16[32,1024]{1,0:T(8,128)(2,1)S(1)}, bf16[32,1024]{1,0:T(8,128)(2,1)S(1)}, u32[]{:S(2)}, u32[]{:S(2)}) %collective-permute-start.3) | collective-permute-done | bytes 65568 | tf_op jit(solution)/shard_map/ppermute | solution.py:45
  13.6 1.5 %shard_map.78 = (bf16[32,1024]{1,0:T(8,128)(2,1)S(1)}, bf16[4,32,640]{2,1,0:T(8,128)(2,1)S(1)}) custom-call(bf16[32,1024]{1,0:T(8,128)(2,1)S(1)} %get-tuple-element.22.refs_0_, bf16[32,1024]{1,0:T(8,128)(2,1)S(1)} %collective-permute-done.1.refs_1_, bf16[32,1024]{1,0:T(8,128)(2,1)S(1)} %collective-permute-done.2.refs_2_, ...), custom_call_target="tpu_custom_call" | custom-call | flops 167772160 | bytes 10977280 | tf_op jit(solution)/shard_map/pallas_call | solution.py:32
  15.1 0.0 collective-permute-start.4
  15.2 3.6 %collective-permute-start.10 = (bf16[64,640]{1,0:T(8,128)(2,1)S(1)}, bf16[64,640]{1,0:T(8,128)(2,1)S(1)}, u32[]{:S(2)}, u32[]{:S(2)}) collective-permute-start(bf16[64,640]{1,0:T(8,128)(2,1)S(1)} %get-tuple-element.34), channel_id=1, source_target_pairs={{0,24},{1,25},{2,26},{3,27},{4,28},{5,29},{6,30},{7,31},{8,16},{9,... | collective-permute-start | bytes 245768 | tf_op jit(solution)/shard_map/ppermute | solution.py:270
  18.8 0.8 %collective-permute-start.12 = (bf16[32,1024]{1,0:T(8,128)(2,1)S(1)}, bf16[32,1024]{1,0:T(8,128)(2,1)S(1)}, u32[]{:S(2)}, u32[]{:S(2)}) collective-permute-start(bf16[32,1024]{1,0:T(8,128)(2,1)S(1)} %get-tuple-element.26.merged_ref.refs_0_), channel_id=1, source_target_pairs={{0,16},{8,24},{16,0},{24,8},{1,17},{9,25},{17,1},{25,9},{2,18},{10... | collective-permute-start | bytes 196616 | tf_op jit(solution)/shard_map/ppermute | solution.py:45
  19.6 1.5 %shard_map.79.kept_ref = bf16[4,32,640]{2,1,0:T(8,128)(2,1)S(1)} custom-call(bf16[32,1024]{1,0:T(8,128)(2,1)S(1)} %get-tuple-element.26.merged_ref.refs_0_, bf16[5120,1024]{1,0:T(8,128)(2,1)S(1)} %bitcast.5), custom_call_target="tpu_custom_call" | custom-call | flops 167772160 | bytes 10715136 | tf_op jit(solution)/shard_map/pallas_call | solution.py:32
  21.1 0.0 collective-permute-done.4.came_ref
  21.2 0.6 %collective-permute-start.5 = (bf16[32,640]{1,0:T(8,128)(2,1)S(1)}, bf16[32,640]{1,0:T(8,128)(2,1)S(1)}, u32[]{:S(2)}, u32[]{:S(2)}) collective-permute-start(bf16[32,640]{1,0:T(8,128)(2,1)S(1)} %get-tuple-element.29), channel_id=1, source_target_pairs={{0,2},{1,3},{2,0},{3,1},{4,6},{5,7},{6,4},{7,5},{8,10},{9,11},{10,... | collective-permute-start | bytes 122888 | tf_op jit(solution)/shard_map/ppermute | solution.py:45
  21.8 0.4 %collective-permute-start.6 = (bf16[32,640]{1,0:T(8,128)(2,1)S(1)}, bf16[32,640]{1,0:T(8,128)(2,1)S(1)}, u32[]{:S(2)}, u32[]{:S(2)}) collective-permute-start(bf16[32,640]{1,0:T(8,128)(2,1)S(1)} %get-tuple-element.30), channel_id=1, source_target_pairs={{0,4},{1,5},{2,6},{3,7},{4,0},{5,1},{6,2},{7,3},{8,12},{9,13},{10,... | collective-permute-start | bytes 122888 | tf_op jit(solution)/shard_map/ppermute | solution.py:45
  22.2 0.2 collective-permute-done.10.refs_3_
  22.4 2.4 %collective-permute-start.7 = (bf16[32,640]{1,0:T(8,128)(2,1)S(1)}, bf16[32,640]{1,0:T(8,128)(2,1)S(1)}, u32[]{:S(2)}, u32[]{:S(2)}) collective-permute-start(bf16[32,640]{1,0:T(8,128)(2,1)S(1)} %get-tuple-element.31), channel_id=1, source_target_pairs={{0,6},{1,7},{2,4},{3,5},{4,2},{5,3},{6,0},{7,1},{8,14},{9,15},{10,... | collective-permute-start | bytes 122888 | tf_op jit(solution)/shard_map/ppermute | solution.py:45
  24.7 0.8 %shard_map.81 = f32[32,640]{1,0:T(8,128)S(1)} custom-call(bf16[32,5120]{1,0:T(8,128)(2,1)} %bitcast.8), custom_call_target="tpu_custom_call" | custom-call | bytes 409600 | tf_op jit(solution)/shard_map/pallas_call | solution.py:32
  25.6 2.6 %collective-permute-start.11 = (bf16[64,640]{1,0:T(8,128)(2,1)S(1)}, bf16[64,640]{1,0:T(8,128)(2,1)S(1)}, u32[]{:S(2)}, u32[]{:S(2)}) collective-permute-start(bf16[64,640]{1,0:T(8,128)(2,1)S(1)} %collective-permute-done.10.refs_3_), channel_id=1, source_target_pairs={{0,1},{1,0},{2,3},{3,2},{4,5},{5,4},{6,7},{7,6},{8,9},{9,8},{10,11... | collective-permute-start | bytes 245768 | tf_op jit(solution)/shard_map/ppermute | solution.py:45
  28.2 0.7 %collective-permute-start.9 = (bf16[64,1280]{1,0:T(8,128)(2,1)S(1)}, bf16[64,1280]{1,0:T(8,128)(2,1)S(1)}, u32[]{:S(2)}, u32[]{:S(2)}) collective-permute-start(bf16[64,1280]{1,0:T(8,128)(2,1)S(1)} %collective-permute-done.8.refs_1_), channel_id=1, source_target_pairs={{0,1},{1,0},{2,3},{3,2},{4,5},{5,4},{6,7},{7,6},{8,9},{9,8},{10,11... | collective-permute-start | bytes 491528 | tf_op jit(solution)/shard_map/ppermute | solution.py:45
  28.9 0.1 collective-permute-start.13
  29.1 2.5 %collective-permute-start.16 = (bf16[32,640]{1,0:T(8,128)(2,1)S(1)}, bf16[32,640]{1,0:T(8,128)(2,1)S(1)}, u32[]{:S(2)}, u32[]{:S(2)}) collective-permute-start(bf16[32,640]{1,0:T(8,128)(2,1)S(1)} %multiply_convert_fusion.refs_0_), channel_id=1, source_target_pairs={{0,24},{8,16},{16,8},{24,0},{1,25},{9,17},{17,9},{25,1},{2,26},{10... | collective-permute-start | bytes 122888 | tf_op jit(solution)/shard_map/ppermute | solution.py:45
  31.6 1.0 %collective-permute-start.15 = (bf16[32,640]{1,0:T(8,128)(2,1)S(1)}, bf16[32,640]{1,0:T(8,128)(2,1)S(1)}, u32[]{:S(2)}, u32[]{:S(2)}) collective-permute-start(bf16[32,640]{1,0:T(8,128)(2,1)S(1)} %multiply_convert_fusion.refs_0_), channel_id=1, source_target_pairs={{0,16},{8,24},{16,0},{24,8},{1,17},{9,25},{17,1},{25,9},{2,18},{10... | collective-permute-start | bytes 122888 | tf_op jit(solution)/shard_map/ppermute | solution.py:45
  32.6 0.9 %collective-permute-start.14 = (bf16[32,640]{1,0:T(8,128)(2,1)S(1)}, bf16[32,640]{1,0:T(8,128)(2,1)S(1)}, u32[]{:S(2)}, u32[]{:S(2)}) collective-permute-start(bf16[32,640]{1,0:T(8,128)(2,1)S(1)} %multiply_convert_fusion.refs_0_), channel_id=1, source_target_pairs={{0,8},{8,0},{16,24},{24,16},{1,9},{9,1},{17,25},{25,17},{2,10},{10... | collective-permute-start | bytes 122888 | tf_op jit(solution)/shard_map/ppermute | solution.py:45
  33.5 0.9 %collective-permute-done.13.refs_6_ = bf16[64,1024]{1,0:T(8,128)(2,1)S(1)} collective-permute-done((bf16[64,1024]{1,0:T(8,128)(2,1)S(1)}, bf16[64,1024]{1,0:T(8,128)(2,1)S(1)}, u32[]{:S(2)}, u32[]{:S(2)}) %collective-permute-start.13) | collective-permute-done | bytes 131104 | tf_op jit(solution)/shard_map/ppermute | solution.py:45
  34.4 2.7 %shard_map.83 = (f32[1280,1024]{1,0:T(8,128)}, bf16[1280,128]{1,0:T(8,128)(2,1)S(1)}) custom-call(bf16[64,1280]{1,0:T(8,128)(2,1)S(1)} %get-tuple-element.32.refs_0_, bf16[64,1280]{1,0:T(8,128)(2,1)S(1)} %collective-permute-done.8.refs_1_, bf16[64,1280]{1,0:T(8,128)(2,1)S(1)} %collective-permute-done.9.refs_2_, ...), custom_call_target="tpu_custom_call" | custom-call | flops 335544320 | bytes 6488064 | tf_op jit(solution)/shard_map/pallas_call | solution.py:32
  37.1 0.1 collective-permute-done.15.refs_2_
  37.3 0.0 collective-permute-done.14.refs_1_
  37.3 2.0 %shard_map.84 = f32[1280,640]{1,0:T(8,128)} custom-call(bf16[1280,128]{1,0:T(8,128)(2,1)S(1)} %get-tuple-element.35.turned_ref, bf16[32,640]{1,0:T(8,128)(2,1)S(1)} %multiply_convert_fusion.refs_0_, bf16[32,640]{1,0:T(8,128)(2,1)S(1)} %collective-permute-done.14.refs_1_, bf16[32,640]{1,0:T(8,128)(2,1)S(1)} %collective-permute-done.15.refs_2_, ...), custom_call_target="tpu_custom_call" | custom-call | flops 209715200 | bytes 3768320 | tf_op jit(solution)/shard_map/pallas_call | solution.py:32
  (21 shorter events, 0.1 us)
Async XLA Ops:
  2.1 1.7 %collective-permute-start = (bf16[4,32,1024]{2,1,0:T(8,128)(2,1)S(1)}, bf16[4,32,1024]{2,1,0:T(8,128)(2,1)S(1)}, u32[]{:S(2)}, u32[]{:S(2)}) collective-permute-start(bf16[4,32,1024]{2,1,0:T(8,128)(2,1)S(1)} %get-tuple-element.21), channel_id=1, source_target_pairs={{0,1},{1,0},{2,3},{3,2},{4,5},{5,4},{6,7},{7,6},{8,9},{9,8},{10,11... | collective-permute-start | bytes 786440 | tf_op jit(solution)/shard_map/ppermute | solution.py:45
  3.9 9.7 %slice-start = ((s8[10485760]{0:T(1024)(128)(4,1)}), s8[4194304]{0:T(1024)(128)(4,1)S(1)}, s32[]{:S(2)}) async-start(s8[10485760]{0:T(1024)(128)(4,1)} %bitcast.4), calls=%async_computation | async-start | bytes 8388608
  3.9 9.7 %slice-start.1 = ((s8[10485760]{0:T(1024)(128)(4,1)}), s8[4194304]{0:T(1024)(128)(4,1)S(1)}, s32[]{:S(2)}) async-start(s8[10485760]{0:T(1024)(128)(4,1)} %bitcast.4), calls=%async_computation.1 | async-start | bytes 8388608
  3.9 9.7 %slice-start.2 = ((s8[10485760]{0:T(1024)(128)(4,1)}), s8[2097152]{0:T(1024)(128)(4,1)S(1)}, s32[]{:S(2)}) async-start(s8[10485760]{0:T(1024)(128)(4,1)} %bitcast.4), calls=%async_computation.2 | async-start | bytes 4194304
  3.9 5.3 %collective-permute-start.1 = (bf16[32,1024]{1,0:T(8,128)(2,1)S(1)}, bf16[32,1024]{1,0:T(8,128)(2,1)S(1)}, u32[]{:S(2)}, u32[]{:S(2)}) collective-permute-start(bf16[32,1024]{1,0:T(8,128)(2,1)S(1)} %get-tuple-element.23), channel_id=1, source_target_pairs={{0,2},{1,3},{2,0},{3,1},{4,6},{5,7},{6,4},{7,5},{8,10},{9,11},{10,... | collective-permute-start | bytes 196616 | tf_op jit(solution)/shard_map/ppermute | solution.py:45
  6.8 4.3 %collective-permute-start.2 = (bf16[32,1024]{1,0:T(8,128)(2,1)S(1)}, bf16[32,1024]{1,0:T(8,128)(2,1)S(1)}, u32[]{:S(2)}, u32[]{:S(2)}) collective-permute-start(bf16[32,1024]{1,0:T(8,128)(2,1)S(1)} %get-tuple-element.24), channel_id=1, source_target_pairs={{0,4},{1,5},{2,6},{3,7},{4,0},{5,1},{6,2},{7,3},{8,12},{9,13},{10,... | collective-permute-start | bytes 196616 | tf_op jit(solution)/shard_map/ppermute | solution.py:45
  8.4 5.2 %collective-permute-start.3 = (bf16[32,1024]{1,0:T(8,128)(2,1)S(1)}, bf16[32,1024]{1,0:T(8,128)(2,1)S(1)}, u32[]{:S(2)}, u32[]{:S(2)}) collective-permute-start(bf16[32,1024]{1,0:T(8,128)(2,1)S(1)} %get-tuple-element.25), channel_id=1, source_target_pairs={{0,6},{1,7},{2,4},{3,5},{4,2},{5,3},{6,0},{7,1},{8,14},{9,15},{10,... | collective-permute-start | bytes 196616 | tf_op jit(solution)/shard_map/ppermute | solution.py:45
  15.1 6.0 %collective-permute-start.4 = (bf16[4,32,640]{2,1,0:T(8,128)(2,1)S(1)}, bf16[4,32,640]{2,1,0:T(8,128)(2,1)S(1)}, u32[]{:S(2)}, u32[]{:S(2)}) collective-permute-start(bf16[4,32,640]{2,1,0:T(8,128)(2,1)S(1)} %get-tuple-element.27), channel_id=1, source_target_pairs={{0,1},{1,0},{2,3},{3,2},{4,5},{5,4},{6,7},{7,6},{8,9},{9,8},{10,11... | collective-permute-start | bytes 491528 | tf_op jit(solution)/shard_map/ppermute | solution.py:45
  15.2 7.2 %collective-permute-start.10 = (bf16[64,640]{1,0:T(8,128)(2,1)S(1)}, bf16[64,640]{1,0:T(8,128)(2,1)S(1)}, u32[]{:S(2)}, u32[]{:S(2)}) collective-permute-start(bf16[64,640]{1,0:T(8,128)(2,1)S(1)} %get-tuple-element.34), channel_id=1, source_target_pairs={{0,24},{1,25},{2,26},{3,27},{4,28},{5,29},{6,30},{7,31},{8,16},{9,... | collective-permute-start | bytes 245768 | tf_op jit(solution)/shard_map/ppermute | solution.py:270
  18.8 6.8 %collective-permute-start.8 = (bf16[64,1280]{1,0:T(8,128)(2,1)S(1)}, bf16[64,1280]{1,0:T(8,128)(2,1)S(1)}, u32[]{:S(2)}, u32[]{:S(2)}) collective-permute-start(bf16[64,1280]{1,0:T(8,128)(2,1)S(1)} %get-tuple-element.33), channel_id=1, source_target_pairs={{0,8},{1,17},{2,10},{3,19},{4,12},{5,21},{6,14},{7,23},{8,0},{9,25... | collective-permute-start | bytes 491528 | tf_op jit(solution)/shard_map/ppermute | solution.py:270
  18.8 9.4 %collective-permute-start.12 = (bf16[32,1024]{1,0:T(8,128)(2,1)S(1)}, bf16[32,1024]{1,0:T(8,128)(2,1)S(1)}, u32[]{:S(2)}, u32[]{:S(2)}) collective-permute-start(bf16[32,1024]{1,0:T(8,128)(2,1)S(1)} %get-tuple-element.26.merged_ref.refs_0_), channel_id=1, source_target_pairs={{0,16},{8,24},{16,0},{24,8},{1,17},{9,25},{17,1},{25,9},{2,18},{10... | collective-permute-start | bytes 196616 | tf_op jit(solution)/shard_map/ppermute | solution.py:45
  21.2 7.7 %collective-permute-start.5 = (bf16[32,640]{1,0:T(8,128)(2,1)S(1)}, bf16[32,640]{1,0:T(8,128)(2,1)S(1)}, u32[]{:S(2)}, u32[]{:S(2)}) collective-permute-start(bf16[32,640]{1,0:T(8,128)(2,1)S(1)} %get-tuple-element.29), channel_id=1, source_target_pairs={{0,2},{1,3},{2,0},{3,1},{4,6},{5,7},{6,4},{7,5},{8,10},{9,11},{10,... | collective-permute-start | bytes 122888 | tf_op jit(solution)/shard_map/ppermute | solution.py:45
  21.8 7.2 %collective-permute-start.6 = (bf16[32,640]{1,0:T(8,128)(2,1)S(1)}, bf16[32,640]{1,0:T(8,128)(2,1)S(1)}, u32[]{:S(2)}, u32[]{:S(2)}) collective-permute-start(bf16[32,640]{1,0:T(8,128)(2,1)S(1)} %get-tuple-element.30), channel_id=1, source_target_pairs={{0,4},{1,5},{2,6},{3,7},{4,0},{5,1},{6,2},{7,3},{8,12},{9,13},{10,... | collective-permute-start | bytes 122888 | tf_op jit(solution)/shard_map/ppermute | solution.py:45
  22.4 6.6 %collective-permute-start.7 = (bf16[32,640]{1,0:T(8,128)(2,1)S(1)}, bf16[32,640]{1,0:T(8,128)(2,1)S(1)}, u32[]{:S(2)}, u32[]{:S(2)}) collective-permute-start(bf16[32,640]{1,0:T(8,128)(2,1)S(1)} %get-tuple-element.31), channel_id=1, source_target_pairs={{0,6},{1,7},{2,4},{3,5},{4,2},{5,3},{6,0},{7,1},{8,14},{9,15},{10,... | collective-permute-start | bytes 122888 | tf_op jit(solution)/shard_map/ppermute | solution.py:45
  25.6 7.0 %collective-permute-start.11 = (bf16[64,640]{1,0:T(8,128)(2,1)S(1)}, bf16[64,640]{1,0:T(8,128)(2,1)S(1)}, u32[]{:S(2)}, u32[]{:S(2)}) collective-permute-start(bf16[64,640]{1,0:T(8,128)(2,1)S(1)} %collective-permute-done.10.refs_3_), channel_id=1, source_target_pairs={{0,1},{1,0},{2,3},{3,2},{4,5},{5,4},{6,7},{7,6},{8,9},{9,8},{10,11... | collective-permute-start | bytes 245768 | tf_op jit(solution)/shard_map/ppermute | solution.py:45
  28.2 5.3 %collective-permute-start.9 = (bf16[64,1280]{1,0:T(8,128)(2,1)S(1)}, bf16[64,1280]{1,0:T(8,128)(2,1)S(1)}, u32[]{:S(2)}, u32[]{:S(2)}) collective-permute-start(bf16[64,1280]{1,0:T(8,128)(2,1)S(1)} %collective-permute-done.8.refs_1_), channel_id=1, source_target_pairs={{0,1},{1,0},{2,3},{3,2},{4,5},{5,4},{6,7},{7,6},{8,9},{9,8},{10,11... | collective-permute-start | bytes 491528 | tf_op jit(solution)/shard_map/ppermute | solution.py:45
  28.9 5.5 %collective-permute-start.13 = (bf16[64,1024]{1,0:T(8,128)(2,1)S(1)}, bf16[64,1024]{1,0:T(8,128)(2,1)S(1)}, u32[]{:S(2)}, u32[]{:S(2)}) collective-permute-start(bf16[64,1024]{1,0:T(8,128)(2,1)S(1)} %shard_map.82.refs_5_), channel_id=1, source_target_pairs={{0,8},{8,0},{16,24},{24,16},{1,9},{9,1},{17,25},{25,17},{2,10},{10... | collective-permute-start | bytes 393224 | tf_op jit(solution)/shard_map/ppermute | solution.py:45
  29.1 10.2 %copy-start = (bf16[32,640]{1,0:T(8,128)(2,1)}, bf16[32,640]{1,0:T(8,128)(2,1)S(1)}, u32[]{:S(2)}) copy-start(bf16[32,640]{1,0:T(8,128)(2,1)S(1)} %multiply_convert_fusion.refs_0_) | copy-start | bytes 122884
  29.1 8.1 %collective-permute-start.16 = (bf16[32,640]{1,0:T(8,128)(2,1)S(1)}, bf16[32,640]{1,0:T(8,128)(2,1)S(1)}, u32[]{:S(2)}, u32[]{:S(2)}) collective-permute-start(bf16[32,640]{1,0:T(8,128)(2,1)S(1)} %multiply_convert_fusion.refs_0_), channel_id=1, source_target_pairs={{0,24},{8,16},{16,8},{24,0},{1,25},{9,17},{17,9},{25,1},{2,26},{10... | collective-permute-start | bytes 122888 | tf_op jit(solution)/shard_map/ppermute | solution.py:45
  31.6 5.7 %collective-permute-start.15 = (bf16[32,640]{1,0:T(8,128)(2,1)S(1)}, bf16[32,640]{1,0:T(8,128)(2,1)S(1)}, u32[]{:S(2)}, u32[]{:S(2)}) collective-permute-start(bf16[32,640]{1,0:T(8,128)(2,1)S(1)} %multiply_convert_fusion.refs_0_), channel_id=1, source_target_pairs={{0,16},{8,24},{16,0},{24,8},{1,17},{9,25},{17,1},{25,9},{2,18},{10... | collective-permute-start | bytes 122888 | tf_op jit(solution)/shard_map/ppermute | solution.py:45
  32.6 4.7 %collective-permute-start.14 = (bf16[32,640]{1,0:T(8,128)(2,1)S(1)}, bf16[32,640]{1,0:T(8,128)(2,1)S(1)}, u32[]{:S(2)}, u32[]{:S(2)}) collective-permute-start(bf16[32,640]{1,0:T(8,128)(2,1)S(1)} %multiply_convert_fusion.refs_0_), channel_id=1, source_target_pairs={{0,8},{8,0},{16,24},{24,16},{1,9},{9,1},{17,25},{25,17},{2,10},{10... | collective-permute-start | bytes 122888 | tf_op jit(solution)/shard_map/ppermute | solution.py:45
